TPU v7x, 32 devices: a whole 2x2x4 slice. The times are simulated.
32 devices in a mesh: gx: 4 (over x, core), gy: 8 (over z, y).
Axes of the slice: x: 2, y: 2, z: 4, core: 2. Of those that a mesh axis runs over, the one named last changes fastest.
Arguments:
- echoes: float32 [2, 256, 16384], P(None, ('gx', 'gy')), may hold values from -6 to 6
- range_ref: float32 [2, 1024], replicated, may hold values from -0.125 to 0.125
- azimuth_ref: float32 [2, 512], replicated, may hold values from -0.1875 to 0.1875
- shift_bins: int32 [256], P(('gx', 'gy')), may hold values from -28 to 28, as said below
- interp_weights: float32 [256, 8], P(('gx', 'gy')), may hold values from -2.5 to 2.5
Outputs:
- image: float32 [2, 256, 16384], P(None, None, ('gx', 'gy'))
Inputs may be any that keep to these rules, and one draw needn't show every extreme that they name: `shift_bins`: both -28 and 28 occur among the offsets.
All inputs are finite; a program needn't handle non-finite values.
Results may differ from a plain program's by a relative error of at most 0.00007.
Values sent between devices are 32-bit elements; how exact they have to be, the bound alone decides.
No kernel may reach another device: no remote copies, remote signals or barrier semaphores. Data moves between devices by JAX's collectives and lax.ppermute only.
A program may use at most 64 MiB of HBM per device.

v0:
```python
import jax
import jax.numpy as jnp
from jax import lax
from jax.sharding import PartitionSpec as P

TAPS = 8
HALO = 32


def banded_table(values, block):
    padded = jnp.concatenate([values, jnp.zeros((2 * block,), jnp.float32)])
    period = 4 * block
    tiled = jnp.tile(padded, block)[: block * (period - 1)]
    shifted = tiled.reshape(block, period - 1)[:, : 3 * block]
    return shifted.T


def toeplitz_matrix(reference_fn, block):
    real_part = banded_table(reference_fn[0], block)
    imag_part = banded_table(reference_fn[1], block)
    from_real = jnp.stack([real_part, 0.0 - imag_part], axis=1)
    from_imag = jnp.stack([imag_part, real_part], axis=1)
    return jnp.stack([from_real, from_imag], axis=0)


def correlate_range(echoes, range_ref):
    block = range_ref.shape[1] // 2
    lines = echoes.shape[1]
    count = echoes.shape[2] // block
    padded = jnp.pad(echoes, ((0, 0), (0, 0), (block, block))).reshape(2, lines, count + 2, block)
    matrix = toeplitz_matrix(range_ref, block)
    total = None
    for section in range(3):
        term = jnp.einsum(
            "cabj,cjdi->dabi",
            padded[:, :, section : section + count],
            matrix[:, section * block : (section + 1) * block],
            precision=lax.Precision.HIGHEST,
            preferred_element_type=jnp.float32,
        )
        total = term if total is None else total + term
    return total.reshape(2, lines, count * block)


def correlate_azimuth(migrated, azimuth_ref):
    block = azimuth_ref.shape[1] // 2
    lines = migrated.shape[1]
    width = migrated.shape[2]
    count = lines // block
    padded = jnp.pad(migrated, ((0, 0), (block, block), (0, 0))).reshape(2, count + 2, block, width)
    matrix = toeplitz_matrix(azimuth_ref, block)
    total = None
    for section in range(3):
        term = jnp.einsum(
            "cbjr,cjdi->dbir",
            padded[:, section : section + count],
            matrix[:, section * block : (section + 1) * block],
            precision=lax.Precision.HIGHEST,
            preferred_element_type=jnp.float32,
        )
        total = term if total is None else total + term
    return total.reshape(2, lines, width)


def migrate_lines(compressed, shift_bins, interp_weights):
    range_total = compressed.shape[2]
    extended = jnp.pad(compressed, ((0, 0), (0, 0), (HALO, HALO)))
    span = range_total + TAPS - 1
    starts = HALO + shift_bins - (TAPS // 2 - 1)

    def one_line(line, start):
        return lax.dynamic_slice_in_dim(line, start, span, 1)

    shifted = jax.vmap(one_line, in_axes=(1, 0), out_axes=1)(extended, starts)
    migrated = interp_weights[None, :, 0, None] * shifted[:, :, 0:range_total]
    for column in range(1, TAPS):
        migrated = (
            migrated
            + interp_weights[None, :, column, None] * shifted[:, :, column : column + range_total]
        )
    return migrated


def per_device(echoes, range_ref, azimuth_ref, shift_bins, interp_weights):
    lines_here = echoes.shape[1]
    range_total = echoes.shape[2]
    devices_all = lax.axis_size(("gx", "gy"))
    bins = range_total // devices_all
    compressed = correlate_range(echoes, range_ref)
    migrated = migrate_lines(compressed, shift_bins, interp_weights)
    pieces = migrated.reshape(2, lines_here, devices_all, bins)
    moved = lax.all_to_all(pieces, ("gx", "gy"), split_axis=2, concat_axis=1, tiled=True)
    turned = moved.reshape(2, devices_all * lines_here, bins)
    return correlate_azimuth(turned, azimuth_ref)


def solution(mesh):
    placed = (P(None, ("gx", "gy"), None), P(), P(), P(("gx", "gy")), P(("gx", "gy"), None))
    return jax.shard_map(
        per_device,
        mesh=mesh,
        in_specs=placed,
        out_specs=P(None, None, ("gx", "gy")),
        check_vma=False,
    )
```

profile of v0, /device:TPU:0, one launch (start us, length us, event | category | flops | bytes accessed | tf_op | source)
XLA Modules:
  0.0 142.7 jit_solution(4825609409878754734)
XLA Ops:
  0.0 0.8 fusion.55
  0.8 0.5 broadcast_bitcast_fusion
  1.3 2.9 %copy.92 = f32[64,16,8,128]{3,1,2,0:T(8,128)} copy(f32[64,16,8,128]{3,2,1,0:T(8,128)S(1)} %broadcast_bitcast_fusion) | data formatting | bytes 8388608
  4.2 6.8 %reshape.62 = f32[512,2047]{1,0:T(8,128)} reshape(f32[1048064]{0:T(1024)} %bitcast.168) | data formatting | bytes 8384512 | tf_op jit(solution)/shard_map/reshape | solution.py:14
  11.0 3.8 %slice.183 = f32[512,1536]{1,0:T(8,128)} slice(f32[512,2047]{1,0:T(8,128)} %reshape.62), slice={[0:512], [0:1536]} | slice | bytes 6291456 | tf_op jit(solution)/shard_map/slice | solution.py:14
  14.8 3.6 %copy.74 = f32[512,1536]{0,1:T(8,128)} copy(f32[512,1536]{1,0:T(8,128)} %slice.183) | data formatting | bytes 6291456
  18.4 4.0 %fusion.12 = f32[1536,1,512]{2,0,1:T(8,128)} fusion(f32[512,1536]{0,1:T(8,128)} %copy.74), kind=kLoop, calls=%fused_computation.23 | loop fusion | flops 786432 | bytes 6291456 | tf_op jit(solution)/shard_map/stack | solution.py:21
  22.4 0.5 broadcast_bitcast_fusion.1
  22.9 2.9 %copy.91 = f32[64,16,8,128]{3,1,2,0:T(8,128)} copy(f32[64,16,8,128]{3,2,1,0:T(8,128)S(1)} %broadcast_bitcast_fusion.1) | data formatting | bytes 8388608
  25.8 6.8 %reshape.61 = f32[512,2047]{1,0:T(8,128)} reshape(f32[1048064]{0:T(1024)} %bitcast.169) | data formatting | bytes 8384512 | tf_op jit(solution)/shard_map/reshape | solution.py:14
  32.6 3.8 %slice.181 = f32[512,1536]{1,0:T(8,128)} slice(f32[512,2047]{1,0:T(8,128)} %reshape.61), slice={[0:512], [0:1536]} | slice | bytes 6291456 | tf_op jit(solution)/shard_map/slice | solution.py:14
  36.4 3.6 %copy.73 = f32[512,1536]{0,1:T(8,128)} copy(f32[512,1536]{1,0:T(8,128)} %slice.181) | data formatting | bytes 6291456
  40.2 0.4 fusion.54
  40.6 1.5 %copy-done = f32[512,1536]{0,1:T(8,128)S(1)} copy-done((f32[512,1536]{0,1:T(8,128)S(1)}, f32[512,1536]{0,1:T(8,128)}, u32[]{:S(2)}) %copy-start) | copy-done | bytes 3145752
  42.0 1.0 copy-done.2
  43.0 4.8 %maximum_bitcast_fusion = (f32[1,1536,2,512]{3,1,0,2:T(8,128)S(1)}, f32[1,1536,2,512]{3,1,0,2:T(8,128)S(1)}) fusion(f32[1536,1,512]{2,0,1:T(8,128)S(1)} %copy-done.2, f32[1536,1,512]{2,0,1:T(8,128)} %bitcast.174, f32[1536,1,512]{2,0,1:T(8,128)S(1)} %bitcast.167), kind=kLoop, calls=%fused_computation.6 | loop fusion | flops 3145728 | bytes 22020096 | tf_op jit(solution)/shard_map/stack | solution.py:23
  47.8 4.3 %fusion.16 = f32[2,512,8,32]{1,3,2,0:T(8,128)S(1)} fusion(f32[1,1536,2,512]{3,1,0,2:T(8,128)S(1)} %get-tuple-element.31, f32[1,1536,2,512]{3,1,0,2:T(8,128)S(1)} %get-tuple-element.32, f32[2,8,32,512]{3,1,2,0:T(8,128)S(1)} %get-tuple-element.34), kind=kOutput, calls=%fused_computation.29 | convolution fusion | flops 3222274048 | bytes 14680064 | tf_op jit(solution)/shard_map/cabj,cjdi->dabi/dot_general | solution.py:34
  52.1 4.3 %fusion.13 = f32[2,512,8,32]{1,3,2,0:T(8,128)S(1)} fusion(f32[1,1536,2,512]{3,1,0,2:T(8,128)S(1)} %get-tuple-element.32, f32[1,1536,2,512]{3,1,0,2:T(8,128)S(1)} %get-tuple-element.31, f32[2,8,32,512]{3,1,2,0:T(8,128)S(1)} %get-tuple-element.35), kind=kOutput, calls=%fused_computation.28 | convolution fusion | flops 3222274048 | bytes 14680064 | tf_op jit(solution)/shard_map/cabj,cjdi->dabi/dot_general | solution.py:34
  56.4 4.6 %fusion.28 = f32[2,8,32,512]{3,2,1,0:T(8,128)S(1)} fusion(f32[2,512,8,32]{1,3,2,0:T(8,128)S(1)} %fusion.13, f32[2,512,8,32]{1,3,2,0:T(8,128)S(1)} %fusion.16, f32[1,1536,2,512]{3,1,0,2:T(8,128)S(1)} %get-tuple-element.31, f32[1,1536,2,512]{3,1,0,2:T(8,128)S(1)} %get-tuple-element.32, f32[2,8,32,512]{3,1,2,0:T(8,128)S(1)} %get-tuple-element.33), kind=kOutput, calls=%fused_computation.36 | convolution fusion | flops 3222798336 | bytes 16777216 | tf_op jit(solution)/shard_map/cabj,cjdi->dabi/dot_general | solution.py:34
  61.1 0.2 reshape.64
  61.3 0.8 copy.55
  62.1 1.2 pad_bitcast_fusion
  63.3 32.5 %while.1 = (s32[]{:T(128)}, f32[8,2,16448]{2,1,0:T(2,128)S(1)}, s32[8,3]{0,1:T(4,128)S(1)}, f32[8,2,16391]{2,0,1:T(8,128)S(1)}, s32[]{:T(128)}, /*index=5*/s32[]{:T(128)}) while((s32[]{:T(128)}, f32[8,2,16448]{2,1,0:T(2,128)S(1)}, s32[8,3]{0,1:T(4,128)S(1)}, f32[8,2,16391]{2,0,1:T(8,128)S(1)}, s32[]{:T(128)}, /*index=5*/s32[]{:T(128)}) %tuple.33), condition=%wide.while_cond, body=%wide.while_body.sunk | while | flops 2 | bytes 786893 | solution.py:72
  63.4 0.6 fusion.58
  64.0 1.5 %constant_dynamic-slice_fusion.5 = f32[1,2,16391]{2,1,0:T(2,128)S(1)} fusion(f32[8,2,16448]{2,1,0:T(2,128)S(1)} %get-tuple-element.86, s32[]{:T(128)} %bitcast.164, s32[]{:T(128)} %bitcast.165), kind=kLoop, calls=%fused_computation.1.clone.1 | loop fusion | bytes 262264 | tf_op jit(solution)/shard_map/vmap()/gather
  65.6 1.7 %dynamic-update-slice.3 = f32[8,2,16391]{2,0,1:T(8,128)S(1)} dynamic-update-slice(f32[8,2,16391]{2,0,1:T(8,128)S(1)} %get-tuple-element.82, f32[1,2,16391]{2,0,1:T(1,128)S(1)} %copy.104, s32[]{:T(128)} %get-tuple-element.79, s32[]{:T(128)} %constant.6.clone.1..sunk, s32[]{:T(128)} %constant.6.clone.1..sunk) | dynamic-update-slice | bytes 262260 | tf_op jit(solution)/shard_map/vmap()/gather
  67.4 0.6 fusion.58
  68.0 1.5 %constant_dynamic-slice_fusion.5 = f32[1,2,16391]{2,1,0:T(2,128)S(1)} fusion(f32[8,2,16448]{2,1,0:T(2,128)S(1)} %get-tuple-element.86, s32[]{:T(128)} %bitcast.164, s32[]{:T(128)} %bitcast.165), kind=kLoop, calls=%fused_computation.1.clone.1 | loop fusion | bytes 262264 | tf_op jit(solution)/shard_map/vmap()/gather
  69.6 1.8 %dynamic-update-slice.3 = f32[8,2,16391]{2,0,1:T(8,128)S(1)} dynamic-update-slice(f32[8,2,16391]{2,0,1:T(8,128)S(1)} %get-tuple-element.82, f32[1,2,16391]{2,0,1:T(1,128)S(1)} %copy.104, s32[]{:T(128)} %get-tuple-element.79, s32[]{:T(128)} %constant.6.clone.1..sunk, s32[]{:T(128)} %constant.6.clone.1..sunk) | dynamic-update-slice | bytes 262260 | tf_op jit(solution)/shard_map/vmap()/gather
  71.5 0.6 fusion.58
  72.1 1.5 %constant_dynamic-slice_fusion.5 = f32[1,2,16391]{2,1,0:T(2,128)S(1)} fusion(f32[8,2,16448]{2,1,0:T(2,128)S(1)} %get-tuple-element.86, s32[]{:T(128)} %bitcast.164, s32[]{:T(128)} %bitcast.165), kind=kLoop, calls=%fused_computation.1.clone.1 | loop fusion | bytes 262264 | tf_op jit(solution)/shard_map/vmap()/gather
  73.6 0.1 copy.104
  73.7 1.8 %dynamic-update-slice.3 = f32[8,2,16391]{2,0,1:T(8,128)S(1)} dynamic-update-slice(f32[8,2,16391]{2,0,1:T(8,128)S(1)} %get-tuple-element.82, f32[1,2,16391]{2,0,1:T(1,128)S(1)} %copy.104, s32[]{:T(128)} %get-tuple-element.79, s32[]{:T(128)} %constant.6.clone.1..sunk, s32[]{:T(128)} %constant.6.clone.1..sunk) | dynamic-update-slice | bytes 262260 | tf_op jit(solution)/shard_map/vmap()/gather
  75.6 0.6 fusion.58
  76.2 1.5 %constant_dynamic-slice_fusion.5 = f32[1,2,16391]{2,1,0:T(2,128)S(1)} fusion(f32[8,2,16448]{2,1,0:T(2,128)S(1)} %get-tuple-element.86, s32[]{:T(128)} %bitcast.164, s32[]{:T(128)} %bitcast.165), kind=kLoop, calls=%fused_computation.1.clone.1 | loop fusion | bytes 262264 | tf_op jit(solution)/shard_map/vmap()/gather
  77.6 0.1 copy.104
  77.8 1.8 %dynamic-update-slice.3 = f32[8,2,16391]{2,0,1:T(8,128)S(1)} dynamic-update-slice(f32[8,2,16391]{2,0,1:T(8,128)S(1)} %get-tuple-element.82, f32[1,2,16391]{2,0,1:T(1,128)S(1)} %copy.104, s32[]{:T(128)} %get-tuple-element.79, s32[]{:T(128)} %constant.6.clone.1..sunk, s32[]{:T(128)} %constant.6.clone.1..sunk) | dynamic-update-slice | bytes 262260 | tf_op jit(solution)/shard_map/vmap()/gather
  79.7 0.6 fusion.58
  80.3 1.5 %constant_dynamic-slice_fusion.5 = f32[1,2,16391]{2,1,0:T(2,128)S(1)} fusion(f32[8,2,16448]{2,1,0:T(2,128)S(1)} %get-tuple-element.86, s32[]{:T(128)} %bitcast.164, s32[]{:T(128)} %bitcast.165), kind=kLoop, calls=%fused_computation.1.clone.1 | loop fusion | bytes 262264 | tf_op jit(solution)/shard_map/vmap()/gather
  81.9 1.8 %dynamic-update-slice.3 = f32[8,2,16391]{2,0,1:T(8,128)S(1)} dynamic-update-slice(f32[8,2,16391]{2,0,1:T(8,128)S(1)} %get-tuple-element.82, f32[1,2,16391]{2,0,1:T(1,128)S(1)} %copy.104, s32[]{:T(128)} %get-tuple-element.79, s32[]{:T(128)} %constant.6.clone.1..sunk, s32[]{:T(128)} %constant.6.clone.1..sunk) | dynamic-update-slice | bytes 262260 | tf_op jit(solution)/shard_map/vmap()/gather
  83.7 0.6 fusion.58
  84.3 1.5 %constant_dynamic-slice_fusion.5 = f32[1,2,16391]{2,1,0:T(2,128)S(1)} fusion(f32[8,2,16448]{2,1,0:T(2,128)S(1)} %get-tuple-element.86, s32[]{:T(128)} %bitcast.164, s32[]{:T(128)} %bitcast.165), kind=kLoop, calls=%fused_computation.1.clone.1 | loop fusion | bytes 262264 | tf_op jit(solution)/shard_map/vmap()/gather
  85.9 1.8 %dynamic-update-slice.3 = f32[8,2,16391]{2,0,1:T(8,128)S(1)} dynamic-update-slice(f32[8,2,16391]{2,0,1:T(8,128)S(1)} %get-tuple-element.82, f32[1,2,16391]{2,0,1:T(1,128)S(1)} %copy.104, s32[]{:T(128)} %get-tuple-element.79, s32[]{:T(128)} %constant.6.clone.1..sunk, s32[]{:T(128)} %constant.6.clone.1..sunk) | dynamic-update-slice | bytes 262260 | tf_op jit(solution)/shard_map/vmap()/gather
  87.8 0.6 fusion.58
  88.4 1.5 %constant_dynamic-slice_fusion.5 = f32[1,2,16391]{2,1,0:T(2,128)S(1)} fusion(f32[8,2,16448]{2,1,0:T(2,128)S(1)} %get-tuple-element.86, s32[]{:T(128)} %bitcast.164, s32[]{:T(128)} %bitcast.165), kind=kLoop, calls=%fused_computation.1.clone.1 | loop fusion | bytes 262264 | tf_op jit(solution)/shard_map/vmap()/gather
  90.0 1.8 %dynamic-update-slice.3 = f32[8,2,16391]{2,0,1:T(8,128)S(1)} dynamic-update-slice(f32[8,2,16391]{2,0,1:T(8,128)S(1)} %get-tuple-element.82, f32[1,2,16391]{2,0,1:T(1,128)S(1)} %copy.104, s32[]{:T(128)} %get-tuple-element.79, s32[]{:T(128)} %constant.6.clone.1..sunk, s32[]{:T(128)} %constant.6.clone.1..sunk) | dynamic-update-slice | bytes 262260 | tf_op jit(solution)/shard_map/vmap()/gather
  91.9 0.6 fusion.58
  92.5 1.5 %constant_dynamic-slice_fusion.5 = f32[1,2,16391]{2,1,0:T(2,128)S(1)} fusion(f32[8,2,16448]{2,1,0:T(2,128)S(1)} %get-tuple-element.86, s32[]{:T(128)} %bitcast.164, s32[]{:T(128)} %bitcast.165), kind=kLoop, calls=%fused_computation.1.clone.1 | loop fusion | bytes 262264 | tf_op jit(solution)/shard_map/vmap()/gather
  94.1 1.8 %dynamic-update-slice.3 = f32[8,2,16391]{2,0,1:T(8,128)S(1)} dynamic-update-slice(f32[8,2,16391]{2,0,1:T(8,128)S(1)} %get-tuple-element.82, f32[1,2,16391]{2,0,1:T(1,128)S(1)} %copy.104, s32[]{:T(128)} %get-tuple-element.79, s32[]{:T(128)} %constant.6.clone.1..sunk, s32[]{:T(128)} %constant.6.clone.1..sunk) | dynamic-update-slice | bytes 262260 | tf_op jit(solution)/shard_map/vmap()/gather
  95.9 0.3 slice_reduce_fusion.7
  96.2 2.0 %fusion.38 = f32[2,8,16384]{2,1,0:T(8,128)S(1)} fusion(f32[2,8,16391]{2,1,0:T(8,128)S(1)} %bitcast.166, f32[8]{0:T(128)S(1)} %get-tuple-element.19, f32[8]{0:T(128)S(1)} %get-tuple-element.20, f32[8]{0:T(128)S(1)} %get-tuple-element.14, f32[8]{0:T(128)S(1)} %get-tuple-element.15, f32[8]{0:T(128)S(1)} %get-tuple-element.16, f32[8]{0:T(128)S(1)} %get-tuple-element.17, ...), kind=kLoop, calls=%fused_computation.49 | loop fusion | flops 3932160 | bytes 9437440 | tf_op jit(solution)/shard_map/add | solution.py:78
  98.2 1.1 copy.101
  99.2 7.7 %all-to-all-start = ((f32[2,8,32,512]{3,1,0,2:T(8,128)}), f32[2,8,32,512]{3,1,0,2:T(8,128)}, u32[]{:S(2)}, u32[]{:S(2)}) async-start(f32[2,8,32,512]{3,1,0,2:T(8,128)} %bitcast.156), calls=%async_computation | async-start | bytes 2097152 | tf_op jit(solution)/shard_map/all_to_all | solution.py:92
  107.1 0.2 copy.90
  107.3 0.6 reshape.60
  108.1 0.2 copy.89
  108.3 0.6 reshape.59
  109.1 1.4 maximum_bitcast_fusion.2
  110.5 23.8 %all-to-all-done = f32[2,8,32,512]{3,1,0,2:T(8,128)} async-done(((f32[2,8,32,512]{3,1,0,2:T(8,128)}), f32[2,8,32,512]{3,1,0,2:T(8,128)}, u32[]{:S(2)}, u32[]{:S(2)}) %all-to-all-start) | async-done | bytes 1048608 | tf_op jit(solution)/shard_map/all_to_all | solution.py:92
  134.2 1.4 copy.102
  135.7 0.4 pad.19
  136.1 1.8 %convolution_bitcast_fusion.1 = f32[2,256,512]{2,1,0:T(8,128)S(1)} fusion(f32[1,768,2,256]{1,3,0,2:T(8,128)S(1)} %get-tuple-element.36, f32[1,768,2,256]{1,3,0,2:T(8,128)S(1)} %copy-done.1, f32[2,3,256,512]{3,2,1,0:T(8,128)S(1)} %bitcast.171), kind=kOutput, calls=%fused_computation.32 | convolution fusion | flops 1610874880 | bytes 5242880 | tf_op jit(solution)/shard_map/cbjr,cjdi->dbir/dot_general | solution.py:54
  137.9 1.9 %convolution_bitcast_fusion = f32[2,256,512]{2,1,0:T(8,128)S(1)} fusion(f32[2,3,256,512]{3,2,1,0:T(8,128)S(1)} %bitcast.172, f32[1,768,2,256]{1,3,0,2:T(8,128)S(1)} %copy-done.1, f32[1,768,2,256]{1,3,0,2:T(8,128)S(1)} %get-tuple-element.36), kind=kOutput, calls=%fused_computation.31 | convolution fusion | flops 1610874880 | bytes 5242880 | tf_op jit(solution)/shard_map/cbjr,cjdi->dbir/dot_general | solution.py:54
  139.8 2.9 %fusion.32 = f32[2,256,512]{2,1,0:T(8,128)} fusion(f32[2,256,512]{2,1,0:T(8,128)S(1)} %convolution_bitcast_fusion, f32[2,256,512]{2,1,0:T(8,128)S(1)} %convolution_bitcast_fusion.1, f32[1,768,2,256]{1,3,0,2:T(8,128)S(1)} %get-tuple-element.36, f32[1,768,2,256]{1,3,0,2:T(8,128)S(1)} %copy-done.1, f32[2,3,256,512]{3,2,1,0:T(8,128)S(1)} %bitcast.173), kind=kOutput, calls=%fused_computation.38 | convolution fusion | flops 1611399168 | bytes 7340032 | tf_op jit(solution)/shard_map/cbjr,cjdi->dbir/dot_general | solution.py:54
  (40 shorter events, 1.9 us)
Async XLA Ops:
  36.4 3.6 %copy-start.3 = (f32[2,8,16384]{2,1,0:T(8,128)S(1)}, f32[2,8,16384]{2,1,0:T(8,128)}, u32[]{:S(2)}) copy-start(f32[2,8,16384]{2,1,0:T(8,128)} %param.5) | copy-start | bytes 3145732
  40.1 1.9 %copy-start = (f32[512,1536]{0,1:T(8,128)S(1)}, f32[512,1536]{0,1:T(8,128)}, u32[]{:S(2)}) copy-start(f32[512,1536]{0,1:T(8,128)} %copy.74) | copy-start | bytes 9437188
  40.1 2.8 %copy-start.2 = (f32[1536,1,512]{2,0,1:T(8,128)S(1)}, f32[1536,1,512]{2,0,1:T(8,128)}, u32[]{:S(2)}) copy-start(f32[1536,1,512]{2,0,1:T(8,128)} %fusion.12) | copy-start | bytes 9437188
  61.1 2.2 %copy-start.6 = (s32[8]{0:T(128)S(1)}, s32[8]{0:T(128)}, u32[]{:S(2)}) copy-start(s32[8]{0:T(128)} %param.8) | copy-start | bytes 100
  62.1 33.8 %copy-start.4 = (f32[8,8]{1,0:T(8,128)S(1)}, f32[8,8]{1,0:T(8,128)}, u32[]{:S(2)}) copy-start(f32[8,8]{1,0:T(8,128)} %param.9) | copy-start | bytes 772
  98.2 8.8 %copy-start.5 = (f32[2,512]{1,0:T(2,128)S(1)}, f32[2,512]{1,0:T(2,128)}, u32[]{:S(2)}) copy-start(f32[2,512]{1,0:T(2,128)} %param.7) | copy-start | bytes 12292
  99.2 35.0 %all-to-all-start = ((f32[2,8,32,512]{3,1,0,2:T(8,128)}), f32[2,8,32,512]{3,1,0,2:T(8,128)}, u32[]{:S(2)}, u32[]{:S(2)}) async-start(f32[2,8,32,512]{3,1,0,2:T(8,128)} %bitcast.156), calls=%async_computation | async-start | bytes 2097152 | tf_op jit(solution)/shard_map/all_to_all | solution.py:92
  134.2 1.8 %copy-start.1 = (f32[1,768,2,256]{1,3,0,2:T(8,128)S(1)}, f32[1,768,2,256]{1,3,0,2:T(8,128)}, u32[]{:S(2)}) copy-start(f32[1,768,2,256]{1,3,0,2:T(8,128)} %get-tuple-element.37) | copy-start | bytes 4718596
where the time goes:
time: 143 us
  local copies, waits for them, and re-layouts  78.5 us (55%)
  waiting for transfers between devices  23.8 us (17%)
  matrix products  19.8 us (14%)
  other arithmetic  12.3 us (9%)
  starting transfers between devices  7.69 us (5%)
    gather x40, local copies, waits for them, and re-layouts  32.2 us
    all_to_all x1, waiting for transfers between devices, per_device(): lax.all_to_all(pieces, ('gx', 'gy'), split_axis=2, concat_axis=1, tiled=T...  23.8 us
    unnamed x25, local copies, waits for them, and re-layouts  17.1 us
    reshape x4, local copies, waits for them, and re-layouts, banded_table(): shifted = tiled.reshape(block, period - 1)[:, :3 * block]  14.9 us
    dot_general x3, matrix products, correlate_range(): jnp.einsum('cabj,cjdi->dabi', padded[:, :, section:section + count], matr...  13.2 us
    all_to_all x1, starting transfers between devices, per_device(): lax.all_to_all(pieces, ('gx', 'gy'), split_axis=2, concat_axis=1, tiled=T...  7.69 us
    slice x2, local copies, waits for them, and re-layouts, banded_table(): shifted = tiled.reshape(block, period - 1)[:, :3 * block]  7.54 us
    dot_general x3, matrix products, correlate_azimuth(): jnp.einsum('cbjr,cjdi->dbir', padded[:, section:section + count], matrix[...  6.58 us
  transfers between devices with their start and end apart: 1, of which 1 were waited for; matrix products, arithmetic and copies ran while one was open for 2% of the time, Pallas kernels for 0%

commit v1 on v0

v1 whole, which is shorter than its diff:
```python
import functools

import jax
import jax.numpy as jnp
from jax import lax
from jax.experimental import pallas as pl
from jax.experimental.pallas import tpu as pltpu
from jax.sharding import PartitionSpec as P

TAPS = 8
BLOCK = 256
LANE = 128
AXES = ("gx", "gy")
ROWS_BY_ROWS = (((1,), (1,)), ((), ()))
PLAIN = (((1,), (0,)), ((), ()))


def split(values):
    high = values.astype(jnp.bfloat16)
    return high, (values - high.astype(jnp.float32)).astype(jnp.bfloat16)


def toeplitz(row, rows, width):
    row = jnp.concatenate([row, jnp.zeros((1, width - row.shape[1]), jnp.float32)], axis=1)
    return pltpu.roll(jnp.broadcast_to(row, (rows, width)), 0, axis=1, stride=1, stride_axis=0)


def range_kernel(
    component, lines, count, sections,
    shift_hbm, taps_hbm, weights_hbm, echoes_hbm, out_ref,
    shift_ref, taps_ref, weights_ref, echoes_ref, even, odd, table, compressed, sems,
):
    pairs = (
        (taps_hbm, taps_ref), (echoes_hbm, echoes_ref), (shift_hbm, shift_ref), (weights_hbm, weights_ref),
    )
    copies = [pltpu.make_async_copy(src, dst, sems.at[n]) for n, (src, dst) in enumerate(pairs)]
    for copy in copies:
        copy.start()
    half = (sections - 1) // 2
    rows = count * lines
    total = count + 2 * half
    copies[0].wait()
    for part in range(2):
        row = taps_ref[part : part + 1, :]
        if component == 1 and part == 1:
            row = 0.0 - row
        table[part, 0], table[part, 1] = split(toeplitz(row, BLOCK, sections * BLOCK))
    copies[1].wait()
    for part in range(2):
        source = part if component == 0 else 1 - part

        def piece(block):
            at = block - half
            if 0 <= at < count:
                return echoes_ref[source, :, at * BLOCK : (at + 1) * BLOCK]
            return jnp.zeros((lines, BLOCK), jnp.float32)

        for offset, ref in ((0, even), (1, odd)):
            for pair in range((total - offset) // 2):
                first = 2 * pair + offset
                both = jnp.concatenate([piece(first), piece(first + 1)], axis=0)
                at = slice(pair * 2 * lines, (pair + 1) * 2 * lines)
                ref[part, 0, at, :], ref[part, 1, at, :] = split(both)
    sums = None
    for part in range(2):
        for section in range(sections):
            ref = even if section % 2 == 0 else odd
            start = (section - section % 2) * lines
            x_high = ref[part, 0, start : start + rows, :]
            x_low = ref[part, 1, start : start + rows, :]
            at = slice(section * BLOCK, (section + 1) * BLOCK)
            t_high, t_low = table[part, 0, :, at], table[part, 1, :, at]
            for left, right in ((x_high, t_high), (x_low, t_high), (x_high, t_low)):
                term = lax.dot_general(left, right, ROWS_BY_ROWS, preferred_element_type=jnp.float32)
                sums = term if sums is None else sums + term
    compressed[0:lines, :] = jnp.zeros((lines, BLOCK), jnp.float32)
    compressed[lines : lines + rows, :] = sums
    compressed[lines + rows :, :] = jnp.zeros((lines, BLOCK), jnp.float32)
    copies[2].wait()
    copies[3].wait()
    migrate(lines, 2 * count, shift_ref, weights_ref, compressed, out_ref)


def migrate(lines, tiles, shift_ref, weights_ref, compressed, out_ref):
    per = out_ref.shape[2] // LANE
    lane = lax.broadcasted_iota(jnp.int32, (lines, LANE), 1)
    row = lax.broadcasted_iota(jnp.int32, (lines, LANE), 0)
    shift = jnp.zeros((lines, LANE), jnp.int32)
    for line in range(lines):
        shift = jnp.where(row == line, shift_ref[line], shift)
    places = [lane + shift - (TAPS // 2 - 1) + step for step in range(2)]
    index = [place & (LANE - 1) for place in places]
    before = [place < 0 for place in places]
    after = [place >= LANE for place in places]
    weight = [jnp.broadcast_to(weights_ref[:, j : j + 1], (lines, LANE)) for j in range(TAPS)]
    inside = lane < LANE - 2

    def turned(tile, step):
        block = tile // 2 + 1
        at = (tile % 2) * LANE
        values = compressed[block * lines : (block + 1) * lines, at : at + LANE]
        return jnp.take_along_axis(values, index[step], axis=1, mode="promise_in_bounds")

    later = [turned(tiles + 1, step) for step in range(2)]
    here = [turned(tiles, step) for step in range(2)]
    carried = [jnp.zeros((lines, LANE), jnp.float32)] * 3
    for tile in range(tiles, -1, -1):
        earlier = [turned(tile - 1, step) for step in range(2)]
        pair = [
            jnp.where(before[step], earlier[step], jnp.where(after[step], later[step], here[step]))
            for step in range(2)
        ]
        total = None
        for k in (3, 2, 1, 0):
            term = weight[2 * k] * pair[0] + weight[2 * k + 1] * pair[1]
            if total is None:
                total = term
            else:
                rolled = pltpu.roll(total, LANE - 2, axis=1)
                total = jnp.where(inside, rolled, carried[k]) + term
                carried[k] = rolled
        if tile < tiles:
            at = (tile % per) * LANE
            out_ref[tile // per, :, at : at + LANE] = total
        later, here = here, earlier


def range_call(component, echoes, range_ref, shift_bins, weights, devices_all):
    lines, range_total = echoes.shape[1], echoes.shape[2]
    count = range_total // BLOCK
    sections = range_ref.shape[1] // BLOCK + 1
    padded = (count + sections - 1) * lines
    bins = range_total // devices_all
    flops = 2 * 3 * 2 * count * lines * sections * BLOCK * BLOCK
    return pl.pallas_call(
        functools.partial(range_kernel, component, lines, count, sections),
        out_shape=jax.ShapeDtypeStruct((devices_all, lines, bins), jnp.float32),
        in_specs=[pl.BlockSpec(memory_space=pl.ANY)] * 4,
        out_specs=pl.BlockSpec(memory_space=pltpu.VMEM),
        scratch_shapes=[
            pltpu.SMEM(shift_bins.shape, jnp.int32),
            pltpu.VMEM(range_ref.shape, jnp.float32),
            pltpu.VMEM(weights.shape, jnp.float32),
            pltpu.VMEM(echoes.shape, jnp.float32),
            pltpu.VMEM((2, 2, padded, BLOCK), jnp.bfloat16),
            pltpu.VMEM((2, 2, padded, BLOCK), jnp.bfloat16),
            pltpu.VMEM((2, 2, BLOCK, sections * BLOCK), jnp.bfloat16),
            pltpu.VMEM(((count + 2) * lines, BLOCK), jnp.float32),
            pltpu.SemaphoreType.DMA((4,)),
        ],
        compiler_params=pltpu.CompilerParams(vmem_limit_bytes=40 << 20),
        cost_estimate=pl.CostEstimate(flops=flops, bytes_accessed=3 * echoes.size * 2, transcendentals=0),
        name="range_" + str(component),
    )(shift_bins, range_ref, weights, echoes)


def azimuth_tables(taps_ref, table):
    length = taps_ref.shape[1]
    diagonals = table.shape[2]
    for part in range(2):
        row = jnp.concatenate(
            [jnp.zeros((1, BLOCK), jnp.float32), taps_ref[part : part + 1, :]], axis=1
        )
        full = toeplitz(row, BLOCK, length + 2 * BLOCK)
        for diagonal in range(diagonals):
            at = (diagonal + 1) * BLOCK
            table[part, 0, diagonal], table[part, 1, diagonal] = split(full[:, at : at + BLOCK])


def azimuth_kernel(component, *refs):
    if component == 0:
        taps_ref, lines_ref, out_ref, table = refs
    else:
        taps_ref, lines_ref, earlier_ref, out_ref, table = refs
    azimuth_tables(taps_ref, table)
    diagonals = table.shape[2]
    middle = diagonals // 2
    blocks = lines_ref.shape[0] // BLOCK
    pieces = [split(lines_ref[b * BLOCK : (b + 1) * BLOCK, :]) for b in range(blocks)]
    for b in range(blocks):
        at = slice(b * BLOCK, (b + 1) * BLOCK)
        for part in range(2):
            sums = None
            for diagonal in range(diagonals):
                other = b + diagonal - middle
                if not 0 <= other < blocks:
                    continue
                m_high, m_low = pieces[other]
                t_high, t_low = table[part, 0, diagonal], table[part, 1, diagonal]
                for left, right in ((t_high, m_high), (t_high, m_low), (t_low, m_high)):
                    term = lax.dot_general(left, right, PLAIN, preferred_element_type=jnp.float32)
                    sums = term if sums is None else sums + term
            if component == 0:
                out_ref[part, at, :] = sums if part == 0 else 0.0 - sums
            else:
                out_ref[1 - part, at, :] = earlier_ref[1 - part, at, :] + sums


def azimuth_call(component, azimuth_ref, lines, earlier=None):
    count, bins = lines.shape
    diagonals = azimuth_ref.shape[1] // BLOCK + 1
    operands = [azimuth_ref, lines] + ([] if earlier is None else [earlier])
    return pl.pallas_call(
        functools.partial(azimuth_kernel, component),
        out_shape=jax.ShapeDtypeStruct((2, count, bins), jnp.float32),
        in_specs=[pl.BlockSpec(memory_space=pltpu.VMEM)] * len(operands),
        out_specs=pl.BlockSpec(memory_space=pltpu.VMEM),
        scratch_shapes=[pltpu.VMEM((2, 2, diagonals, BLOCK, BLOCK), jnp.bfloat16)],
        compiler_params=pltpu.CompilerParams(vmem_limit_bytes=40 << 20),
        cost_estimate=pl.CostEstimate(
            flops=2 * 3 * 2 * count * BLOCK * bins, bytes_accessed=4 * 3 * count * bins, transcendentals=0
        ),
        name="azimuth_" + str(component),
    )(*operands)


def per_device(echoes, range_ref, azimuth_ref, shift_bins, interp_weights):
    devices_all = lax.axis_size(AXES)
    lines_total = devices_all * echoes.shape[1]
    image = None
    for component in range(2):
        migrated = range_call(component, echoes, range_ref, shift_bins, interp_weights, devices_all)
        moved = lax.all_to_all(migrated, AXES, split_axis=0, concat_axis=0, tiled=True)
        image = azimuth_call(component, azimuth_ref, moved.reshape(lines_total, -1), image)
    return image


def solution(mesh):
    placed = (P(None, AXES, None), P(), P(), P(AXES), P(AXES, None))
    return jax.shard_map(
        per_device,
        mesh=mesh,
        in_specs=placed,
        out_specs=P(None, None, AXES),
        check_vma=False,
    )
```

time: 143 us -> 77 us (0.54)
  local copies, waits for them, and re-layouts: 78.5 us -> 3.29 us
  Pallas kernels: 0 us -> 44.3 us
  matrix products: 19.8 us -> 0 us
  other arithmetic: 12.3 us -> 0 us
  waiting for transfers between devices: 23.8 us -> 15.7 us
  starting transfers between devices: 7.69 us -> 13.1 us
    pallas_call x0 -> x4, Pallas kernels: none -> 44.3 us  [the longest x2 42 us: range_call(): pl.pallas_call(functools.partial(range_kernel, component, lines, count, s...]
    gather x40 -> x0, local copies, waits for them, and re-layouts: 32.2 us -> none
    dot_general x6 -> x0, matrix products: 19.8 us -> none  [the longest x3 13.2 us: correlate_range(): jnp.einsum('cabj,cjdi->dabi', padded[:, :, section:section + count], matr...]
    reshape x7 -> x0, local copies, waits for them, and re-layouts: 17 us -> none  [the longest x4 14.9 us: banded_table(): shifted = tiled.reshape(block, period - 1)[:, :3 * block]]
    unnamed x25 -> x18, local copies, waits for them, and re-layouts: 17.1 us -> 3.29 us
    another operation x4 -> x0, other arithmetic: 10.3 us -> none  [the longest x2 6.25 us: toeplitz_matrix(): return jnp.stack([from_real, from_imag], axis=0)]
    slice x6 -> x0, local copies, waits for them, and re-layouts: 9.02 us -> none  [the longest x2 7.54 us: banded_table(): shifted = tiled.reshape(block, period - 1)[:, :3 * block]]
    all_to_all x1 -> x2, waiting for transfers between devices: 23.8 us -> 15.7 us  [per_device(): lax.all_to_all(migrated, AXES, split_axis=0, concat_axis=0, tiled=True)]
  transfers between devices with their start and end apart: 1 -> 2, of which waited for: 1 -> 1; matrix products, arithmetic and copies ran while one was open for 2% -> 0% of each run, Pallas kernels for 0% -> 28%
where the time goes in v1:
time: 77 us; the launch traced here: 76.5 us
  Pallas kernels  44.3 us (58%)
  waiting for transfers between devices  15.7 us (20%)
  starting transfers between devices  13.1 us (17%)
  local copies, waits for them, and re-layouts  3.29 us (4%)
    pallas_call x2, Pallas kernels, range_call(): pl.pallas_call(functools.partial(range_kernel, component, lines, count, s...  42 us
    all_to_all x2, waiting for transfers between devices, per_device(): lax.all_to_all(migrated, AXES, split_axis=0, concat_axis=0, tiled=True)  15.7 us
    all_to_all x2, starting transfers between devices, per_device(): lax.all_to_all(migrated, AXES, split_axis=0, concat_axis=0, tiled=True)  13.1 us
    unnamed x18, local copies, waits for them, and re-layouts  3.29 us
    pallas_call x2, Pallas kernels, azimuth_call(): pl.pallas_call(functools.partial(azimuth_kernel, component), out_shape=ja...  2.27 us
  transfers between devices with their start and end apart: 2, of which 1 were waited for; matrix products, arithmetic and copies ran while one was open for 0% of the time, Pallas kernels for 28%

profile of v1, /device:TPU:0, one launch (start us, length us, event | category | flops | bytes accessed | tf_op | source)
XLA Modules:
  0.0 76.5 jit_solution(11706344306253083202)
XLA Ops:
  0.0 0.0 copy-start.1
  0.0 1.2 %copy-done.1 = f32[2,8,16384]{2,1,0:T(8,128)S(1)} copy-done((f32[2,8,16384]{2,1,0:T(8,128)S(1)}, f32[2,8,16384]{2,1,0:T(8,128)}, u32[]{:S(2)}) %copy-start.1) | copy-done | bytes 1048600
  1.2 0.0 copy-start.3
  1.2 0.7 copy-done.3
  1.9 0.0 copy-start.5
  1.9 0.7 copy-done.5
  2.6 0.0 copy-start.7
  2.6 0.7 copy-done.7
  3.3 0.0 copy-start.4
  3.3 0.0 copy-start.6
  3.3 0.0 copy-start.8
  3.3 21.0 %range_0.1 = f32[32,8,512]{2,1,0:T(8,128)} custom-call(s32[8]{0:T(128)S(1)} %copy-done.7, f32[2,1024]{1,0:T(2,128)S(1)} %copy-done.3, f32[8,8]{1,0:T(8,128)S(1)} %copy-done.5, f32[2,8,16384]{2,1,0:T(8,128)S(1)} %copy-done.1), custom_call_target="tpu_custom_call" | custom-call | flops 2013265920 | bytes 1572864 | tf_op jit(solution)/shard_map/range_0/pallas_call | solution.py:135
  24.3 0.0 copy-start.2
  24.3 7.3 %all-to-all-start.1 = ((f32[32,8,512]{2,1,0:T(8,128)}), f32[32,8,512]{2,1,0:T(8,128)S(1)}, u32[]{:S(2)}, u32[]{:S(2)}) async-start(f32[32,8,512]{2,1,0:T(8,128)} %range_0.1), calls=%async_computation.1 | async-start | bytes 1048576 | tf_op jit(solution)/shard_map/all_to_all | solution.py:223
  31.6 0.0 copy-done.4
  31.6 0.0 copy-done.6
  31.6 0.0 copy-done.8
  31.7 0.0 copy-done.2
  31.7 21.0 %range_1.1 = f32[32,8,512]{2,1,0:T(8,128)} custom-call(s32[8]{0:T(128)S(1)} %copy-done.8, f32[2,1024]{1,0:T(2,128)S(1)} %copy-done.4, f32[8,8]{1,0:T(8,128)S(1)} %copy-done.6, f32[2,8,16384]{2,1,0:T(8,128)S(1)} %copy-done.2), custom_call_target="tpu_custom_call" | custom-call | flops 2013265920 | bytes 1572864 | tf_op jit(solution)/shard_map/range_1/pallas_call | solution.py:135
  52.7 0.0 all-to-all-done.1
  52.7 0.0 copy-start
  52.7 5.8 %all-to-all-start = ((f32[32,8,512]{2,1,0:T(8,128)}), f32[32,8,512]{2,1,0:T(8,128)S(1)}, u32[]{:S(2)}, u32[]{:S(2)}) async-start(f32[32,8,512]{2,1,0:T(8,128)} %range_1.1), calls=%async_computation | async-start | bytes 1048576 | tf_op jit(solution)/shard_map/all_to_all | solution.py:223
  58.6 0.0 copy-done
  58.6 0.7 azimuth_0.1.refs_2_
  59.2 15.7 %all-to-all-done = f32[32,8,512]{2,1,0:T(8,128)S(1)} async-done(((f32[32,8,512]{2,1,0:T(8,128)}), f32[32,8,512]{2,1,0:T(8,128)S(1)}, u32[]{:S(2)}, u32[]{:S(2)}) %all-to-all-start) | async-done | bytes 524320 | tf_op jit(solution)/shard_map/all_to_all | solution.py:223
  74.9 1.6 %azimuth_1.1 = f32[2,256,512]{2,1,0:T(8,128)} custom-call(f32[2,512]{1,0:T(2,128)S(1)} %copy-done, f32[256,512]{1,0:T(8,128)S(1)} %bitcast.3, f32[2,256,512]{2,1,0:T(8,128)S(1)} %azimuth_0.1.refs_2_), custom_call_target="tpu_custom_call" | custom-call | flops 402653184 | bytes 1572864 | tf_op jit(solution)/shard_map/azimuth_1/pallas_call | solution.py:203
Async XLA Ops:
  0.0 1.2 %copy-start.1 = (f32[2,8,16384]{2,1,0:T(8,128)S(1)}, f32[2,8,16384]{2,1,0:T(8,128)}, u32[]{:S(2)}) copy-start(f32[2,8,16384]{2,1,0:T(8,128)} %echoes_hbm.3) | copy-start | bytes 3145732
  1.2 0.7 copy-start.3
  1.9 0.7 copy-start.5
  2.6 0.7 copy-start.7
  3.3 28.4 %copy-start.4 = (f32[2,1024]{1,0:T(2,128)S(1)}, f32[2,1024]{1,0:T(2,128)}, u32[]{:S(2)}) copy-start(f32[2,1024]{1,0:T(2,128)} %taps_hbm.3) | copy-start | bytes 24580
  3.3 28.4 %copy-start.6 = (f32[8,8]{1,0:T(8,128)S(1)}, f32[8,8]{1,0:T(8,128)}, u32[]{:S(2)}) copy-start(f32[8,8]{1,0:T(8,128)} %weights_hbm.3) | copy-start | bytes 772
  3.3 28.4 %copy-start.8 = (s32[8]{0:T(128)S(1)}, s32[8]{0:T(128)}, u32[]{:S(2)}) copy-start(s32[8]{0:T(128)} %shift_hbm.3) | copy-start | bytes 100
  24.3 7.4 %copy-start.2 = (f32[2,8,16384]{2,1,0:T(8,128)S(1)}, f32[2,8,16384]{2,1,0:T(8,128)}, u32[]{:S(2)}) copy-start(f32[2,8,16384]{2,1,0:T(8,128)} %echoes_hbm.3) | copy-start | bytes 3145732
  24.3 28.4 %all-to-all-start.1 = ((f32[32,8,512]{2,1,0:T(8,128)}), f32[32,8,512]{2,1,0:T(8,128)S(1)}, u32[]{:S(2)}, u32[]{:S(2)}) async-start(f32[32,8,512]{2,1,0:T(8,128)} %range_0.1), calls=%async_computation.1 | async-start | bytes 1048576 | tf_op jit(solution)/shard_map/all_to_all | solution.py:223
  52.7 5.9 %copy-start = (f32[2,512]{1,0:T(2,128)S(1)}, f32[2,512]{1,0:T(2,128)}, u32[]{:S(2)}) copy-start(f32[2,512]{1,0:T(2,128)} %refs_0_.3) | copy-start | bytes 12292
  52.7 22.2 %all-to-all-start = ((f32[32,8,512]{2,1,0:T(8,128)}), f32[32,8,512]{2,1,0:T(8,128)S(1)}, u32[]{:S(2)}, u32[]{:S(2)}) async-start(f32[32,8,512]{2,1,0:T(8,128)} %range_1.1), calls=%async_computation | async-start | bytes 1048576 | tf_op jit(solution)/shard_map/all_to_all | solution.py:223

commit v2 on v1

--- a/solution.py
+++ b/solution.py
@@ -27,12 +27,10 @@
 
 def range_kernel(
     component, lines, count, sections,
-    shift_hbm, taps_hbm, weights_hbm, echoes_hbm, out_ref,
-    shift_ref, taps_ref, weights_ref, echoes_ref, even, odd, table, compressed, sems,
+    shift_ref, taps_hbm, weights_hbm, echoes_hbm, out_ref,
+    taps_ref, weights_ref, echoes_ref, even, odd, table, compressed, sems,
 ):
-    pairs = (
-        (taps_hbm, taps_ref), (echoes_hbm, echoes_ref), (shift_hbm, shift_ref), (weights_hbm, weights_ref),
-    )
+    pairs = ((taps_hbm, taps_ref), (echoes_hbm, echoes_ref), (weights_hbm, weights_ref))
     copies = [pltpu.make_async_copy(src, dst, sems.at[n]) for n, (src, dst) in enumerate(pairs)]
     for copy in copies:
         copy.start()
@@ -40,6 +38,7 @@
     rows = count * lines
     total = count + 2 * half
     copies[0].wait()
+    copies[2].wait()
     for part in range(2):
         row = taps_ref[part : part + 1, :]
         if component == 1 and part == 1:
@@ -76,8 +75,6 @@
     compressed[0:lines, :] = jnp.zeros((lines, BLOCK), jnp.float32)
     compressed[lines : lines + rows, :] = sums
     compressed[lines + rows :, :] = jnp.zeros((lines, BLOCK), jnp.float32)
-    copies[2].wait()
-    copies[3].wait()
     migrate(lines, 2 * count, shift_ref, weights_ref, compressed, out_ref)
 
 
@@ -135,10 +132,9 @@
     return pl.pallas_call(
         functools.partial(range_kernel, component, lines, count, sections),
         out_shape=jax.ShapeDtypeStruct((devices_all, lines, bins), jnp.float32),
-        in_specs=[pl.BlockSpec(memory_space=pl.ANY)] * 4,
+        in_specs=[pl.BlockSpec(memory_space=pltpu.SMEM)] + [pl.BlockSpec(memory_space=pltpu.HBM)] * 3,
         out_specs=pl.BlockSpec(memory_space=pltpu.VMEM),
         scratch_shapes=[
-            pltpu.SMEM(shift_bins.shape, jnp.int32),
             pltpu.VMEM(range_ref.shape, jnp.float32),
             pltpu.VMEM(weights.shape, jnp.float32),
             pltpu.VMEM(echoes.shape, jnp.float32),
@@ -146,9 +142,9 @@
             pltpu.VMEM((2, 2, padded, BLOCK), jnp.bfloat16),
             pltpu.VMEM((2, 2, BLOCK, sections * BLOCK), jnp.bfloat16),
             pltpu.VMEM(((count + 2) * lines, BLOCK), jnp.float32),
-            pltpu.SemaphoreType.DMA((4,)),
+            pltpu.SemaphoreType.DMA((3,)),
         ],
-        compiler_params=pltpu.CompilerParams(vmem_limit_bytes=40 << 20),
+        compiler_params=pltpu.CompilerParams(vmem_limit_bytes=60 << 20),
         cost_estimate=pl.CostEstimate(flops=flops, bytes_accessed=3 * echoes.size * 2, transcendentals=0),
         name="range_" + str(component),
     )(shift_bins, range_ref, weights, echoes)

time: 77 us -> 50.8 us (0.66)
  Pallas kernels: 44.3 us -> 14.1 us
  waiting for transfers between devices: 15.7 us -> 26.1 us
  local copies, waits for them, and re-layouts: 3.29 us -> 0.01 us
  starting transfers between devices: 13.1 us -> 10 us
    pallas_call x2, Pallas kernels: 42 us -> 11.8 us  [range_call(): pl.pallas_call(functools.partial(range_kernel, component, lines, count, s...]
    all_to_all x2, waiting for transfers between devices: 15.7 us -> 26.1 us  [per_device(): lax.all_to_all(migrated, AXES, split_axis=0, concat_axis=0, tiled=True)]
    unnamed x18 -> x2, local copies, waits for them, and re-layouts: 3.29 us -> 0.01 us
    all_to_all x2, starting transfers between devices: 13.1 us -> 10 us  [per_device(): lax.all_to_all(migrated, AXES, split_axis=0, concat_axis=0, tiled=True)]
  transfers between devices with their start and end apart: 2 -> 2, of which waited for: 1 -> 2; matrix products, arithmetic and copies ran while one was open for 0% -> 0% of each run, Pallas kernels for 28% -> 13%
where the time goes in v2:
time: 50.8 us; the launch traced here: 50.3 us
  waiting for transfers between devices  26.1 us (51%)
  Pallas kernels  14.1 us (28%)
  starting transfers between devices  10 us (20%)
    all_to_all x2, waiting for transfers between devices, per_device(): lax.all_to_all(migrated, AXES, split_axis=0, concat_axis=0, tiled=True)  26.1 us
    pallas_call x2, Pallas kernels, range_call(): pl.pallas_call(functools.partial(range_kernel, component, lines, count, s...  11.8 us
    all_to_all x2, starting transfers between devices, per_device(): lax.all_to_all(migrated, AXES, split_axis=0, concat_axis=0, tiled=True)  10 us
    pallas_call x2, Pallas kernels, azimuth_call(): pl.pallas_call(functools.partial(azimuth_kernel, component), out_shape=ja...  2.28 us
  transfers between devices with their start and end apart: 2, of which 2 were waited for; matrix products, arithmetic and copies ran while one was open for 0% of the time, Pallas kernels for 13%

profile of v2, /device:TPU:0, one launch (start us, length us, event | category | flops | bytes accessed | tf_op | source)
XLA Modules:
  0.0 50.3 jit_solution(3307813923086329166)
XLA Ops:
  0.0 5.9 %range_0.1 = f32[32,8,512]{2,1,0:T(8,128)} custom-call(s32[8]{0:T(128)} %shift_ref.3, f32[2,1024]{1,0:T(2,128)} %taps_hbm.3, f32[8,8]{1,0:T(8,128)} %weights_hbm.3, f32[2,8,16384]{2,1,0:T(8,128)} %echoes_hbm.3), custom_call_target="tpu_custom_call" | custom-call | flops 2013265920 | bytes 1572864 | tf_op jit(solution)/shard_map/range_0/pallas_call | solution.py:132
  5.9 7.3 %all-to-all-start.1 = ((f32[32,8,512]{2,1,0:T(8,128)}), f32[32,8,512]{2,1,0:T(8,128)S(1)}, u32[]{:S(2)}, u32[]{:S(2)}) async-start(f32[32,8,512]{2,1,0:T(8,128)} %range_0.1), calls=%async_computation.1 | async-start | bytes 1048576 | tf_op jit(solution)/shard_map/all_to_all | solution.py:219
  13.2 5.9 %range_1.1 = f32[32,8,512]{2,1,0:T(8,128)} custom-call(s32[8]{0:T(128)} %shift_ref.3, f32[2,1024]{1,0:T(2,128)} %taps_hbm.3, f32[8,8]{1,0:T(8,128)} %weights_hbm.3, f32[2,8,16384]{2,1,0:T(8,128)} %echoes_hbm.3), custom_call_target="tpu_custom_call" | custom-call | flops 2013265920 | bytes 1572864 | tf_op jit(solution)/shard_map/range_1/pallas_call | solution.py:132
  19.1 10.4 %all-to-all-done.1 = f32[32,8,512]{2,1,0:T(8,128)S(1)} async-done(((f32[32,8,512]{2,1,0:T(8,128)}), f32[32,8,512]{2,1,0:T(8,128)S(1)}, u32[]{:S(2)}, u32[]{:S(2)}) %all-to-all-start.1) | async-done | bytes 524320 | tf_op jit(solution)/shard_map/all_to_all | solution.py:219
  29.6 0.0 copy-start
  29.6 2.7 %all-to-all-start = ((f32[32,8,512]{2,1,0:T(8,128)}), f32[32,8,512]{2,1,0:T(8,128)S(1)}, u32[]{:S(2)}, u32[]{:S(2)}) async-start(f32[32,8,512]{2,1,0:T(8,128)} %range_1.1), calls=%async_computation | async-start | bytes 1048576 | tf_op jit(solution)/shard_map/all_to_all | solution.py:219
  32.3 0.0 copy-done
  32.3 0.6 %azimuth_0.1.refs_2_ = f32[2,256,512]{2,1,0:T(8,128)S(1)} custom-call(f32[2,512]{1,0:T(2,128)S(1)} %copy-done, f32[256,512]{1,0:T(8,128)S(1)} %bitcast.2), custom_call_target="tpu_custom_call" | custom-call | flops 402653184 | bytes 1572864 | tf_op jit(solution)/shard_map/azimuth_0/pallas_call | solution.py:199
  33.0 15.7 %all-to-all-done = f32[32,8,512]{2,1,0:T(8,128)S(1)} async-done(((f32[32,8,512]{2,1,0:T(8,128)}), f32[32,8,512]{2,1,0:T(8,128)S(1)}, u32[]{:S(2)}, u32[]{:S(2)}) %all-to-all-start) | async-done | bytes 524320 | tf_op jit(solution)/shard_map/all_to_all | solution.py:219
  48.7 1.6 %azimuth_1.1 = f32[2,256,512]{2,1,0:T(8,128)} custom-call(f32[2,512]{1,0:T(2,128)S(1)} %copy-done, f32[256,512]{1,0:T(8,128)S(1)} %bitcast.3, f32[2,256,512]{2,1,0:T(8,128)S(1)} %azimuth_0.1.refs_2_), custom_call_target="tpu_custom_call" | custom-call | flops 402653184 | bytes 1572864 | tf_op jit(solution)/shard_map/azimuth_1/pallas_call | solution.py:199
Async XLA Ops:
  5.9 23.7 %all-to-all-start.1 = ((f32[32,8,512]{2,1,0:T(8,128)}), f32[32,8,512]{2,1,0:T(8,128)S(1)}, u32[]{:S(2)}, u32[]{:S(2)}) async-start(f32[32,8,512]{2,1,0:T(8,128)} %range_0.1), calls=%async_computation.1 | async-start | bytes 1048576 | tf_op jit(solution)/shard_map/all_to_all | solution.py:219
  29.6 2.8 %copy-start = (f32[2,512]{1,0:T(2,128)S(1)}, f32[2,512]{1,0:T(2,128)}, u32[]{:S(2)}) copy-start(f32[2,512]{1,0:T(2,128)} %refs_0_.3) | copy-start | bytes 12292
  29.6 19.1 %all-to-all-start = ((f32[32,8,512]{2,1,0:T(8,128)}), f32[32,8,512]{2,1,0:T(8,128)S(1)}, u32[]{:S(2)}, u32[]{:S(2)}) async-start(f32[32,8,512]{2,1,0:T(8,128)} %range_1.1), calls=%async_computation | async-start | bytes 1048576 | tf_op jit(solution)/shard_map/all_to_all | solution.py:219

commit v3 on v2

--- a/solution.py
+++ b/solution.py
@@ -11,6 +11,7 @@
 BLOCK = 256
 LANE = 128
 AXES = ("gx", "gy")
+LEVELS = 4
 ROWS_BY_ROWS = (((1,), (1,)), ((), ()))
 PLAIN = (((1,), (0,)), ((), ()))
 
@@ -25,11 +26,11 @@
     return pltpu.roll(jnp.broadcast_to(row, (rows, width)), 0, axis=1, stride=1, stride_axis=0)
 
 
-def range_kernel(
-    component, lines, count, sections,
-    shift_ref, taps_hbm, weights_hbm, echoes_hbm, out_ref,
-    taps_ref, weights_ref, echoes_ref, even, odd, table, compressed, sems,
-):
+def range_kernel(component, lines, count, sections, shift_ref, taps_hbm, weights_hbm, echoes_hbm, *refs):
+    if component == 0:
+        *outs, taps_ref, weights_ref, echoes_ref, even, odd, table, compressed, sems, ready, out_sems = refs
+    else:
+        ready, taps_ref, weights_ref, echoes_ref, even, odd, table, compressed, sems = refs
     pairs = ((taps_hbm, taps_ref), (echoes_hbm, echoes_ref), (weights_hbm, weights_ref))
     copies = [pltpu.make_async_copy(src, dst, sems.at[n]) for n, (src, dst) in enumerate(pairs)]
     for copy in copies:
@@ -75,11 +76,27 @@
     compressed[0:lines, :] = jnp.zeros((lines, BLOCK), jnp.float32)
     compressed[lines : lines + rows, :] = sums
     compressed[lines + rows :, :] = jnp.zeros((lines, BLOCK), jnp.float32)
-    migrate(lines, 2 * count, shift_ref, weights_ref, compressed, out_ref)
+    migrate(lines, 2 * count, shift_ref, weights_ref, compressed, ready)
+    if component == 0:
+        mine = lax.axis_index("gy") // (ready.shape[2])
+        sends = []
+        for k, out in enumerate(outs):
+            sends.append(pltpu.make_async_copy(ready.at[:, mine ^ k], out, out_sems.at[k]))
+            sends[-1].start()
+        for send in sends:
+            send.wait()
+
+
+def place_of(device, shape):
+    at = []
+    for extent in reversed(shape[:-2]):
+        at.insert(0, device % extent)
+        device //= extent
+    return at
 
 
 def migrate(lines, tiles, shift_ref, weights_ref, compressed, out_ref):
-    per = out_ref.shape[2] // LANE
+    per = out_ref.shape[-1] // LANE
     lane = lax.broadcasted_iota(jnp.int32, (lines, LANE), 1)
     row = lax.broadcasted_iota(jnp.int32, (lines, LANE), 0)
     shift = jnp.zeros((lines, LANE), jnp.int32)
@@ -118,36 +135,79 @@
                 carried[k] = rolled
         if tile < tiles:
             at = (tile % per) * LANE
-            out_ref[tile // per, :, at : at + LANE] = total
+            out_ref[(*place_of(tile // per, out_ref.shape), slice(None), slice(at, at + LANE))] = total
         later, here = here, earlier
 
 
-def range_call(component, echoes, range_ref, shift_bins, weights, devices_all):
+def range_call(component, echoes, range_ref, shift_bins, weights, planes):
     lines, range_total = echoes.shape[1], echoes.shape[2]
     count = range_total // BLOCK
     sections = range_ref.shape[1] // BLOCK + 1
     padded = (count + sections - 1) * lines
-    bins = range_total // devices_all
+    outer, levels, inner = planes
+    bins = range_total // (outer * levels * inner)
     flops = 2 * 3 * 2 * count * lines * sections * BLOCK * BLOCK
+    scratch = [
+        pltpu.VMEM(range_ref.shape, jnp.float32),
+        pltpu.VMEM(weights.shape, jnp.float32),
+        pltpu.VMEM(echoes.shape, jnp.float32),
+        pltpu.VMEM((2, 2, padded, BLOCK), jnp.bfloat16),
+        pltpu.VMEM((2, 2, padded, BLOCK), jnp.bfloat16),
+        pltpu.VMEM((2, 2, BLOCK, sections * BLOCK), jnp.bfloat16),
+        pltpu.VMEM(((count + 2) * lines, BLOCK), jnp.float32),
+        pltpu.SemaphoreType.DMA((3,)),
+    ]
+    if component == 0:
+        out_shape = [jax.ShapeDtypeStruct((outer, inner, lines, bins), jnp.float32)] * levels
+        out_specs = [pl.BlockSpec(memory_space=pltpu.HBM)] * levels
+        scratch += [
+            pltpu.VMEM((outer, levels, inner, lines, bins), jnp.float32),
+            pltpu.SemaphoreType.DMA((levels,)),
+        ]
+    else:
+        out_shape = jax.ShapeDtypeStruct((outer * levels * inner, lines, bins), jnp.float32)
+        out_specs = pl.BlockSpec(memory_space=pltpu.VMEM)
     return pl.pallas_call(
         functools.partial(range_kernel, component, lines, count, sections),
-        out_shape=jax.ShapeDtypeStruct((devices_all, lines, bins), jnp.float32),
+        out_shape=out_shape,
         in_specs=[pl.BlockSpec(memory_space=pltpu.SMEM)] + [pl.BlockSpec(memory_space=pltpu.HBM)] * 3,
-        out_specs=pl.BlockSpec(memory_space=pltpu.VMEM),
-        scratch_shapes=[
-            pltpu.VMEM(range_ref.shape, jnp.float32),
-            pltpu.VMEM(weights.shape, jnp.float32),
-            pltpu.VMEM(echoes.shape, jnp.float32),
-            pltpu.VMEM((2, 2, padded, BLOCK), jnp.bfloat16),
-            pltpu.VMEM((2, 2, padded, BLOCK), jnp.bfloat16),
-            pltpu.VMEM((2, 2, BLOCK, sections * BLOCK), jnp.bfloat16),
-            pltpu.VMEM(((count + 2) * lines, BLOCK), jnp.float32),
-            pltpu.SemaphoreType.DMA((3,)),
-        ],
+        out_specs=out_specs,
+        scratch_shapes=scratch,
         compiler_params=pltpu.CompilerParams(vmem_limit_bytes=60 << 20),
         cost_estimate=pl.CostEstimate(flops=flops, bytes_accessed=3 * echoes.size * 2, transcendentals=0),
         name="range_" + str(component),
     )(shift_bins, range_ref, weights, echoes)
+
+
+def regroup_kernel(levels, plane, *refs):
+    sources, outs, sems = refs[:levels], refs[levels:-1], refs[-1]
+    inner = sources[0].shape[1]
+    mine = lax.axis_index("gx") * inner + lax.rem(lax.axis_index("gy"), inner)
+    copies = []
+    for q in range(plane):
+        place = mine ^ q
+        for k in range(levels):
+            source = sources[k].at[place // inner, lax.rem(place, inner)]
+            copies.append(pltpu.make_async_copy(source, outs[q].at[k], sems.at[q, k]))
+            copies[-1].start()
+    for copy in copies:
+        copy.wait()
+
+
+def regroup_call(received):
+    levels = len(received)
+    outer, inner, lines, bins = received[0].shape
+    plane = outer * inner
+    return pl.pallas_call(
+        functools.partial(regroup_kernel, levels, plane),
+        out_shape=[jax.ShapeDtypeStruct((levels, lines, bins), jnp.float32)] * plane,
+        in_specs=[pl.BlockSpec(memory_space=pl.ANY)] * levels,
+        out_specs=[pl.BlockSpec(memory_space=pltpu.HBM)] * plane,
+        scratch_shapes=[pltpu.SemaphoreType.DMA((plane, levels))],
+        compiler_params=pltpu.CompilerParams(vmem_limit_bytes=8 << 20),
+        cost_estimate=pl.CostEstimate(flops=0, bytes_accessed=8 * levels * plane * lines * bins, transcendentals=0),
+        name="regroup",
+    )(*received)
 
 
 def azimuth_tables(taps_ref, table):
@@ -163,12 +223,7 @@
             table[part, 0, diagonal], table[part, 1, diagonal] = split(full[:, at : at + BLOCK])
 
 
-def azimuth_kernel(component, *refs):
-    if component == 0:
-        taps_ref, lines_ref, out_ref, table = refs
-    else:
-        taps_ref, lines_ref, earlier_ref, out_ref, table = refs
-    azimuth_tables(taps_ref, table)
+def azimuth_sums(table, lines_ref):
     diagonals = table.shape[2]
     middle = diagonals // 2
     blocks = lines_ref.shape[0] // BLOCK
@@ -186,39 +241,97 @@
                 for left, right in ((t_high, m_high), (t_high, m_low), (t_low, m_high)):
                     term = lax.dot_general(left, right, PLAIN, preferred_element_type=jnp.float32)
                     sums = term if sums is None else sums + term
-            if component == 0:
-                out_ref[part, at, :] = sums if part == 0 else 0.0 - sums
-            else:
-                out_ref[1 - part, at, :] = earlier_ref[1 - part, at, :] + sums
-
-
-def azimuth_call(component, azimuth_ref, lines, earlier=None):
-    count, bins = lines.shape
+            yield part, at, sums
+
+
+def azimuth_first(planes, *refs):
+    outer, levels, inner = planes
+    taps_ref, *sources, out_ref, table, lines_ref, sems = refs
+    lines = sources[0].shape[1]
+    level = lax.axis_index("gy") // inner
+    place = lax.axis_index("gx") * inner + lax.rem(lax.axis_index("gy"), inner)
+    copies = []
+    for q, source in enumerate(sources):
+        other = place ^ q
+        for k in range(levels):
+            device = ((other // inner) * levels + (level ^ k)) * inner + lax.rem(other, inner)
+            rows = pl.ds(pl.multiple_of(device * lines, lines), lines)
+            copies.append(pltpu.make_async_copy(source.at[k], lines_ref.at[rows], sems.at[q, k]))
+            copies[-1].start()
+    for copy in copies:
+        copy.wait()
+    azimuth_tables(taps_ref, table)
+    for part, at, sums in azimuth_sums(table, lines_ref):
+        out_ref[part, at, :] = sums if part == 0 else 0.0 - sums
+
+
+def azimuth_second(taps_ref, lines_ref, earlier_ref, out_ref, table):
+    azimuth_tables(taps_ref, table)
+    for part, at, sums in azimuth_sums(table, lines_ref):
+        out_ref[1 - part, at, :] = earlier_ref[1 - part, at, :] + sums
+
+
+def azimuth_call(azimuth_ref, lines, planes, earlier=None):
+    outer, levels, inner = planes
+    bins = lines[0].shape[-1]
+    count = sum(array.size for array in lines) // bins
     diagonals = azimuth_ref.shape[1] // BLOCK + 1
-    operands = [azimuth_ref, lines] + ([] if earlier is None else [earlier])
+    vmem = pl.BlockSpec(memory_space=pltpu.VMEM)
+    scratch = [pltpu.VMEM((2, 2, diagonals, BLOCK, BLOCK), jnp.bfloat16)]
+    if earlier is None:
+        kernel = functools.partial(azimuth_first, planes)
+        operands = [azimuth_ref, *lines]
+        in_specs = [vmem] + [pl.BlockSpec(memory_space=pl.ANY)] * len(lines)
+        scratch += [pltpu.VMEM((count, bins), jnp.float32), pltpu.SemaphoreType.DMA((outer * inner, levels))]
+    else:
+        kernel = azimuth_second
+        operands = [azimuth_ref, lines[0].reshape(count, bins), earlier]
+        in_specs = [vmem] * 3
     return pl.pallas_call(
-        functools.partial(azimuth_kernel, component),
+        kernel,
         out_shape=jax.ShapeDtypeStruct((2, count, bins), jnp.float32),
-        in_specs=[pl.BlockSpec(memory_space=pltpu.VMEM)] * len(operands),
-        out_specs=pl.BlockSpec(memory_space=pltpu.VMEM),
-        scratch_shapes=[pltpu.VMEM((2, 2, diagonals, BLOCK, BLOCK), jnp.bfloat16)],
+        in_specs=in_specs,
+        out_specs=vmem,
+        scratch_shapes=scratch,
         compiler_params=pltpu.CompilerParams(vmem_limit_bytes=40 << 20),
         cost_estimate=pl.CostEstimate(
-            flops=2 * 3 * 2 * count * BLOCK * bins, bytes_accessed=4 * 3 * count * bins, transcendentals=0
+            flops=20 * 2 * 3 * 2 * count * BLOCK * bins, bytes_accessed=4 * 3 * count * bins, transcendentals=0
         ),
-        name="azimuth_" + str(component),
+        name="azimuth_" + ("first" if earlier is None else "second"),
     )(*operands)
 
 
+def pairs_of(planes, level_step, place_step):
+    outer, levels, inner = planes
+    pairs = []
+    for device in range(outer * levels * inner):
+        place = (device // (levels * inner)) * inner + device % inner
+        level = (device // inner) % levels
+        place, level = place ^ place_step, level ^ level_step
+        pairs.append((device, ((place // inner) * levels + level) * inner + place % inner))
+    return pairs
+
+
 def per_device(echoes, range_ref, azimuth_ref, shift_bins, interp_weights):
-    devices_all = lax.axis_size(AXES)
-    lines_total = devices_all * echoes.shape[1]
-    image = None
-    for component in range(2):
-        migrated = range_call(component, echoes, range_ref, shift_bins, interp_weights, devices_all)
-        moved = lax.all_to_all(migrated, AXES, split_axis=0, concat_axis=0, tiled=True)
-        image = azimuth_call(component, azimuth_ref, moved.reshape(lines_total, -1), image)
-    return image
+    outer, level_all = lax.axis_size("gx"), lax.axis_size("gy")
+    levels = LEVELS
+    planes = (outer, levels, level_all // levels)
+    inputs = (echoes, range_ref, shift_bins, interp_weights)
+    by_level = range_call(0, *inputs, planes)
+    *by_level, shift_later = lax.optimization_barrier((*by_level, shift_bins))
+    later = (echoes, range_ref, shift_later, interp_weights)
+    received = [by_level[0]] + [
+        lax.ppermute(by_level[k], AXES, pairs_of(planes, k, 0)) for k in range(1, levels)
+    ]
+    migrated = range_call(1, *later, planes)
+    moved = lax.all_to_all(migrated, AXES, split_axis=0, concat_axis=0, tiled=True)
+    *received, migrated = lax.optimization_barrier((*received, migrated))
+    by_place = regroup_call(received)
+    first = [by_place[0]] + [
+        lax.ppermute(by_place[q], AXES, pairs_of(planes, 0, q)) for q in range(1, planes[0] * planes[2])
+    ]
+    image = azimuth_call(azimuth_ref, first, planes)
+    return azimuth_call(azimuth_ref, [moved], planes, image)
 
 
 def solution(mesh):

time: 50.8 us -> 43.5 us (0.86)
  waiting for transfers between devices: 26.1 us -> 6.26 us
  starting transfers between devices: 10 us -> 20 us
  Pallas kernels: 14.1 us -> 16.3 us
    all_to_all x2 -> x1, waiting for transfers between devices: 26.1 us -> 0.01 us  [per_device(): lax.all_to_all(migrated, AXES, split_axis=0, concat_axis=0, tiled=True)]
    ppermute x0 -> x10, starting transfers between devices: none -> 13.9 us  [the longest x7 8.25 us: per_device(): lax.ppermute(by_place[q], AXES, pairs_of(planes, 0, q))]
    ppermute x0 -> x10, waiting for transfers between devices: none -> 6.26 us  [the longest x7 6.25 us: per_device(): lax.ppermute(by_place[q], AXES, pairs_of(planes, 0, q))]
    all_to_all x2 -> x1, starting transfers between devices: 10 us -> 6.07 us  [per_device(): lax.all_to_all(migrated, AXES, split_axis=0, concat_axis=0, tiled=True)]
    pallas_call x2 -> x3, Pallas kernels: 2.28 us -> 4.51 us  [the longest x2 3.41 us: azimuth_call(): pl.pallas_call(kernel, out_shape=jax.ShapeDtypeStruct((2, count, bins), j...]
  transfers between devices with their start and end apart: 2 -> 11, of which waited for: 2 -> 4; matrix products, arithmetic and copies ran while one was open for 0% -> 0% of each run, Pallas kernels for 13% -> 21%
where the time goes in v3:
time: 43.5 us; the launch traced here: 42.7 us
  starting transfers between devices  20 us (46%)
  Pallas kernels  16.3 us (37%)
  waiting for transfers between devices  6.26 us (14%)
    pallas_call x2, Pallas kernels, range_call(): pl.pallas_call(functools.partial(range_kernel, component, lines, count, s...  11.8 us
    ppermute x7, starting transfers between devices, per_device(): lax.ppermute(by_place[q], AXES, pairs_of(planes, 0, q))  8.25 us
    ppermute x7, waiting for transfers between devices, per_device(): lax.ppermute(by_place[q], AXES, pairs_of(planes, 0, q))  6.25 us
    all_to_all x1, starting transfers between devices, per_device(): lax.all_to_all(migrated, AXES, split_axis=0, concat_axis=0, tiled=True)  6.07 us
    ppermute x3, starting transfers between devices, per_device(): lax.ppermute(by_level[k], AXES, pairs_of(planes, k, 0))  5.68 us
    pallas_call x2, Pallas kernels, azimuth_call(): pl.pallas_call(kernel, out_shape=jax.ShapeDtypeStruct((2, count, bins), j...  3.41 us
    pallas_call x1, Pallas kernels, regroup_call(): pl.pallas_call(functools.partial(regroup_kernel, levels, plane), out_shap...  1.1 us
  transfers between devices with their start and end apart: 11, of which 4 were waited for; matrix products, arithmetic and copies ran while one was open for 0% of the time, Pallas kernels for 21%

profile of v3, /device:TPU:0, one launch (start us, length us, event | category | flops | bytes accessed | tf_op | source)
XLA Modules:
  0.0 42.7 jit_solution(12800870736812030022)
XLA Ops:
  0.0 5.9 %range_0.1 = (f32[4,2,8,512]{3,2,1,0:T(8,128)}, f32[4,2,8,512]{3,2,1,0:T(8,128)}, f32[4,2,8,512]{3,2,1,0:T(8,128)}, f32[4,2,8,512]{3,2,1,0:T(8,128)}) custom-call(s32[8]{0:T(128)} %shift_ref.2, f32[2,1024]{1,0:T(2,128)} %taps_hbm.3, f32[8,8]{1,0:T(8,128)} %weights_hbm.3, f32[2,8,16384]{2,1,0:T(8,128)} %echoes_hbm.3), custom_call_target="tpu_custom_call" | custom-call | flops 2013265920 | bytes 1572864 | tf_op jit(solution)/shard_map/range_0/pallas_call | solution.py:170
  5.9 3.1 %collective-permute-start = (f32[4,2,8,512]{3,2,1,0:T(8,128)}, f32[4,2,8,512]{3,2,1,0:T(8,128)S(1)}, u32[]{:S(2)}, u32[]{:S(2)}) collective-permute-start(f32[4,2,8,512]{3,2,1,0:T(8,128)} %get-tuple-element.32), channel_id=1, source_target_pairs={{0,2},{1,3},{2,0},{3,1},{4,6},{5,7},{6,4},{7,5},{8,10},{9,11},{10,... | collective-permute-start | bytes 393224 | tf_op jit(solution)/shard_map/ppermute | solution.py:324
  9.0 2.6 %collective-permute-start.1 = (f32[4,2,8,512]{3,2,1,0:T(8,128)}, f32[4,2,8,512]{3,2,1,0:T(8,128)S(1)}, u32[]{:S(2)}, u32[]{:S(2)}) collective-permute-start(f32[4,2,8,512]{3,2,1,0:T(8,128)} %get-tuple-element.33), channel_id=1, source_target_pairs={{0,4},{1,5},{2,6},{3,7},{4,0},{5,1},{6,2},{7,3},{8,12},{9,13},{10,... | collective-permute-start | bytes 393224 | tf_op jit(solution)/shard_map/ppermute | solution.py:324
  11.6 0.0 collective-permute-start.2
  11.6 5.9 %range_1.1 = f32[32,8,512]{2,1,0:T(8,128)} custom-call(s32[8]{0:T(128)} %shift_ref.2, f32[2,1024]{1,0:T(2,128)} %taps_hbm.3, f32[8,8]{1,0:T(8,128)} %weights_hbm.3, f32[2,8,16384]{2,1,0:T(8,128)} %echoes_hbm.3), custom_call_target="tpu_custom_call" | custom-call | flops 2013265920 | bytes 1572864 | tf_op jit(solution)/shard_map/range_1/pallas_call | solution.py:170
  17.5 0.0 copy-start
  17.5 6.1 %all-to-all-start = ((f32[32,8,512]{2,1,0:T(8,128)}), f32[32,8,512]{2,1,0:T(8,128)S(1)}, u32[]{:S(2)}, u32[]{:S(2)}) async-start(f32[32,8,512]{2,1,0:T(8,128)} %range_1.1), calls=%async_computation | async-start | bytes 1048576 | tf_op jit(solution)/shard_map/all_to_all | solution.py:327
  23.6 0.0 collective-permute-done.refs_1_
  23.6 0.0 collective-permute-done.1.refs_2_
  23.6 0.0 collective-permute-done.2.refs_3_
  23.6 0.0 copy-done
  23.6 1.1 %regroup.1 = (f32[4,8,512]{2,1,0:T(8,128)S(1)}, f32[4,8,512]{2,1,0:T(8,128)S(1)}, f32[4,8,512]{2,1,0:T(8,128)S(1)}, f32[4,8,512]{2,1,0:T(8,128)S(1)}, f32[4,8,51...) custom-call(f32[4,2,8,512]{3,2,1,0:T(8,128)S(1)} %copy-done, ...), custom_call_target="tpu_custom_call" | custom-call | bytes 1048576 | tf_op jit(solution)/shard_map/regroup/pallas_call | solution.py:201
  24.8 1.8 %collective-permute-start.3 = (f32[4,8,512]{2,1,0:T(8,128)S(1)}, f32[4,8,512]{2,1,0:T(8,128)S(1)}, u32[]{:S(2)}, u32[]{:S(2)}) collective-permute-start(f32[4,8,512]{2,1,0:T(8,128)S(1)} %get-tuple-element.40), channel_id=1, source_target_pairs={{0,1},{1,0},{2,3},{3,2},{4,5},{5,4},{6,7},{7,6},{8,9},{9,8},{10,11... | collective-permute-start | bytes 196616 | tf_op jit(solution)/shard_map/ppermute | solution.py:331
  26.6 0.0 collective-permute-start.4
  26.6 0.4 collective-permute-start.5
  27.0 0.0 copy-start.1
  27.0 1.8 %collective-permute-start.6 = (f32[4,8,512]{2,1,0:T(8,128)S(1)}, f32[4,8,512]{2,1,0:T(8,128)S(1)}, u32[]{:S(2)}, u32[]{:S(2)}) collective-permute-start(f32[4,8,512]{2,1,0:T(8,128)S(1)} %get-tuple-element.43), channel_id=1, source_target_pairs={{0,16},{1,17},{2,18},{3,19},{4,20},{5,21},{6,22},{7,23},{8,24},{9,... | collective-permute-start | bytes 196616 | tf_op jit(solution)/shard_map/ppermute | solution.py:331
  28.7 1.5 %collective-permute-start.7 = (f32[4,8,512]{2,1,0:T(8,128)S(1)}, f32[4,8,512]{2,1,0:T(8,128)S(1)}, u32[]{:S(2)}, u32[]{:S(2)}) collective-permute-start(f32[4,8,512]{2,1,0:T(8,128)S(1)} %get-tuple-element.44), channel_id=1, source_target_pairs={{0,17},{1,16},{2,19},{3,18},{4,21},{5,20},{6,23},{7,22},{8,25},{9,... | collective-permute-start | bytes 196616 | tf_op jit(solution)/shard_map/ppermute | solution.py:331
  30.2 2.7 %collective-permute-done.3.refs_2_ = f32[4,8,512]{2,1,0:T(8,128)S(1)} collective-permute-done((f32[4,8,512]{2,1,0:T(8,128)S(1)}, f32[4,8,512]{2,1,0:T(8,128)S(1)}, u32[]{:S(2)}, u32[]{:S(2)}) %collective-permute-start.3) | collective-permute-done | bytes 65568 | tf_op jit(solution)/shard_map/ppermute | solution.py:331
  32.9 0.0 collective-permute-start.8
  32.9 0.0 collective-permute-done.4.refs_3_
  32.9 2.8 %collective-permute-start.9 = (f32[4,8,512]{2,1,0:T(8,128)S(1)}, f32[4,8,512]{2,1,0:T(8,128)S(1)}, u32[]{:S(2)}, u32[]{:S(2)}) collective-permute-start(f32[4,8,512]{2,1,0:T(8,128)S(1)} %get-tuple-element.46), channel_id=1, source_target_pairs={{0,25},{1,24},{2,27},{3,26},{4,29},{5,28},{6,31},{7,30},{8,17},{9,... | collective-permute-start | bytes 196616 | tf_op jit(solution)/shard_map/ppermute | solution.py:331
  35.8 0.2 collective-permute-done.5.refs_4_
  36.0 0.0 collective-permute-done.6.refs_5_
  36.0 0.0 collective-permute-done.7.refs_6_
  36.0 1.6 %collective-permute-done.8.refs_7_ = f32[4,8,512]{2,1,0:T(8,128)S(1)} collective-permute-done((f32[4,8,512]{2,1,0:T(8,128)S(1)}, f32[4,8,512]{2,1,0:T(8,128)S(1)}, u32[]{:S(2)}, u32[]{:S(2)}) %collective-permute-start.8) | collective-permute-done | bytes 65568 | tf_op jit(solution)/shard_map/ppermute | solution.py:331
  37.5 1.7 %collective-permute-done.9.refs_8_ = f32[4,8,512]{2,1,0:T(8,128)S(1)} collective-permute-done((f32[4,8,512]{2,1,0:T(8,128)S(1)}, f32[4,8,512]{2,1,0:T(8,128)S(1)}, u32[]{:S(2)}, u32[]{:S(2)}) %collective-permute-start.9) | collective-permute-done | bytes 65568 | tf_op jit(solution)/shard_map/ppermute | solution.py:331
  39.3 0.0 copy-done.1
  39.3 1.8 %azimuth_first.1.earlier_ref = f32[2,256,512]{2,1,0:T(8,128)S(1)} custom-call(f32[2,512]{1,0:T(2,128)S(1)} %copy-done.1, f32[4,8,512]{2,1,0:T(8,128)S(1)} %get-tuple-element.39.refs_1_, f32[4,8,512]{2,1,0:T(8,128)S(1)} %collective-permute-done.3.refs_2_, f32[4,8,512]{2,1,0:T(8,128)S(1)} %collective-permute-done.4.refs_3_, ...), custom_call_target="tpu_custom_call" | custom-call | flops 8053063680 | bytes 1572864 | tf_op jit(solution)/shard_map/azimuth_first/pallas_call | solution.py:290
  41.1 0.0 all-to-all-done
  41.1 1.6 %azimuth_second.1 = f32[2,256,512]{2,1,0:T(8,128)} custom-call(f32[2,512]{1,0:T(2,128)S(1)} %copy-done.1, f32[256,512]{1,0:T(8,128)S(1)} %bitcast.1, f32[2,256,512]{2,1,0:T(8,128)S(1)} %azimuth_first.1.earlier_ref), custom_call_target="tpu_custom_call" | custom-call | flops 8053063680 | bytes 1572864 | tf_op jit(solution)/shard_map/azimuth_second/pallas_call | solution.py:290
Async XLA Ops:
  5.9 17.7 %collective-permute-start = (f32[4,2,8,512]{3,2,1,0:T(8,128)}, f32[4,2,8,512]{3,2,1,0:T(8,128)S(1)}, u32[]{:S(2)}, u32[]{:S(2)}) collective-permute-start(f32[4,2,8,512]{3,2,1,0:T(8,128)} %get-tuple-element.32), channel_id=1, source_target_pairs={{0,2},{1,3},{2,0},{3,1},{4,6},{5,7},{6,4},{7,5},{8,10},{9,11},{10,... | collective-permute-start | bytes 393224 | tf_op jit(solution)/shard_map/ppermute | solution.py:324
  9.0 14.6 %collective-permute-start.1 = (f32[4,2,8,512]{3,2,1,0:T(8,128)}, f32[4,2,8,512]{3,2,1,0:T(8,128)S(1)}, u32[]{:S(2)}, u32[]{:S(2)}) collective-permute-start(f32[4,2,8,512]{3,2,1,0:T(8,128)} %get-tuple-element.33), channel_id=1, source_target_pairs={{0,4},{1,5},{2,6},{3,7},{4,0},{5,1},{6,2},{7,3},{8,12},{9,13},{10,... | collective-permute-start | bytes 393224 | tf_op jit(solution)/shard_map/ppermute | solution.py:324
  11.6 12.0 %collective-permute-start.2 = (f32[4,2,8,512]{3,2,1,0:T(8,128)}, f32[4,2,8,512]{3,2,1,0:T(8,128)S(1)}, u32[]{:S(2)}, u32[]{:S(2)}) collective-permute-start(f32[4,2,8,512]{3,2,1,0:T(8,128)} %get-tuple-element.34), channel_id=1, source_target_pairs={{0,6},{1,7},{2,4},{3,5},{4,2},{5,3},{6,0},{7,1},{8,14},{9,15},{10,... | collective-permute-start | bytes 393224 | tf_op jit(solution)/shard_map/ppermute | solution.py:324
  17.5 6.1 %copy-start = (f32[4,2,8,512]{3,2,1,0:T(8,128)S(1)}, f32[4,2,8,512]{3,2,1,0:T(8,128)}, u32[]{:S(2)}) copy-start(f32[4,2,8,512]{3,2,1,0:T(8,128)} %get-tuple-element.35.refs_0_) | copy-start | bytes 393220
  17.5 23.5 %all-to-all-start = ((f32[32,8,512]{2,1,0:T(8,128)}), f32[32,8,512]{2,1,0:T(8,128)S(1)}, u32[]{:S(2)}, u32[]{:S(2)}) async-start(f32[32,8,512]{2,1,0:T(8,128)} %range_1.1), calls=%async_computation | async-start | bytes 1048576 | tf_op jit(solution)/shard_map/all_to_all | solution.py:327
  24.8 8.2 %collective-permute-start.3 = (f32[4,8,512]{2,1,0:T(8,128)S(1)}, f32[4,8,512]{2,1,0:T(8,128)S(1)}, u32[]{:S(2)}, u32[]{:S(2)}) collective-permute-start(f32[4,8,512]{2,1,0:T(8,128)S(1)} %get-tuple-element.40), channel_id=1, source_target_pairs={{0,1},{1,0},{2,3},{3,2},{4,5},{5,4},{6,7},{7,6},{8,9},{9,8},{10,11... | collective-permute-start | bytes 196616 | tf_op jit(solution)/shard_map/ppermute | solution.py:331
  26.6 6.3 %collective-permute-start.4 = (f32[4,8,512]{2,1,0:T(8,128)S(1)}, f32[4,8,512]{2,1,0:T(8,128)S(1)}, u32[]{:S(2)}, u32[]{:S(2)}) collective-permute-start(f32[4,8,512]{2,1,0:T(8,128)S(1)} %get-tuple-element.41), channel_id=1, source_target_pairs={{0,8},{1,9},{2,10},{3,11},{4,12},{5,13},{6,14},{7,15},{8,0},{9,1},... | collective-permute-start | bytes 196616 | tf_op jit(solution)/shard_map/ppermute | solution.py:331
  26.6 9.4 %collective-permute-start.5 = (f32[4,8,512]{2,1,0:T(8,128)S(1)}, f32[4,8,512]{2,1,0:T(8,128)S(1)}, u32[]{:S(2)}, u32[]{:S(2)}) collective-permute-start(f32[4,8,512]{2,1,0:T(8,128)S(1)} %get-tuple-element.42), channel_id=1, source_target_pairs={{0,9},{1,8},{2,11},{3,10},{4,13},{5,12},{6,15},{7,14},{8,1},{9,0},... | collective-permute-start | bytes 196616 | tf_op jit(solution)/shard_map/ppermute | solution.py:331
  27.0 12.3 %copy-start.1 = (f32[2,512]{1,0:T(2,128)S(1)}, f32[2,512]{1,0:T(2,128)}, u32[]{:S(2)}) copy-start(f32[2,512]{1,0:T(2,128)} %taps_ref.1) | copy-start | bytes 12292
  27.0 9.0 %collective-permute-start.6 = (f32[4,8,512]{2,1,0:T(8,128)S(1)}, f32[4,8,512]{2,1,0:T(8,128)S(1)}, u32[]{:S(2)}, u32[]{:S(2)}) collective-permute-start(f32[4,8,512]{2,1,0:T(8,128)S(1)} %get-tuple-element.43), channel_id=1, source_target_pairs={{0,16},{1,17},{2,18},{3,19},{4,20},{5,21},{6,22},{7,23},{8,24},{9,... | collective-permute-start | bytes 196616 | tf_op jit(solution)/shard_map/ppermute | solution.py:331
  28.7 7.2 %collective-permute-start.7 = (f32[4,8,512]{2,1,0:T(8,128)S(1)}, f32[4,8,512]{2,1,0:T(8,128)S(1)}, u32[]{:S(2)}, u32[]{:S(2)}) collective-permute-start(f32[4,8,512]{2,1,0:T(8,128)S(1)} %get-tuple-element.44), channel_id=1, source_target_pairs={{0,17},{1,16},{2,19},{3,18},{4,21},{5,20},{6,23},{7,22},{8,25},{9,... | collective-permute-start | bytes 196616 | tf_op jit(solution)/shard_map/ppermute | solution.py:331
  32.9 4.6 %collective-permute-start.8 = (f32[4,8,512]{2,1,0:T(8,128)S(1)}, f32[4,8,512]{2,1,0:T(8,128)S(1)}, u32[]{:S(2)}, u32[]{:S(2)}) collective-permute-start(f32[4,8,512]{2,1,0:T(8,128)S(1)} %get-tuple-element.45), channel_id=1, source_target_pairs={{0,24},{1,25},{2,26},{3,27},{4,28},{5,29},{6,30},{7,31},{8,16},{9,... | collective-permute-start | bytes 196616 | tf_op jit(solution)/shard_map/ppermute | solution.py:331
  32.9 6.3 %collective-permute-start.9 = (f32[4,8,512]{2,1,0:T(8,128)S(1)}, f32[4,8,512]{2,1,0:T(8,128)S(1)}, u32[]{:S(2)}, u32[]{:S(2)}) collective-permute-start(f32[4,8,512]{2,1,0:T(8,128)S(1)} %get-tuple-element.46), channel_id=1, source_target_pairs={{0,25},{1,24},{2,27},{3,26},{4,29},{5,28},{6,31},{7,30},{8,17},{9,... | collective-permute-start | bytes 196616 | tf_op jit(solution)/shard_map/ppermute | solution.py:331

commit v4 on v3

v4 whole, which is shorter than its diff:
```python
import functools

import jax
import jax.numpy as jnp
from jax import lax
from jax.experimental import pallas as pl
from jax.experimental.pallas import tpu as pltpu
from jax.sharding import PartitionSpec as P

TAPS = 8
BLOCK = 256
LANE = 128
AXES = ("gx", "gy")
CORES = 2
LEVELS = 4
AHEAD = 10

ROWS_BY_ROWS = (((1,), (1,)), ((), ()))
PLAIN = (((1,), (0,)), ((), ()))


def split(values):
    high = values.astype(jnp.bfloat16)
    return high, (values - high.astype(jnp.float32)).astype(jnp.bfloat16)


def toeplitz(row, rows, width):
    row = jnp.concatenate([row, jnp.zeros((1, width - row.shape[1]), jnp.float32)], axis=1)
    return pltpu.roll(jnp.broadcast_to(row, (rows, width)), 0, axis=1, stride=1, stride_axis=0)


def range_kernel(own, planes, lines, blocks, sections, shift_ref, taps_hbm, weights_hbm, echoes_hbm, *refs):
    if own:
        *outs, taps_ref, weights_ref, echoes_ref, even, odd, table, compressed, sems, ready, out_sems = refs
    else:
        ready, taps_ref, weights_ref, echoes_ref, even, odd, table, compressed, sems = refs
    segments, levels, inner = planes
    core = lax.rem(lax.axis_index("gx"), CORES)
    width = blocks // (CORES * segments)
    halo = (sections - 1) // 2 + 1
    span = width + 2 * halo

    def lanes(block, count):
        return pl.ds(pl.multiple_of(block * BLOCK, BLOCK), count * BLOCK)

    copies = [
        pltpu.make_async_copy(taps_hbm, taps_ref, sems.at[0]),
        pltpu.make_async_copy(weights_hbm, weights_ref, sems.at[1]),
    ]
    for segment in range(segments):
        first = (CORES * segment + core) * width
        moves = (
            (jnp.maximum(first - halo, 0), 0, halo),
            (first, halo, width),
            (jnp.minimum(first + width, blocks - halo), halo + width, halo),
        )
        for n, (source, to, count) in enumerate(moves):
            target = echoes_ref.at[segment, :, :, to * BLOCK : (to + count) * BLOCK]
            copies.append(
                pltpu.make_async_copy(
                    echoes_hbm.at[:, :, lanes(source, count)], target, sems.at[2 + 3 * segment + n]
                )
            )
    for copy in copies:
        copy.start()
    copies[0].wait()
    copies[1].wait()
    real = toeplitz(taps_ref[0:1, :], BLOCK, sections * BLOCK)
    imag = toeplitz(taps_ref[1:2, :], BLOCK, sections * BLOCK)
    for kind, values in enumerate((real, imag, real - imag)):
        table[kind, 0], table[kind, 1] = split(values)
    for copy in copies[2:]:
        copy.wait()
    at_start, at_end = core == 0, core == CORES - 1

    def piece(segment, part, block):
        values = echoes_ref[segment, part, :, block * BLOCK : (block + 1) * BLOCK]
        if segment == 0 and block < halo:
            values = jnp.where(at_start, 0.0, values)
        if segment == segments - 1 and block >= halo + width:
            values = jnp.where(at_end, 0.0, values)
        return values

    for segment in range(segments):
        for offset, ref in ((0, even), (1, odd)):
            for pair in range((span - offset) // 2):
                first = 2 * pair + offset
                parts = [
                    jnp.concatenate([piece(segment, part, first), piece(segment, part, first + 1)], axis=0)
                    for part in range(2)
                ]
                at = slice((segment * span + 2 * pair) * lines, (segment * span + 2 * pair + 2) * lines)
                for kind, values in enumerate((parts[0], parts[1], parts[0] + parts[1])):
                    ref[kind, 0, at, :], ref[kind, 1, at, :] = split(values)
    rows = (width + 2) * lines
    products = []
    for kind in range(3):
        sums = None
        for section in range(sections):
            ref = even if section % 2 == 0 else odd
            starts = [(segment * span + section - section % 2) * lines for segment in range(segments)]
            x_high, x_low = [
                jnp.concatenate([ref[kind, which, start : start + rows, :] for start in starts], axis=0)
                for which in range(2)
            ]
            at = slice(section * BLOCK, (section + 1) * BLOCK)
            t_high, t_low = table[kind, 0, :, at], table[kind, 1, :, at]
            for left, right in ((x_high, t_high), (x_low, t_high), (x_high, t_low)):
                term = lax.dot_general(left, right, ROWS_BY_ROWS, preferred_element_type=jnp.float32)
                sums = term if sums is None else sums + term
        products.append(sums)
    compressed[0] = products[0] + products[1]
    compressed[1] = products[2] - products[0] + products[1]
    for part in range(2):
        low, high = slice(0, lines), slice(segments * rows - lines, segments * rows)
        compressed[part, low, :] = jnp.where(at_start, 0.0, compressed[part, low, :])
        compressed[part, high, :] = jnp.where(at_end, 0.0, compressed[part, high, :])
    migrate(lines, segments, width, shift_ref, weights_ref, compressed, ready)
    if own:
        mine = lax.axis_index("gy") // inner
        sends = []
        for k, out in enumerate(outs):
            sends.append(pltpu.make_async_copy(ready.at[:, mine ^ k], out, out_sems.at[k]))
            sends[-1].start()
        for send in sends:
            send.wait()


def place_of(device, shape):
    at = []
    for extent in reversed(shape[:-2]):
        at.insert(0, device % extent)
        device //= extent
    return at


def migrate(lines, segments, width, shift_ref, weights_ref, compressed, out_ref):
    per = out_ref.shape[-1] // LANE
    lane = lax.broadcasted_iota(jnp.int32, (lines, LANE), 1)
    row = lax.broadcasted_iota(jnp.int32, (lines, LANE), 0)
    shift = jnp.zeros((lines, LANE), jnp.int32)
    for line in range(lines):
        shift = jnp.where(row == line, shift_ref[line], shift)
    places = [lane + shift - (TAPS // 2 - 1) + step for step in range(2)]
    index = [place & (LANE - 1) for place in places]
    before = [place < 0 for place in places]
    after = [place >= LANE for place in places]
    weight = [jnp.broadcast_to(weights_ref[:, j : j + 1], (lines, LANE)) for j in range(TAPS)]
    inside = lane < LANE - 2
    tiles = width * BLOCK // LANE
    first = BLOCK // LANE

    for segment in range(segments):
        for part in range(2):

            def turned(tile, step):
                block = segment * (width + 2) + (tile + first) * LANE // BLOCK
                at = ((tile + first) * LANE) % BLOCK
                values = compressed[part, block * lines : (block + 1) * lines, at : at + LANE]
                return jnp.take_along_axis(values, index[step], axis=1, mode="promise_in_bounds")

            later = [turned(tiles + 1, step) for step in range(2)]
            here = [turned(tiles, step) for step in range(2)]
            carried = [jnp.zeros((lines, LANE), jnp.float32)] * 3
            for tile in range(tiles, -1, -1):
                earlier = [turned(tile - 1, step) for step in range(2)]
                pair = [
                    jnp.where(before[step], earlier[step], jnp.where(after[step], later[step], here[step]))
                    for step in range(2)
                ]
                total = None
                for k in (3, 2, 1, 0):
                    term = weight[2 * k] * pair[0] + weight[2 * k + 1] * pair[1]
                    if total is None:
                        total = term
                    else:
                        rolled = pltpu.roll(total, LANE - 2, axis=1)
                        total = jnp.where(inside, rolled, carried[k]) + term
                        carried[k] = rolled
                if tile < tiles:
                    place = place_of(segment * (tiles // per) + tile // per, out_ref.shape)
                    at = (tile % per) * LANE
                    out_ref[(*place, slice(part * lines, (part + 1) * lines), slice(at, at + LANE))] = total
                later, here = here, earlier


def range_call(own, echoes, range_ref, shift_bins, weights, planes):
    lines, range_total = echoes.shape[1], echoes.shape[2]
    blocks = range_total // BLOCK
    sections = range_ref.shape[1] // BLOCK + 1
    segments, levels, inner = planes
    bins = range_total // (CORES * segments * levels * inner)
    width = blocks // (CORES * segments)
    span = width + sections + 1
    flops = 2 * 3 * 3 * segments * (width + 2) * lines * sections * BLOCK * BLOCK
    scratch = [
        pltpu.VMEM(range_ref.shape, jnp.float32),
        pltpu.VMEM(weights.shape, jnp.float32),
        pltpu.VMEM((segments, 2, lines, span * BLOCK), jnp.float32),
        pltpu.VMEM((3, 2, segments * span * lines, BLOCK), jnp.bfloat16),
        pltpu.VMEM((3, 2, segments * span * lines, BLOCK), jnp.bfloat16),
        pltpu.VMEM((3, 2, BLOCK, sections * BLOCK), jnp.bfloat16),
        pltpu.VMEM((2, segments * (width + 2) * lines, BLOCK), jnp.float32),
        pltpu.SemaphoreType.DMA((2 + 3 * segments,)),
    ]
    if own:
        out_shape = [jax.ShapeDtypeStruct((segments, inner, 2 * lines, bins), jnp.float32)] * levels
        out_specs = [pl.BlockSpec(memory_space=pltpu.HBM)] * levels
        scratch += [
            pltpu.VMEM((segments, levels, inner, 2 * lines, bins), jnp.float32),
            pltpu.SemaphoreType.DMA((levels,)),
        ]
    else:
        out_shape = jax.ShapeDtypeStruct((segments * levels * inner, 2 * lines, bins), jnp.float32)
        out_specs = pl.BlockSpec(memory_space=pltpu.VMEM)
    return pl.pallas_call(
        functools.partial(range_kernel, own, planes, lines, blocks, sections),
        out_shape=out_shape,
        in_specs=[pl.BlockSpec(memory_space=pltpu.SMEM)] + [pl.BlockSpec(memory_space=pltpu.HBM if own else pl.ANY)] * 3,
        out_specs=out_specs,
        scratch_shapes=scratch,
        compiler_params=pltpu.CompilerParams(vmem_limit_bytes=(60 if own else 40) << 20),
        cost_estimate=pl.CostEstimate(flops=flops, bytes_accessed=3 * echoes.size * 2, transcendentals=0),
        name="range_own" if own else "range_partner",
    )(shift_bins, range_ref, weights, echoes)


def regroup_kernel(levels, plane, *refs):
    sources, outs, sems = refs[:levels], refs[levels:-1], refs[-1]
    inner = sources[0].shape[1]
    mine = place_here(inner)
    copies = []
    for q in range(plane):
        place = mine ^ q
        for k in range(levels):
            source = sources[k].at[place // inner, lax.rem(place, inner)]
            copies.append(pltpu.make_async_copy(source, outs[q].at[k], sems.at[q, k]))
            copies[-1].start()
    for copy in copies:
        copy.wait()


def place_here(inner):
    return (lax.axis_index("gx") // CORES) * inner + lax.rem(lax.axis_index("gy"), inner)


def regroup_call(received):
    levels = len(received)
    segments, inner, rows, bins = received[0].shape
    plane = segments * inner
    return pl.pallas_call(
        functools.partial(regroup_kernel, levels, plane),
        out_shape=[jax.ShapeDtypeStruct((levels, rows, bins), jnp.float32)] * plane,
        in_specs=[pl.BlockSpec(memory_space=pl.ANY)] * levels,
        out_specs=[pl.BlockSpec(memory_space=pltpu.HBM)] * plane,
        scratch_shapes=[pltpu.SemaphoreType.DMA((plane, levels))],
        compiler_params=pltpu.CompilerParams(vmem_limit_bytes=8 << 20),
        cost_estimate=pl.CostEstimate(flops=0, bytes_accessed=8 * levels * plane * rows * bins, transcendentals=0),
        name="regroup",
    )(*received)


def azimuth_tables(taps_ref, table):
    length = taps_ref.shape[1]
    diagonals = table.shape[2]
    for part in range(2):
        row = jnp.concatenate(
            [jnp.zeros((1, BLOCK), jnp.float32), taps_ref[part : part + 1, :]], axis=1
        )
        full = toeplitz(row, BLOCK, length + 2 * BLOCK)
        for diagonal in range(diagonals):
            at = (diagonal + 1) * BLOCK
            table[part, 0, diagonal], table[part, 1, diagonal] = split(full[:, at : at + BLOCK])


def azimuth_sums(table, lines_ref):
    diagonals = table.shape[2]
    middle = diagonals // 2
    blocks = lines_ref.shape[1] // BLOCK
    pieces = [
        [split(lines_ref[part, b * BLOCK : (b + 1) * BLOCK, :]) for b in range(blocks)] for part in range(2)
    ]

    def product(b, taps, part):
        sums = None
        for diagonal in range(diagonals):
            other = b + diagonal - middle
            if not 0 <= other < blocks:
                continue
            m_high, m_low = pieces[part][other]
            t_high, t_low = table[taps, 0, diagonal], table[taps, 1, diagonal]
            for left, right in ((t_high, m_high), (t_high, m_low), (t_low, m_high)):
                term = lax.dot_general(left, right, PLAIN, preferred_element_type=jnp.float32)
                sums = term if sums is None else sums + term
        return sums

    for b in range(blocks):
        at = slice(b * BLOCK, (b + 1) * BLOCK)
        yield 0, at, product(b, 0, 0) + product(b, 1, 1)
        yield 1, at, product(b, 0, 1) - product(b, 1, 0)


def clear_other(lines_ref, segments, core):
    run = lines_ref.shape[1] // (CORES * segments)
    for segment in range(segments):
        rows = pl.ds(pl.multiple_of((CORES * segment + 1 - core) * run, run), run)
        for part in range(2):
            lines_ref[part, rows, :] = jnp.zeros((run, lines_ref.shape[2]), jnp.float32)


def azimuth_first(planes, *refs):
    segments, levels, inner = planes
    taps_ref, *sources, out_ref, table, lines_ref, sems = refs
    lines = sources[0].shape[1] // 2
    core = lax.rem(lax.axis_index("gx"), CORES)
    level = lax.axis_index("gy") // inner
    mine = place_here(inner)
    copies = []
    for q, source in enumerate(sources):
        place = mine ^ q
        for k in range(levels):
            device = (((place // inner) * CORES + core) * levels + (level ^ k)) * inner + lax.rem(place, inner)
            rows = pl.ds(pl.multiple_of(device * lines, lines), lines)
            for part in range(2):
                copies.append(
                    pltpu.make_async_copy(
                        source.at[k, part * lines : (part + 1) * lines], lines_ref.at[part, rows], sems.at[q, k, part]
                    )
                )
                copies[-1].start()
    clear_other(lines_ref, segments, core)
    for copy in copies:
        copy.wait()
    azimuth_tables(taps_ref, table)
    for part, at, sums in azimuth_sums(table, lines_ref):
        out_ref[part, at, :] = sums


def azimuth_second(planes, table, moved_ref, earlier_ref, out_ref, lines_ref):
    segments, levels, inner = planes
    lines = moved_ref.shape[1] // 2
    run = levels * inner * lines
    core = lax.rem(lax.axis_index("gx"), CORES)
    clear_other(lines_ref, segments, 1 - core)
    for segment in range(segments):
        rows = pl.ds(pl.multiple_of((CORES * segment + 1 - core) * run, run), run)
        for part in range(2):
            values = moved_ref[
                segment * levels * inner : (segment + 1) * levels * inner, part * lines : (part + 1) * lines, :
            ]
            lines_ref[part, rows, :] = values.reshape(run, values.shape[-1])
    for part, at, sums in azimuth_sums(table, lines_ref):
        out_ref[part, at, :] = earlier_ref[part, at, :] + sums


def azimuth_call(planes, count, bins, azimuth_ref, arrived=None, table=None, moved=None, earlier=None):
    segments, levels, inner = planes
    diagonals = azimuth_ref.shape[1] // BLOCK + 1
    image = jax.ShapeDtypeStruct((2, count, bins), jnp.float32)
    vmem = pl.BlockSpec(memory_space=pltpu.VMEM)
    scratch = [pltpu.VMEM((2, count, bins), jnp.float32)]
    if earlier is None:
        kernel = azimuth_first
        operands = [azimuth_ref, *arrived]
        in_specs = [vmem] + [pl.BlockSpec(memory_space=pl.ANY)] * len(arrived)
        out_shape = [image, jax.ShapeDtypeStruct((2, 2, diagonals, BLOCK, BLOCK), jnp.bfloat16)]
        out_specs = [vmem, vmem]
        scratch += [pltpu.SemaphoreType.DMA((segments * inner, levels, 2))]
        weight = AHEAD
    else:
        kernel = azimuth_second
        operands = [table, moved, earlier]
        in_specs = [vmem] * 3
        out_shape, out_specs = image, vmem
        weight = 1
    return pl.pallas_call(
        functools.partial(kernel, planes),
        out_shape=out_shape,
        in_specs=in_specs,
        out_specs=out_specs,
        scratch_shapes=scratch,
        compiler_params=pltpu.CompilerParams(vmem_limit_bytes=40 << 20),
        cost_estimate=pl.CostEstimate(
            flops=weight * 2 * 3 * 4 * count * BLOCK * bins, bytes_accessed=4 * 4 * count * bins, transcendentals=0
        ),
        name="azimuth_first" if earlier is None else "azimuth_second",
    )(*operands)


def pairs_of(planes, level_step=0, place_step=0, core_step=0):
    segments, levels, inner = planes
    pairs = []
    for device in range(CORES * segments * levels * inner):
        core = (device // (levels * inner)) % CORES
        place = (device // (CORES * levels * inner)) * inner + device % inner
        level = (device // inner) % levels
        place, level, core = place ^ place_step, level ^ level_step, core ^ core_step
        pairs.append((device, (((place // inner) * CORES + core) * levels + level) * inner + place % inner))
    return pairs


def per_device(echoes, range_ref, azimuth_ref, shift_bins, interp_weights):
    outer, run = lax.axis_size("gx"), lax.axis_size("gy")
    segments, levels = outer // CORES, LEVELS
    planes = (segments, levels, run // levels)
    devices_all = outer * run
    bins = echoes.shape[2] // devices_all
    partner = [
        lax.ppermute(array, AXES, pairs_of(planes, core_step=1)) for array in (echoes, shift_bins, interp_weights)
    ]
    by_level = range_call(True, echoes, range_ref, shift_bins, interp_weights, planes)
    received = [by_level[0]] + [
        lax.ppermute(by_level[k], AXES, pairs_of(planes, level_step=k)) for k in range(1, levels)
    ]
    *by_level, taps_later = lax.optimization_barrier((*by_level, range_ref))
    migrated = range_call(False, partner[0], taps_later, partner[1], partner[2], planes)
    groups = [
        [(segment * CORES + core) * run + at for segment in range(segments) for at in range(run)]
        for core in range(CORES)
    ]
    moved = lax.all_to_all(migrated, AXES, split_axis=0, concat_axis=0, axis_index_groups=groups, tiled=True)
    *received, migrated = lax.optimization_barrier((*received, migrated))
    by_place = regroup_call(received)
    arrived = [by_place[0]] + [
        lax.ppermute(by_place[q], AXES, pairs_of(planes, place_step=q)) for q in range(1, len(by_place))
    ]
    count = devices_all * echoes.shape[1]
    image, table = azimuth_call(planes, count, bins, azimuth_ref, arrived)
    return azimuth_call(planes, count, bins, azimuth_ref, table=table, moved=moved, earlier=image)


def solution(mesh):
    placed = (P(None, AXES, None), P(), P(), P(AXES), P(AXES, None))
    return jax.shard_map(
        per_device,
        mesh=mesh,
        in_specs=placed,
        out_specs=P(None, None, AXES),
        check_vma=False,
    )
```

time: 43.5 us -> 42.6 us (0.979); the launches traced: 42.7 us -> 42.3 us
  waiting for transfers between devices: 6.26 us -> 9.7 us
  starting transfers between devices: 20 us -> 16.9 us
  Pallas kernels: 16.3 us -> 15.6 us
    ppermute x10 -> x9, starting transfers between devices: 13.9 us -> 9.8 us  [the longest x3 5.28 us: per_device(): lax.ppermute(by_level[k], AXES, pairs_of(planes, level_step=k))]
    ppermute x10 -> x9, waiting for transfers between devices: 6.26 us -> 9.7 us  [the longest x3 9.69 us: per_device(): lax.ppermute(by_place[q], AXES, pairs_of(planes, place_step=q))]
    all_to_all x1, starting transfers between devices: 6.07 us -> 7.08 us  [per_device(): lax.all_to_all(migrated, AXES, split_axis=0, concat_axis=0, axis_index_gr...]
    pallas_call x4, Pallas kernels: 15.2 us -> 14.7 us  [the longest x2 10.4 us: range_call(): pl.pallas_call(functools.partial(range_kernel, own, planes, lines, blocks...]
  transfers between devices with their start and end apart: 11 -> 10, of which waited for: 4 -> 3; matrix products, arithmetic and copies ran while one was open for 0% -> 0% of each run, Pallas kernels for 21% -> 32%
where the time goes in v4:
time: 42.6 us; the launch traced here: 42.3 us
  starting transfers between devices  16.9 us (40%)
  Pallas kernels  15.6 us (37%)
  waiting for transfers between devices  9.7 us (23%)
    pallas_call x2, Pallas kernels, range_call(): pl.pallas_call(functools.partial(range_kernel, own, planes, lines, blocks...  10.4 us
    ppermute x3, waiting for transfers between devices, per_device(): lax.ppermute(by_place[q], AXES, pairs_of(planes, place_step=q))  9.69 us
    all_to_all x1, starting transfers between devices, per_device(): lax.all_to_all(migrated, AXES, split_axis=0, concat_axis=0, axis_index_gr...  7.08 us
    ppermute x3, starting transfers between devices, per_device(): lax.ppermute(by_level[k], AXES, pairs_of(planes, level_step=k))  5.28 us
    pallas_call x2, Pallas kernels, azimuth_call(): pl.pallas_call(functools.partial(kernel, planes), out_shape=out_shape, in...  4.31 us
    ppermute x3, starting transfers between devices, per_device(): lax.ppermute(by_place[q], AXES, pairs_of(planes, place_step=q))  3.55 us
    ppermute x3, starting transfers between devices, per_device(): lax.ppermute(array, AXES, pairs_of(planes, core_step=1))  0.96 us
    pallas_call x1, Pallas kernels, regroup_call(): pl.pallas_call(functools.partial(regroup_kernel, levels, plane), out_shap...  0.9 us
  transfers between devices with their start and end apart: 10, of which 3 were waited for; matrix products, arithmetic and copies ran while one was open for 0% of the time, Pallas kernels for 32%

profile of v4, /device:TPU:0, one launch (start us, length us, event | category | flops | bytes accessed | tf_op | source)
XLA Modules:
  0.0 42.3 jit_solution(13200252854180243325)
XLA Ops:
  0.0 0.0 copy-start.1
  0.0 0.5 %collective-permute-start.5 = (f32[2,8,16384]{2,1,0:T(8,128)}, f32[2,8,16384]{2,1,0:T(8,128)S(1)}, u32[]{:S(2)}, u32[]{:S(2)}) collective-permute-start(f32[2,8,16384]{2,1,0:T(8,128)} %echoes_hbm.1), channel_id=1, source_target_pairs={{0,8},{1,9},{2,10},{3,11},{4,12},{5,13},{6,14},{7,15},{8,0},{9,1},... | collective-permute-start | bytes 3145736 | tf_op jit(solution)/shard_map/ppermute | solution.py:409
  0.5 0.1 collective-permute-start.3
  0.5 0.4 %collective-permute-start.4 = (f32[8,8]{1,0:T(8,128)}, f32[8,8]{1,0:T(8,128)S(1)}, u32[]{:S(2)}, u32[]{:S(2)}) collective-permute-start(f32[8,8]{1,0:T(8,128)} %weights_hbm.1), channel_id=1, source_target_pairs={{0,8},{1,9},{2,10},{3,11},{4,12},{5,13},{6,14},{7,15},{8,0},{9,1},... | collective-permute-start | bytes 776 | tf_op jit(solution)/shard_map/ppermute | solution.py:409
  1.0 5.6 %range_own.1 = (f32[2,2,16,512]{3,2,1,0:T(8,128)}, f32[2,2,16,512]{3,2,1,0:T(8,128)}, f32[2,2,16,512]{3,2,1,0:T(8,128)}, f32[2,2,16,512]{3,2,1,0:T(8,128)}) custom-call(s32[8]{0:T(128)} %shift_ref.1, f32[2,1024]{1,0:T(2,128)} %taps_hbm.2, f32[8,8]{1,0:T(8,128)} %weights_hbm.1, f32[2,8,16384]{2,1,0:T(8,128)} %echoes_hbm.1), custom_call_target="tpu_custom_call" | custom-call | flops 1698693120 | bytes 1572864 | tf_op jit(solution)/shard_map/range_own/pallas_call | solution.py:216
  6.5 2.7 %collective-permute-start = (f32[2,2,16,512]{3,2,1,0:T(8,128)}, f32[2,2,16,512]{3,2,1,0:T(8,128)S(1)}, u32[]{:S(2)}, u32[]{:S(2)}) collective-permute-start(f32[2,2,16,512]{3,2,1,0:T(8,128)} %get-tuple-element.21), channel_id=1, source_target_pairs={{0,2},{1,3},{2,0},{3,1},{4,6},{5,7},{6,4},{7,5},{8,10},{9,11},{10,... | collective-permute-start | bytes 393224 | tf_op jit(solution)/shard_map/ppermute | solution.py:413
  9.2 2.6 %collective-permute-start.1 = (f32[2,2,16,512]{3,2,1,0:T(8,128)}, f32[2,2,16,512]{3,2,1,0:T(8,128)S(1)}, u32[]{:S(2)}, u32[]{:S(2)}) collective-permute-start(f32[2,2,16,512]{3,2,1,0:T(8,128)} %get-tuple-element.22), channel_id=1, source_target_pairs={{0,4},{1,5},{2,6},{3,7},{4,0},{5,1},{6,2},{7,3},{8,12},{9,13},{10,... | collective-permute-start | bytes 393224 | tf_op jit(solution)/shard_map/ppermute | solution.py:413
  11.8 0.0 copy-start
  11.8 0.0 collective-permute-done.3.shift_ref
  11.8 0.0 collective-permute-start.2
  11.8 0.0 collective-permute-done.4.weights_hbm
  11.8 0.0 collective-permute-done.5.echoes_hbm
  11.8 0.0 copy-done.1
  11.9 4.8 %range_partner.1 = f32[16,16,512]{2,1,0:T(8,128)} custom-call(s32[8]{0:T(128)S(1)} %collective-permute-done.3.shift_ref, f32[2,1024]{1,0:T(2,128)S(1)} %copy-done.1, f32[8,8]{1,0:T(8,128)S(1)} %collective-permute-done.4.weights_hbm, f32[2,8,16384]{2,1,0:T(8,128)S(1)} %collective-permute-done.5.echoes_hbm), custom_call_target="tpu_custom_call" | custom-call | flops 1698693120 | bytes 1572864 | tf_op jit(solution)/shard_map/range_partner/pallas_call | solution.py:216
  16.7 0.0 copy-start.2
  16.7 7.1 %all-to-all-start = ((f32[16,16,512]{2,1,0:T(8,128)}), f32[16,16,512]{2,1,0:T(8,128)S(1)}, u32[]{:S(2)}, u32[]{:S(2)}) async-start(f32[16,16,512]{2,1,0:T(8,128)} %range_partner.1), calls=%async_computation | async-start | bytes 1048576 | tf_op jit(solution)/shard_map/all_to_all | solution.py:421
  23.8 0.0 collective-permute-done.refs_1_
  23.8 0.0 collective-permute-done.1.refs_2_
  23.8 0.0 collective-permute-done.2.refs_3_
  23.8 0.0 copy-done
  23.9 0.9 %regroup.1 = (f32[4,16,512]{2,1,0:T(8,128)S(1)}, f32[4,16,512]{2,1,0:T(8,128)S(1)}, f32[4,16,512]{2,1,0:T(8,128)S(1)}, f32[4,16,512]{2,1,0:T(8,128)S(1)}) custom-call(f32[2,2,16,512]{3,2,1,0:T(8,128)S(1)} %copy-done, f32[2,2,16,512]{3,2,1,0:T(8,128)S(1)} %collective-permute-done.refs_1_, f32[2,2,16,512]{3,2,1,0:T(8,128)S(1)} %collective-permute-done.1.refs_2_, ...), custom_call_target="tpu_custom_call" | custom-call | bytes 1048576 | tf_op jit(solution)/shard_map/regroup/pallas_call | solution.py:251
  24.8 2.0 %collective-permute-start.6 = (f32[4,16,512]{2,1,0:T(8,128)S(1)}, f32[4,16,512]{2,1,0:T(8,128)S(1)}, u32[]{:S(2)}, u32[]{:S(2)}) collective-permute-start(f32[4,16,512]{2,1,0:T(8,128)S(1)} %get-tuple-element.30), channel_id=1, source_target_pairs={{0,1},{1,0},{2,3},{3,2},{4,5},{5,4},{6,7},{7,6},{8,9},{9,8},{10,11... | collective-permute-start | bytes 393224 | tf_op jit(solution)/shard_map/ppermute | solution.py:425
  26.7 1.5 %collective-permute-start.7 = (f32[4,16,512]{2,1,0:T(8,128)S(1)}, f32[4,16,512]{2,1,0:T(8,128)S(1)}, u32[]{:S(2)}, u32[]{:S(2)}) collective-permute-start(f32[4,16,512]{2,1,0:T(8,128)S(1)} %get-tuple-element.31), channel_id=1, source_target_pairs={{0,16},{1,17},{2,18},{3,19},{4,20},{5,21},{6,22},{7,23},{8,24},{9,... | collective-permute-start | bytes 393224 | tf_op jit(solution)/shard_map/ppermute | solution.py:425
  28.2 0.1 collective-permute-start.8
  28.3 4.5 %collective-permute-done.6.refs_2_ = f32[4,16,512]{2,1,0:T(8,128)S(1)} collective-permute-done((f32[4,16,512]{2,1,0:T(8,128)S(1)}, f32[4,16,512]{2,1,0:T(8,128)S(1)}, u32[]{:S(2)}, u32[]{:S(2)}) %collective-permute-start.6) | collective-permute-done | bytes 131104 | tf_op jit(solution)/shard_map/ppermute | solution.py:425
  32.8 1.9 %collective-permute-done.7.refs_3_ = f32[4,16,512]{2,1,0:T(8,128)S(1)} collective-permute-done((f32[4,16,512]{2,1,0:T(8,128)S(1)}, f32[4,16,512]{2,1,0:T(8,128)S(1)}, u32[]{:S(2)}, u32[]{:S(2)}) %collective-permute-start.7) | collective-permute-done | bytes 131104 | tf_op jit(solution)/shard_map/ppermute | solution.py:425
  34.7 3.3 %collective-permute-done.8.refs_4_ = f32[4,16,512]{2,1,0:T(8,128)S(1)} collective-permute-done((f32[4,16,512]{2,1,0:T(8,128)S(1)}, f32[4,16,512]{2,1,0:T(8,128)S(1)}, u32[]{:S(2)}, u32[]{:S(2)}) %collective-permute-start.8) | collective-permute-done | bytes 131104 | tf_op jit(solution)/shard_map/ppermute | solution.py:425
  38.0 0.0 copy-done.2
  38.0 2.2 %azimuth_first.1 = (f32[2,256,512]{2,1,0:T(8,128)S(1)}, bf16[2,2,3,256,256]{4,3,2,1,0:T(8,128)(2,1)S(1)}) custom-call(f32[2,512]{1,0:T(2,128)S(1)} %copy-done.2, f32[4,16,512]{2,1,0:T(8,128)S(1)} %get-tuple-element.29.refs_1_, f32[4,16,512]{2,1,0:T(8,128)S(1)} %collective-permute-done.6.refs_2_, f32[4,16,512]{2,1,0:T(8,128)S(1)} %collective-permute-done.7.refs_3_, ...), custom_call_target="tpu_custom_call" | custom-call | flops 8053063680 | bytes 2097152 | tf_op jit(solution)/shard_map/azimuth_first/pallas_call | solution.py:376
  40.2 0.0 all-to-all-done.moved_ref
  40.3 2.1 %azimuth_second.1 = f32[2,256,512]{2,1,0:T(8,128)} custom-call(bf16[2,2,3,256,256]{4,3,2,1,0:T(8,128)(2,1)S(1)} %get-tuple-element.33.table, f32[16,16,512]{2,1,0:T(8,128)S(1)} %all-to-all-done.moved_ref, f32[2,256,512]{2,1,0:T(8,128)S(1)} %get-tuple-element.34.earlier_ref), custom_call_target="tpu_custom_call" | custom-call | flops 805306368 | bytes 2097152 | tf_op jit(solution)/shard_map/azimuth_second/pallas_call | solution.py:376
Async XLA Ops:
  0.0 11.8 %copy-start.1 = (f32[2,1024]{1,0:T(2,128)S(1)}, f32[2,1024]{1,0:T(2,128)}, u32[]{:S(2)}) copy-start(f32[2,1024]{1,0:T(2,128)} %taps_hbm.2) | copy-start | bytes 24580
  0.0 11.8 %collective-permute-start.5 = (f32[2,8,16384]{2,1,0:T(8,128)}, f32[2,8,16384]{2,1,0:T(8,128)S(1)}, u32[]{:S(2)}, u32[]{:S(2)}) collective-permute-start(f32[2,8,16384]{2,1,0:T(8,128)} %echoes_hbm.1), channel_id=1, source_target_pairs={{0,8},{1,9},{2,10},{3,11},{4,12},{5,13},{6,14},{7,15},{8,0},{9,1},... | collective-permute-start | bytes 3145736 | tf_op jit(solution)/shard_map/ppermute | solution.py:409
  0.5 11.4 %collective-permute-start.3 = (s32[8]{0:T(128)}, s32[8]{0:T(128)S(1)}, u32[]{:S(2)}, u32[]{:S(2)}) collective-permute-start(s32[8]{0:T(128)} %shift_ref.1), channel_id=1, source_target_pairs={{0,8},{1,9},{2,10},{3,11},{4,12},{5,13},{6,14},{7,15},{8,0},{9,1},... | collective-permute-start | bytes 104 | tf_op jit(solution)/shard_map/ppermute | solution.py:409
  0.5 11.3 %collective-permute-start.4 = (f32[8,8]{1,0:T(8,128)}, f32[8,8]{1,0:T(8,128)S(1)}, u32[]{:S(2)}, u32[]{:S(2)}) collective-permute-start(f32[8,8]{1,0:T(8,128)} %weights_hbm.1), channel_id=1, source_target_pairs={{0,8},{1,9},{2,10},{3,11},{4,12},{5,13},{6,14},{7,15},{8,0},{9,1},... | collective-permute-start | bytes 776 | tf_op jit(solution)/shard_map/ppermute | solution.py:409
  6.5 17.3 %collective-permute-start = (f32[2,2,16,512]{3,2,1,0:T(8,128)}, f32[2,2,16,512]{3,2,1,0:T(8,128)S(1)}, u32[]{:S(2)}, u32[]{:S(2)}) collective-permute-start(f32[2,2,16,512]{3,2,1,0:T(8,128)} %get-tuple-element.21), channel_id=1, source_target_pairs={{0,2},{1,3},{2,0},{3,1},{4,6},{5,7},{6,4},{7,5},{8,10},{9,11},{10,... | collective-permute-start | bytes 393224 | tf_op jit(solution)/shard_map/ppermute | solution.py:413
  9.2 14.6 %collective-permute-start.1 = (f32[2,2,16,512]{3,2,1,0:T(8,128)}, f32[2,2,16,512]{3,2,1,0:T(8,128)S(1)}, u32[]{:S(2)}, u32[]{:S(2)}) collective-permute-start(f32[2,2,16,512]{3,2,1,0:T(8,128)} %get-tuple-element.22), channel_id=1, source_target_pairs={{0,4},{1,5},{2,6},{3,7},{4,0},{5,1},{6,2},{7,3},{8,12},{9,13},{10,... | collective-permute-start | bytes 393224 | tf_op jit(solution)/shard_map/ppermute | solution.py:413
  11.8 12.0 %copy-start = (f32[2,2,16,512]{3,2,1,0:T(8,128)S(1)}, f32[2,2,16,512]{3,2,1,0:T(8,128)}, u32[]{:S(2)}) copy-start(f32[2,2,16,512]{3,2,1,0:T(8,128)} %get-tuple-element.25.refs_0_) | copy-start | bytes 393220
  11.8 12.0 %collective-permute-start.2 = (f32[2,2,16,512]{3,2,1,0:T(8,128)}, f32[2,2,16,512]{3,2,1,0:T(8,128)S(1)}, u32[]{:S(2)}, u32[]{:S(2)}) collective-permute-start(f32[2,2,16,512]{3,2,1,0:T(8,128)} %get-tuple-element.23), channel_id=1, source_target_pairs={{0,6},{1,7},{2,4},{3,5},{4,2},{5,3},{6,0},{7,1},{8,14},{9,15},{10,... | collective-permute-start | bytes 393224 | tf_op jit(solution)/shard_map/ppermute | solution.py:413
  16.7 21.3 %copy-start.2 = (f32[2,512]{1,0:T(2,128)S(1)}, f32[2,512]{1,0:T(2,128)}, u32[]{:S(2)}) copy-start(f32[2,512]{1,0:T(2,128)} %refs_0_.1) | copy-start | bytes 12292
  16.7 23.5 %all-to-all-start = ((f32[16,16,512]{2,1,0:T(8,128)}), f32[16,16,512]{2,1,0:T(8,128)S(1)}, u32[]{:S(2)}, u32[]{:S(2)}) async-start(f32[16,16,512]{2,1,0:T(8,128)} %range_partner.1), calls=%async_computation | async-start | bytes 1048576 | tf_op jit(solution)/shard_map/all_to_all | solution.py:421
  24.8 8.0 %collective-permute-start.6 = (f32[4,16,512]{2,1,0:T(8,128)S(1)}, f32[4,16,512]{2,1,0:T(8,128)S(1)}, u32[]{:S(2)}, u32[]{:S(2)}) collective-permute-start(f32[4,16,512]{2,1,0:T(8,128)S(1)} %get-tuple-element.30), channel_id=1, source_target_pairs={{0,1},{1,0},{2,3},{3,2},{4,5},{5,4},{6,7},{7,6},{8,9},{9,8},{10,11... | collective-permute-start | bytes 393224 | tf_op jit(solution)/shard_map/ppermute | solution.py:425
  26.7 7.9 %collective-permute-start.7 = (f32[4,16,512]{2,1,0:T(8,128)S(1)}, f32[4,16,512]{2,1,0:T(8,128)S(1)}, u32[]{:S(2)}, u32[]{:S(2)}) collective-permute-start(f32[4,16,512]{2,1,0:T(8,128)S(1)} %get-tuple-element.31), channel_id=1, source_target_pairs={{0,16},{1,17},{2,18},{3,19},{4,20},{5,21},{6,22},{7,23},{8,24},{9,... | collective-permute-start | bytes 393224 | tf_op jit(solution)/shard_map/ppermute | solution.py:425
  28.2 9.8 %collective-permute-start.8 = (f32[4,16,512]{2,1,0:T(8,128)S(1)}, f32[4,16,512]{2,1,0:T(8,128)S(1)}, u32[]{:S(2)}, u32[]{:S(2)}) collective-permute-start(f32[4,16,512]{2,1,0:T(8,128)S(1)} %get-tuple-element.32), channel_id=1, source_target_pairs={{0,17},{1,16},{2,19},{3,18},{4,21},{5,20},{6,23},{7,22},{8,25},{9,... | collective-permute-start | bytes 393224 | tf_op jit(solution)/shard_map/ppermute | solution.py:425

commit v5 on v4

--- a/solution.py
+++ b/solution.py
@@ -25,59 +25,50 @@
 
 
 def toeplitz(row, rows, width):
-    row = jnp.concatenate([row, jnp.zeros((1, width - row.shape[1]), jnp.float32)], axis=1)
+    if width > row.shape[1]:
+        row = jnp.concatenate([row, jnp.zeros((1, width - row.shape[1]), jnp.float32)], axis=1)
     return pltpu.roll(jnp.broadcast_to(row, (rows, width)), 0, axis=1, stride=1, stride_axis=0)
 
 
-def range_kernel(own, planes, lines, blocks, sections, shift_ref, taps_hbm, weights_hbm, echoes_hbm, *refs):
+def range_kernel(own, planes, lines, blocks, sections, *refs):
     if own:
-        *outs, taps_ref, weights_ref, echoes_ref, even, odd, table, compressed, sems, ready, out_sems = refs
+        shift_ref, taps_hbm, weights_hbm, echoes_hbm, *outs, table, taps_ref, weights_ref, echoes_ref, even, odd, compressed, sems = refs
     else:
-        ready, taps_ref, weights_ref, echoes_ref, even, odd, table, compressed, sems = refs
+        shift_ref, table, weights_ref, echoes_ref, out_ref, even, odd, compressed = refs
     segments, levels, inner = planes
     core = lax.rem(lax.axis_index("gx"), CORES)
     width = blocks // (CORES * segments)
-    halo = (sections - 1) // 2 + 1
-    span = width + 2 * halo
-
-    def lanes(block, count):
-        return pl.ds(pl.multiple_of(block * BLOCK, BLOCK), count * BLOCK)
-
-    copies = [
-        pltpu.make_async_copy(taps_hbm, taps_ref, sems.at[0]),
-        pltpu.make_async_copy(weights_hbm, weights_ref, sems.at[1]),
-    ]
-    for segment in range(segments):
-        first = (CORES * segment + core) * width
-        moves = (
-            (jnp.maximum(first - halo, 0), 0, halo),
-            (first, halo, width),
-            (jnp.minimum(first + width, blocks - halo), halo + width, halo),
-        )
-        for n, (source, to, count) in enumerate(moves):
-            target = echoes_ref.at[segment, :, :, to * BLOCK : (to + count) * BLOCK]
-            copies.append(
-                pltpu.make_async_copy(
-                    echoes_hbm.at[:, :, lanes(source, count)], target, sems.at[2 + 3 * segment + n]
-                )
-            )
-    for copy in copies:
-        copy.start()
-    copies[0].wait()
-    copies[1].wait()
-    real = toeplitz(taps_ref[0:1, :], BLOCK, sections * BLOCK)
-    imag = toeplitz(taps_ref[1:2, :], BLOCK, sections * BLOCK)
-    for kind, values in enumerate((real, imag, real - imag)):
-        table[kind, 0], table[kind, 1] = split(values)
-    for copy in copies[2:]:
-        copy.wait()
+    halo = (sections - 1) // 2
+    span = width + 2 + 2 * halo
     at_start, at_end = core == 0, core == CORES - 1
+    if own:
+        copies = [
+            pltpu.make_async_copy(taps_hbm, taps_ref, sems.at[0]),
+            pltpu.make_async_copy(weights_hbm, weights_ref, sems.at[1]),
+            pltpu.make_async_copy(echoes_hbm, echoes_ref, sems.at[2]),
+        ]
+        for copy in copies:
+            copy.start()
+        copies[0].wait()
+        copies[1].wait()
+        real = toeplitz(taps_ref[0:1, :], BLOCK, sections * BLOCK)
+        imag = toeplitz(taps_ref[1:2, :], BLOCK, sections * BLOCK)
+        for kind, values in enumerate((real, imag, real - imag)):
+            table[kind, 0], table[kind, 1] = split(values)
+        copies[2].wait()
 
     def piece(segment, part, block):
-        values = echoes_ref[segment, part, :, block * BLOCK : (block + 1) * BLOCK]
-        if segment == 0 and block < halo:
+        at = (CORES * segment + core) * width + block - halo - 1
+        low = segment == 0 and block <= halo
+        high = segment == segments - 1 and block > halo + width
+        if low:
+            at = jnp.maximum(at, 0)
+        if high:
+            at = jnp.minimum(at, blocks - 1)
+        values = echoes_ref[part, :, pl.ds(pl.multiple_of(at * BLOCK, BLOCK), BLOCK)]
+        if low:
             values = jnp.where(at_start, 0.0, values)
-        if segment == segments - 1 and block >= halo + width:
+        if high:
             values = jnp.where(at_end, 0.0, values)
         return values
 
@@ -115,114 +106,113 @@
         low, high = slice(0, lines), slice(segments * rows - lines, segments * rows)
         compressed[part, low, :] = jnp.where(at_start, 0.0, compressed[part, low, :])
         compressed[part, high, :] = jnp.where(at_end, 0.0, compressed[part, high, :])
-    migrate(lines, segments, width, shift_ref, weights_ref, compressed, ready)
-    if own:
-        mine = lax.axis_index("gy") // inner
-        sends = []
-        for k, out in enumerate(outs):
-            sends.append(pltpu.make_async_copy(ready.at[:, mine ^ k], out, out_sems.at[k]))
-            sends[-1].start()
-        for send in sends:
-            send.wait()
-
-
-def place_of(device, shape):
-    at = []
-    for extent in reversed(shape[:-2]):
-        at.insert(0, device % extent)
-        device //= extent
-    return at
-
-
-def migrate(lines, segments, width, shift_ref, weights_ref, compressed, out_ref):
-    per = out_ref.shape[-1] // LANE
+
+    run = width // levels
+    for segment in range(segments):
+        for step in range(levels):
+            level = (lax.axis_index("gy") // inner) ^ step if own else step
+            first = (segment * (width + 2) + 1 + level * run) * lines
+            for part in range(2):
+
+                def load(tile):
+                    block, at = tile * LANE // BLOCK, tile * LANE % BLOCK
+                    start = first + block * lines
+                    if own:
+                        start = pl.multiple_of(start, lines)
+                    return compressed[part, pl.ds(start, lines), at : at + LANE]
+
+                moved = migrate(lines, run * BLOCK // LANE, shift_ref, weights_ref, load)
+                for tile, values in enumerate(moved):
+                    rows_at = slice(part * lines, (part + 1) * lines)
+                    if own:
+                        per = outs[step].shape[-1] // LANE
+                        at = (tile % per) * LANE
+                        outs[step][segment, tile // per, rows_at, at : at + LANE] = values
+                    else:
+                        per = out_ref.shape[-1] // LANE
+                        at = (tile % per) * LANE
+                        place = (segment * levels + step) * inner + tile // per
+                        out_ref[place, rows_at, at : at + LANE] = values
+
+
+def migrate(lines, tiles, shift_ref, weights_ref, load):
     lane = lax.broadcasted_iota(jnp.int32, (lines, LANE), 1)
     row = lax.broadcasted_iota(jnp.int32, (lines, LANE), 0)
     shift = jnp.zeros((lines, LANE), jnp.int32)
     for line in range(lines):
         shift = jnp.where(row == line, shift_ref[line], shift)
-    places = [lane + shift - (TAPS // 2 - 1) + step for step in range(2)]
-    index = [place & (LANE - 1) for place in places]
-    before = [place < 0 for place in places]
-    after = [place >= LANE for place in places]
-    weight = [jnp.broadcast_to(weights_ref[:, j : j + 1], (lines, LANE)) for j in range(TAPS)]
     inside = lane < LANE - 2
-    tiles = width * BLOCK // LANE
-    first = BLOCK // LANE
-
-    for segment in range(segments):
-        for part in range(2):
-
-            def turned(tile, step):
-                block = segment * (width + 2) + (tile + first) * LANE // BLOCK
-                at = ((tile + first) * LANE) % BLOCK
-                values = compressed[part, block * lines : (block + 1) * lines, at : at + LANE]
-                return jnp.take_along_axis(values, index[step], axis=1, mode="promise_in_bounds")
-
-            later = [turned(tiles + 1, step) for step in range(2)]
-            here = [turned(tiles, step) for step in range(2)]
-            carried = [jnp.zeros((lines, LANE), jnp.float32)] * 3
-            for tile in range(tiles, -1, -1):
-                earlier = [turned(tile - 1, step) for step in range(2)]
-                pair = [
-                    jnp.where(before[step], earlier[step], jnp.where(after[step], later[step], here[step]))
-                    for step in range(2)
-                ]
-                total = None
-                for k in (3, 2, 1, 0):
-                    term = weight[2 * k] * pair[0] + weight[2 * k + 1] * pair[1]
-                    if total is None:
-                        total = term
-                    else:
-                        rolled = pltpu.roll(total, LANE - 2, axis=1)
-                        total = jnp.where(inside, rolled, carried[k]) + term
-                        carried[k] = rolled
-                if tile < tiles:
-                    place = place_of(segment * (tiles // per) + tile // per, out_ref.shape)
-                    at = (tile % per) * LANE
-                    out_ref[(*place, slice(part * lines, (part + 1) * lines), slice(at, at + LANE))] = total
-                later, here = here, earlier
-
-
-def range_call(own, echoes, range_ref, shift_bins, weights, planes):
+    pairs = []
+    for step in range(2):
+        place = lane + shift - (TAPS // 2 - 1) + step
+        index = place & (LANE - 1)
+        turned = [
+            jnp.take_along_axis(load(tile), index, axis=1, mode="promise_in_bounds") for tile in range(-1, tiles + 2)
+        ]
+        pairs.append(
+            [
+                jnp.where(place < 0, turned[tile], jnp.where(place >= LANE, turned[tile + 2], turned[tile + 1]))
+                for tile in range(tiles + 1)
+            ]
+        )
+    totals = None
+    for k in (3, 2, 1, 0):
+        even, odd = [jnp.broadcast_to(weights_ref[:, 2 * k + n : 2 * k + n + 1], (lines, LANE)) for n in range(2)]
+        terms = [even * first + odd * second for first, second in zip(*pairs)]
+        if totals is None:
+            totals = terms
+        else:
+            rolled = [pltpu.roll(total, LANE - 2, axis=1) for total in totals]
+            rolled.append(jnp.zeros((lines, LANE), jnp.float32))
+            totals = [
+                jnp.where(inside, rolled[tile], rolled[tile + 1]) + terms[tile] for tile in range(tiles + 1)
+            ]
+    return totals[:tiles]
+
+
+def range_call(own, echoes, taps, shift_bins, weights, planes):
     lines, range_total = echoes.shape[1], echoes.shape[2]
     blocks = range_total // BLOCK
-    sections = range_ref.shape[1] // BLOCK + 1
+    sections = (taps.shape[1] if own else taps.shape[-1] - BLOCK) // BLOCK + 1
     segments, levels, inner = planes
     bins = range_total // (CORES * segments * levels * inner)
     width = blocks // (CORES * segments)
     span = width + sections + 1
     flops = 2 * 3 * 3 * segments * (width + 2) * lines * sections * BLOCK * BLOCK
+    vmem, hbm = pl.BlockSpec(memory_space=pltpu.VMEM), pl.BlockSpec(memory_space=pltpu.HBM)
     scratch = [
-        pltpu.VMEM(range_ref.shape, jnp.float32),
-        pltpu.VMEM(weights.shape, jnp.float32),
-        pltpu.VMEM((segments, 2, lines, span * BLOCK), jnp.float32),
         pltpu.VMEM((3, 2, segments * span * lines, BLOCK), jnp.bfloat16),
         pltpu.VMEM((3, 2, segments * span * lines, BLOCK), jnp.bfloat16),
-        pltpu.VMEM((3, 2, BLOCK, sections * BLOCK), jnp.bfloat16),
         pltpu.VMEM((2, segments * (width + 2) * lines, BLOCK), jnp.float32),
-        pltpu.SemaphoreType.DMA((2 + 3 * segments,)),
-    ]
+    ]
+    operands = [shift_bins, taps, weights, echoes]
     if own:
+        operands = [pltpu.with_memory_space_constraint(array, pltpu.HBM) for array in operands]
+        in_specs = [pl.BlockSpec(memory_space=pltpu.SMEM), hbm, hbm, hbm]
         out_shape = [jax.ShapeDtypeStruct((segments, inner, 2 * lines, bins), jnp.float32)] * levels
-        out_specs = [pl.BlockSpec(memory_space=pltpu.HBM)] * levels
-        scratch += [
-            pltpu.VMEM((segments, levels, inner, 2 * lines, bins), jnp.float32),
-            pltpu.SemaphoreType.DMA((levels,)),
+        out_shape += [jax.ShapeDtypeStruct((3, 2, BLOCK, sections * BLOCK), jnp.bfloat16)]
+        out_specs = [vmem] * (levels + 1)
+        scratch = [
+            pltpu.VMEM(taps.shape, jnp.float32),
+            pltpu.VMEM(weights.shape, jnp.float32),
+            pltpu.VMEM(echoes.shape, jnp.float32),
+            *scratch,
+            pltpu.SemaphoreType.DMA((3,)),
         ]
     else:
+        in_specs = [pl.BlockSpec(memory_space=pltpu.SMEM), vmem, vmem, vmem]
         out_shape = jax.ShapeDtypeStruct((segments * levels * inner, 2 * lines, bins), jnp.float32)
-        out_specs = pl.BlockSpec(memory_space=pltpu.VMEM)
+        out_specs = vmem
     return pl.pallas_call(
         functools.partial(range_kernel, own, planes, lines, blocks, sections),
         out_shape=out_shape,
-        in_specs=[pl.BlockSpec(memory_space=pltpu.SMEM)] + [pl.BlockSpec(memory_space=pltpu.HBM if own else pl.ANY)] * 3,
+        in_specs=in_specs,
         out_specs=out_specs,
         scratch_shapes=scratch,
-        compiler_params=pltpu.CompilerParams(vmem_limit_bytes=(60 if own else 40) << 20),
+        compiler_params=pltpu.CompilerParams(vmem_limit_bytes=24 << 20),
         cost_estimate=pl.CostEstimate(flops=flops, bytes_accessed=3 * echoes.size * 2, transcendentals=0),
         name="range_own" if own else "range_partner",
-    )(shift_bins, range_ref, weights, echoes)
+    )(*operands)
 
 
 def regroup_kernel(levels, plane, *refs):
@@ -263,14 +253,15 @@
 def azimuth_tables(taps_ref, table):
     length = taps_ref.shape[1]
     diagonals = table.shape[2]
+    first = (length // BLOCK + 1 - diagonals) // 2
+    zeros = jnp.zeros((1, BLOCK), jnp.float32)
     for part in range(2):
-        row = jnp.concatenate(
-            [jnp.zeros((1, BLOCK), jnp.float32), taps_ref[part : part + 1, :]], axis=1
-        )
-        full = toeplitz(row, BLOCK, length + 2 * BLOCK)
-        for diagonal in range(diagonals):
-            at = (diagonal + 1) * BLOCK
-            table[part, 0, diagonal], table[part, 1, diagonal] = split(full[:, at : at + BLOCK])
+        row = jnp.concatenate([zeros, taps_ref[part : part + 1, :], zeros], axis=1)
+        width = (diagonals + 1) * BLOCK
+        full = toeplitz(row[:, first * BLOCK : first * BLOCK + width], BLOCK, width)
+        for n in range(diagonals):
+            at = (n + 1) * BLOCK
+            table[part, 0, n], table[part, 1, n] = split(full[:, at : at + BLOCK])
 
 
 def azimuth_sums(table, lines_ref):
@@ -355,7 +346,7 @@
 
 def azimuth_call(planes, count, bins, azimuth_ref, arrived=None, table=None, moved=None, earlier=None):
     segments, levels, inner = planes
-    diagonals = azimuth_ref.shape[1] // BLOCK + 1
+    diagonals = min(azimuth_ref.shape[1] // BLOCK + 1, 2 * (count // BLOCK) - 1)
     image = jax.ShapeDtypeStruct((2, count, bins), jnp.float32)
     vmem = pl.BlockSpec(memory_space=pltpu.VMEM)
     scratch = [pltpu.VMEM((2, count, bins), jnp.float32)]
@@ -379,7 +370,7 @@
         in_specs=in_specs,
         out_specs=out_specs,
         scratch_shapes=scratch,
-        compiler_params=pltpu.CompilerParams(vmem_limit_bytes=40 << 20),
+        compiler_params=pltpu.CompilerParams(vmem_limit_bytes=24 << 20),
         cost_estimate=pl.CostEstimate(
             flops=weight * 2 * 3 * 4 * count * BLOCK * bins, bytes_accessed=4 * 4 * count * bins, transcendentals=0
         ),
@@ -408,12 +399,11 @@
     partner = [
         lax.ppermute(array, AXES, pairs_of(planes, core_step=1)) for array in (echoes, shift_bins, interp_weights)
     ]
-    by_level = range_call(True, echoes, range_ref, shift_bins, interp_weights, planes)
+    *by_level, table = range_call(True, echoes, range_ref, shift_bins, interp_weights, planes)
     received = [by_level[0]] + [
         lax.ppermute(by_level[k], AXES, pairs_of(planes, level_step=k)) for k in range(1, levels)
     ]
-    *by_level, taps_later = lax.optimization_barrier((*by_level, range_ref))
-    migrated = range_call(False, partner[0], taps_later, partner[1], partner[2], planes)
+    migrated = range_call(False, partner[0], table, partner[1], partner[2], planes)
     groups = [
         [(segment * CORES + core) * run + at for segment in range(segments) for at in range(run)]
         for core in range(CORES)

time: 42.6 us -> 41.2 us (0.967)
  Pallas kernels: 15.6 us -> 14.6 us
    pallas_call x2, Pallas kernels: 10.4 us -> 9.48 us  [range_call(): pl.pallas_call(functools.partial(range_kernel, own, planes, lines, blocks...]
  transfers between devices with their start and end apart: 10 -> 10, of which waited for: 3 -> 3; matrix products, arithmetic and copies ran while one was open for 0% -> 0% of each run, Pallas kernels for 32% -> 31%
where the time goes in v5:
time: 41.2 us; the launch traced here: 41 us
  starting transfers between devices  16.8 us (41%)
  Pallas kernels  14.6 us (35%)
  waiting for transfers between devices  9.48 us (23%)
    pallas_call x2, Pallas kernels, range_call(): pl.pallas_call(functools.partial(range_kernel, own, planes, lines, blocks...  9.48 us
    ppermute x3, waiting for transfers between devices, per_device(): lax.ppermute(by_place[q], AXES, pairs_of(planes, place_step=q))  9.46 us
    all_to_all x1, starting transfers between devices, per_device(): lax.all_to_all(migrated, AXES, split_axis=0, concat_axis=0, axis_index_gr...  7.07 us
    ppermute x3, starting transfers between devices, per_device(): lax.ppermute(by_level[k], AXES, pairs_of(planes, level_step=k))  5.23 us
    pallas_call x2, Pallas kernels, azimuth_call(): pl.pallas_call(functools.partial(kernel, planes), out_shape=out_shape, in...  4.22 us
    ppermute x3, starting transfers between devices, per_device(): lax.ppermute(by_place[q], AXES, pairs_of(planes, place_step=q))  3.55 us
    ppermute x3, starting transfers between devices, per_device(): lax.ppermute(array, AXES, pairs_of(planes, core_step=1))  0.96 us
    pallas_call x1, Pallas kernels, regroup_call(): pl.pallas_call(functools.partial(regroup_kernel, levels, plane), out_shap...  0.9 us
  transfers between devices with their start and end apart: 10, of which 3 were waited for; matrix products, arithmetic and copies ran while one was open for 0% of the time, Pallas kernels for 31%

profile of v5, /device:TPU:0, one launch (start us, length us, event | category | flops | bytes accessed | tf_op | source)
XLA Modules:
  0.0 41.0 jit_solution(2342195368248575252)
XLA Ops:
  0.0 0.5 %collective-permute-start.5 = (f32[2,8,16384]{2,1,0:T(8,128)}, f32[2,8,16384]{2,1,0:T(8,128)S(1)}, u32[]{:S(2)}, u32[]{:S(2)}) collective-permute-start(f32[2,8,16384]{2,1,0:T(8,128)} %refs_3_.1), channel_id=1, source_target_pairs={{0,8},{1,9},{2,10},{3,11},{4,12},{5,13},{6,14},{7,15},{8,0},{9,1},... | collective-permute-start | bytes 3145736 | tf_op jit(solution)/shard_map/ppermute | solution.py:400
  0.5 0.1 collective-permute-start.3
  0.5 0.5 %collective-permute-start.4 = (f32[8,8]{1,0:T(8,128)}, f32[8,8]{1,0:T(8,128)S(1)}, u32[]{:S(2)}, u32[]{:S(2)}) collective-permute-start(f32[8,8]{1,0:T(8,128)} %refs_2_.1), channel_id=1, source_target_pairs={{0,8},{1,9},{2,10},{3,11},{4,12},{5,13},{6,14},{7,15},{8,0},{9,1},... | collective-permute-start | bytes 776 | tf_op jit(solution)/shard_map/ppermute | solution.py:400
  1.0 4.9 %range_own.1 = (f32[2,2,16,512]{3,2,1,0:T(8,128)S(1)}, f32[2,2,16,512]{3,2,1,0:T(8,128)S(1)}, f32[2,2,16,512]{3,2,1,0:T(8,128)S(1)}, f32[2,2,16,512]{3,2,1,0:T(8,128)S(1)}, bf16[3,2,256,1280]{3,2,1,0:T(8,128)(2,1)S(1)}) custom-call(s32[8]{0:T(128)} %refs_0_.2, f32[2,1024]{1,0:T(2,128)} %refs_1_.1, f32[8,8]{1,0:T(8,128)} %refs_2_.1, f32[2,8,16384]{2,1,0:T(8,128)} %refs_3_.1), custom_call_target="tpu_custom_call" | custom-call | flops 1698693120 | bytes 1572864 | tf_op jit(solution)/shard_map/range_own/pallas_call | solution.py:206
  5.9 2.6 %collective-permute-start = (f32[2,2,16,512]{3,2,1,0:T(8,128)S(1)}, f32[2,2,16,512]{3,2,1,0:T(8,128)S(1)}, u32[]{:S(2)}, u32[]{:S(2)}) collective-permute-start(f32[2,2,16,512]{3,2,1,0:T(8,128)S(1)} %get-tuple-element.21), channel_id=1, source_target_pairs={{0,2},{1,3},{2,0},{3,1},{4,6},{5,7},{6,4},{7,5},{8,10},{9,11},{10,... | collective-permute-start | bytes 393224 | tf_op jit(solution)/shard_map/ppermute | solution.py:404
  8.6 2.6 %collective-permute-start.1 = (f32[2,2,16,512]{3,2,1,0:T(8,128)S(1)}, f32[2,2,16,512]{3,2,1,0:T(8,128)S(1)}, u32[]{:S(2)}, u32[]{:S(2)}) collective-permute-start(f32[2,2,16,512]{3,2,1,0:T(8,128)S(1)} %get-tuple-element.22), channel_id=1, source_target_pairs={{0,4},{1,5},{2,6},{3,7},{4,0},{5,1},{6,2},{7,3},{8,12},{9,13},{10,... | collective-permute-start | bytes 393224 | tf_op jit(solution)/shard_map/ppermute | solution.py:404
  11.1 0.0 collective-permute-done.3.refs_0_
  11.1 0.0 collective-permute-start.2
  11.1 0.0 collective-permute-done.4.refs_2_
  11.1 0.0 collective-permute-done.5.refs_3_
  11.2 0.0 copy-start
  11.2 4.5 %range_partner.1 = f32[16,16,512]{2,1,0:T(8,128)} custom-call(s32[8]{0:T(128)S(1)} %collective-permute-done.3.refs_0_, bf16[3,2,256,1280]{3,2,1,0:T(8,128)(2,1)S(1)} %get-tuple-element.24.refs_1_, f32[8,8]{1,0:T(8,128)S(1)} %collective-permute-done.4.refs_2_, f32[2,8,16384]{2,1,0:T(8,128)S(1)} %collective-permute-done.5.refs_3_), custom_call_target="tpu_custom_call" | custom-call | flops 1698693120 | bytes 1572864 | tf_op jit(solution)/shard_map/range_partner/pallas_call | solution.py:206
  15.7 7.1 %all-to-all-start = ((f32[16,16,512]{2,1,0:T(8,128)}), f32[16,16,512]{2,1,0:T(8,128)S(1)}, u32[]{:S(2)}, u32[]{:S(2)}) async-start(f32[16,16,512]{2,1,0:T(8,128)} %range_partner.1), calls=%async_computation | async-start | bytes 1048576 | tf_op jit(solution)/shard_map/all_to_all | solution.py:411
  22.8 0.0 collective-permute-done.refs_1_
  22.8 0.0 collective-permute-done.1.refs_2_
  22.8 0.0 collective-permute-done.2.refs_3_
  22.8 0.9 %regroup.1 = (f32[4,16,512]{2,1,0:T(8,128)S(1)}, f32[4,16,512]{2,1,0:T(8,128)S(1)}, f32[4,16,512]{2,1,0:T(8,128)S(1)}, f32[4,16,512]{2,1,0:T(8,128)S(1)}) custom-call(f32[2,2,16,512]{3,2,1,0:T(8,128)S(1)} %get-tuple-element.25.refs_0_, f32[2,2,16,512]{3,2,1,0:T(8,128)S(1)} %collective-permute-done.refs_1_, ...), custom_call_target="tpu_custom_call" | custom-call | bytes 1048576 | tf_op jit(solution)/shard_map/regroup/pallas_call | solution.py:241
  23.7 2.0 %collective-permute-start.6 = (f32[4,16,512]{2,1,0:T(8,128)S(1)}, f32[4,16,512]{2,1,0:T(8,128)S(1)}, u32[]{:S(2)}, u32[]{:S(2)}) collective-permute-start(f32[4,16,512]{2,1,0:T(8,128)S(1)} %get-tuple-element.30), channel_id=1, source_target_pairs={{0,1},{1,0},{2,3},{3,2},{4,5},{5,4},{6,7},{7,6},{8,9},{9,8},{10,11... | collective-permute-start | bytes 393224 | tf_op jit(solution)/shard_map/ppermute | solution.py:415
  25.7 1.5 %collective-permute-start.7 = (f32[4,16,512]{2,1,0:T(8,128)S(1)}, f32[4,16,512]{2,1,0:T(8,128)S(1)}, u32[]{:S(2)}, u32[]{:S(2)}) collective-permute-start(f32[4,16,512]{2,1,0:T(8,128)S(1)} %get-tuple-element.31), channel_id=1, source_target_pairs={{0,16},{1,17},{2,18},{3,19},{4,20},{5,21},{6,22},{7,23},{8,24},{9,... | collective-permute-start | bytes 393224 | tf_op jit(solution)/shard_map/ppermute | solution.py:415
  27.2 0.1 collective-permute-start.8
  27.3 4.4 %collective-permute-done.6.refs_2_ = f32[4,16,512]{2,1,0:T(8,128)S(1)} collective-permute-done((f32[4,16,512]{2,1,0:T(8,128)S(1)}, f32[4,16,512]{2,1,0:T(8,128)S(1)}, u32[]{:S(2)}, u32[]{:S(2)}) %collective-permute-start.6) | collective-permute-done | bytes 131104 | tf_op jit(solution)/shard_map/ppermute | solution.py:415
  31.7 2.0 %collective-permute-done.7.refs_3_ = f32[4,16,512]{2,1,0:T(8,128)S(1)} collective-permute-done((f32[4,16,512]{2,1,0:T(8,128)S(1)}, f32[4,16,512]{2,1,0:T(8,128)S(1)}, u32[]{:S(2)}, u32[]{:S(2)}) %collective-permute-start.7) | collective-permute-done | bytes 131104 | tf_op jit(solution)/shard_map/ppermute | solution.py:415
  33.7 3.1 %collective-permute-done.8.refs_4_ = f32[4,16,512]{2,1,0:T(8,128)S(1)} collective-permute-done((f32[4,16,512]{2,1,0:T(8,128)S(1)}, f32[4,16,512]{2,1,0:T(8,128)S(1)}, u32[]{:S(2)}, u32[]{:S(2)}) %collective-permute-start.8) | collective-permute-done | bytes 131104 | tf_op jit(solution)/shard_map/ppermute | solution.py:415
  36.8 0.0 copy-done
  36.8 2.1 %azimuth_first.1 = (f32[2,256,512]{2,1,0:T(8,128)S(1)}, bf16[2,2,1,256,256]{4,3,2,1,0:T(8,128)(2,1)S(1)}) custom-call(f32[2,512]{1,0:T(2,128)S(1)} %copy-done, f32[4,16,512]{2,1,0:T(8,128)S(1)} %get-tuple-element.29.refs_1_, f32[4,16,512]{2,1,0:T(8,128)S(1)} %collective-permute-done.6.refs_2_, f32[4,16,512]{2,1,0:T(8,128)S(1)} %collective-permute-done.7.refs_3_, ...), custom_call_target="tpu_custom_call" | custom-call | flops 8053063680 | bytes 2097152 | tf_op jit(solution)/shard_map/azimuth_first/pallas_call | solution.py:367
  38.9 0.0 all-to-all-done.moved_ref
  38.9 2.1 %azimuth_second.1 = f32[2,256,512]{2,1,0:T(8,128)} custom-call(bf16[2,2,1,256,256]{4,3,2,1,0:T(8,128)(2,1)S(1)} %get-tuple-element.33.table, f32[16,16,512]{2,1,0:T(8,128)S(1)} %all-to-all-done.moved_ref, f32[2,256,512]{2,1,0:T(8,128)S(1)} %get-tuple-element.34.earlier_ref), custom_call_target="tpu_custom_call" | custom-call | flops 805306368 | bytes 2097152 | tf_op jit(solution)/shard_map/azimuth_second/pallas_call | solution.py:367
Async XLA Ops:
  0.0 11.2 %collective-permute-start.5 = (f32[2,8,16384]{2,1,0:T(8,128)}, f32[2,8,16384]{2,1,0:T(8,128)S(1)}, u32[]{:S(2)}, u32[]{:S(2)}) collective-permute-start(f32[2,8,16384]{2,1,0:T(8,128)} %refs_3_.1), channel_id=1, source_target_pairs={{0,8},{1,9},{2,10},{3,11},{4,12},{5,13},{6,14},{7,15},{8,0},{9,1},... | collective-permute-start | bytes 3145736 | tf_op jit(solution)/shard_map/ppermute | solution.py:400
  0.5 10.7 %collective-permute-start.3 = (s32[8]{0:T(128)}, s32[8]{0:T(128)S(1)}, u32[]{:S(2)}, u32[]{:S(2)}) collective-permute-start(s32[8]{0:T(128)} %refs_0_.2), channel_id=1, source_target_pairs={{0,8},{1,9},{2,10},{3,11},{4,12},{5,13},{6,14},{7,15},{8,0},{9,1},... | collective-permute-start | bytes 104 | tf_op jit(solution)/shard_map/ppermute | solution.py:400
  0.5 10.6 %collective-permute-start.4 = (f32[8,8]{1,0:T(8,128)}, f32[8,8]{1,0:T(8,128)S(1)}, u32[]{:S(2)}, u32[]{:S(2)}) collective-permute-start(f32[8,8]{1,0:T(8,128)} %refs_2_.1), channel_id=1, source_target_pairs={{0,8},{1,9},{2,10},{3,11},{4,12},{5,13},{6,14},{7,15},{8,0},{9,1},... | collective-permute-start | bytes 776 | tf_op jit(solution)/shard_map/ppermute | solution.py:400
  5.9 16.9 %collective-permute-start = (f32[2,2,16,512]{3,2,1,0:T(8,128)S(1)}, f32[2,2,16,512]{3,2,1,0:T(8,128)S(1)}, u32[]{:S(2)}, u32[]{:S(2)}) collective-permute-start(f32[2,2,16,512]{3,2,1,0:T(8,128)S(1)} %get-tuple-element.21), channel_id=1, source_target_pairs={{0,2},{1,3},{2,0},{3,1},{4,6},{5,7},{6,4},{7,5},{8,10},{9,11},{10,... | collective-permute-start | bytes 393224 | tf_op jit(solution)/shard_map/ppermute | solution.py:404
  8.6 14.3 %collective-permute-start.1 = (f32[2,2,16,512]{3,2,1,0:T(8,128)S(1)}, f32[2,2,16,512]{3,2,1,0:T(8,128)S(1)}, u32[]{:S(2)}, u32[]{:S(2)}) collective-permute-start(f32[2,2,16,512]{3,2,1,0:T(8,128)S(1)} %get-tuple-element.22), channel_id=1, source_target_pairs={{0,4},{1,5},{2,6},{3,7},{4,0},{5,1},{6,2},{7,3},{8,12},{9,13},{10,... | collective-permute-start | bytes 393224 | tf_op jit(solution)/shard_map/ppermute | solution.py:404
  11.1 11.7 %collective-permute-start.2 = (f32[2,2,16,512]{3,2,1,0:T(8,128)S(1)}, f32[2,2,16,512]{3,2,1,0:T(8,128)S(1)}, u32[]{:S(2)}, u32[]{:S(2)}) collective-permute-start(f32[2,2,16,512]{3,2,1,0:T(8,128)S(1)} %get-tuple-element.23), channel_id=1, source_target_pairs={{0,6},{1,7},{2,4},{3,5},{4,2},{5,3},{6,0},{7,1},{8,14},{9,15},{10,... | collective-permute-start | bytes 393224 | tf_op jit(solution)/shard_map/ppermute | solution.py:404
  11.2 25.6 %copy-start = (f32[2,512]{1,0:T(2,128)S(1)}, f32[2,512]{1,0:T(2,128)}, u32[]{:S(2)}) copy-start(f32[2,512]{1,0:T(2,128)} %refs_0_.3) | copy-start | bytes 12292
  15.7 23.2 %all-to-all-start = ((f32[16,16,512]{2,1,0:T(8,128)}), f32[16,16,512]{2,1,0:T(8,128)S(1)}, u32[]{:S(2)}, u32[]{:S(2)}) async-start(f32[16,16,512]{2,1,0:T(8,128)} %range_partner.1), calls=%async_computation | async-start | bytes 1048576 | tf_op jit(solution)/shard_map/all_to_all | solution.py:411
  23.7 8.0 %collective-permute-start.6 = (f32[4,16,512]{2,1,0:T(8,128)S(1)}, f32[4,16,512]{2,1,0:T(8,128)S(1)}, u32[]{:S(2)}, u32[]{:S(2)}) collective-permute-start(f32[4,16,512]{2,1,0:T(8,128)S(1)} %get-tuple-element.30), channel_id=1, source_target_pairs={{0,1},{1,0},{2,3},{3,2},{4,5},{5,4},{6,7},{7,6},{8,9},{9,8},{10,11... | collective-permute-start | bytes 393224 | tf_op jit(solution)/shard_map/ppermute | solution.py:415
  25.7 7.9 %collective-permute-start.7 = (f32[4,16,512]{2,1,0:T(8,128)S(1)}, f32[4,16,512]{2,1,0:T(8,128)S(1)}, u32[]{:S(2)}, u32[]{:S(2)}) collective-permute-start(f32[4,16,512]{2,1,0:T(8,128)S(1)} %get-tuple-element.31), channel_id=1, source_target_pairs={{0,16},{1,17},{2,18},{3,19},{4,20},{5,21},{6,22},{7,23},{8,24},{9,... | collective-permute-start | bytes 393224 | tf_op jit(solution)/shard_map/ppermute | solution.py:415
  27.2 9.6 %collective-permute-start.8 = (f32[4,16,512]{2,1,0:T(8,128)S(1)}, f32[4,16,512]{2,1,0:T(8,128)S(1)}, u32[]{:S(2)}, u32[]{:S(2)}) collective-permute-start(f32[4,16,512]{2,1,0:T(8,128)S(1)} %get-tuple-element.32), channel_id=1, source_target_pairs={{0,17},{1,16},{2,19},{3,18},{4,21},{5,20},{6,23},{7,22},{8,25},{9,... | collective-permute-start | bytes 393224 | tf_op jit(solution)/shard_map/ppermute | solution.py:415

commit v6 on v5

--- a/solution.py
+++ b/solution.py
@@ -13,7 +13,7 @@
 AXES = ("gx", "gy")
 CORES = 2
 LEVELS = 4
-AHEAD = 10
+AHEAD = 20000
 
 ROWS_BY_ROWS = (((1,), (1,)), ((), ()))
 PLAIN = (((1,), (0,)), ((), ()))
@@ -34,7 +34,7 @@
     if own:
         shift_ref, taps_hbm, weights_hbm, echoes_hbm, *outs, table, taps_ref, weights_ref, echoes_ref, even, odd, compressed, sems = refs
     else:
-        shift_ref, table, weights_ref, echoes_ref, out_ref, even, odd, compressed = refs
+        shift_ref, table, weights_ref, echoes_ref, out_ref, even, odd, compressed, ready, sems = refs
     segments, levels, inner = planes
     core = lax.rem(lax.axis_index("gx"), CORES)
     width = blocks // (CORES * segments)
@@ -107,67 +107,94 @@
         compressed[part, low, :] = jnp.where(at_start, 0.0, compressed[part, low, :])
         compressed[part, high, :] = jnp.where(at_end, 0.0, compressed[part, high, :])
 
+    plan = migration_plan(lines, shift_ref, weights_ref)
+    sends = []
     run = width // levels
-    for segment in range(segments):
-        for step in range(levels):
-            level = (lax.axis_index("gy") // inner) ^ step if own else step
+    for step in range(levels):
+        level = (lax.axis_index("gy") // inner) ^ step if own else step
+        streams = [(segment, part) for segment in range(segments) for part in range(2)]
+
+        def loader(segment, part):
             first = (segment * (width + 2) + 1 + level * run) * lines
-            for part in range(2):
-
-                def load(tile):
-                    block, at = tile * LANE // BLOCK, tile * LANE % BLOCK
-                    start = first + block * lines
-                    if own:
-                        start = pl.multiple_of(start, lines)
-                    return compressed[part, pl.ds(start, lines), at : at + LANE]
-
-                moved = migrate(lines, run * BLOCK // LANE, shift_ref, weights_ref, load)
-                for tile, values in enumerate(moved):
-                    rows_at = slice(part * lines, (part + 1) * lines)
-                    if own:
-                        per = outs[step].shape[-1] // LANE
-                        at = (tile % per) * LANE
-                        outs[step][segment, tile // per, rows_at, at : at + LANE] = values
-                    else:
-                        per = out_ref.shape[-1] // LANE
-                        at = (tile % per) * LANE
-                        place = (segment * levels + step) * inner + tile // per
-                        out_ref[place, rows_at, at : at + LANE] = values
-
-
-def migrate(lines, tiles, shift_ref, weights_ref, load):
+
+            def load(tile):
+                block, at = tile * LANE // BLOCK, tile * LANE % BLOCK
+                start = first + block * lines
+                if own:
+                    start = pl.multiple_of(start, lines)
+                return compressed[part, pl.ds(start, lines), at : at + LANE]
+
+            return load
+
+        moved = migrate(run * BLOCK // LANE, plan, [loader(*stream) for stream in streams])
+        for (segment, part), row in zip(streams, moved):
+            target = (outs[step] if own else ready.at[step]).at[segment]
+            per = target.shape[-1] // LANE
+            for tile, values in enumerate(row):
+                at = (tile % per) * LANE
+                target[tile // per, part * lines : (part + 1) * lines, at : at + LANE] = values
+        if not own:
+            for segment in range(segments):
+                first = (segment * levels + step) * inner
+                sends.append(
+                    pltpu.make_async_copy(
+                        ready.at[step, segment], out_ref.at[first : first + inner], sems.at[step, segment]
+                    )
+                )
+                sends[-1].start()
+    for send in sends:
+        send.wait()
+
+
+def migration_plan(lines, shift_ref, weights_ref):
     lane = lax.broadcasted_iota(jnp.int32, (lines, LANE), 1)
     row = lax.broadcasted_iota(jnp.int32, (lines, LANE), 0)
     shift = jnp.zeros((lines, LANE), jnp.int32)
     for line in range(lines):
         shift = jnp.where(row == line, shift_ref[line], shift)
-    inside = lane < LANE - 2
-    pairs = []
+    steps = []
     for step in range(2):
         place = lane + shift - (TAPS // 2 - 1) + step
-        index = place & (LANE - 1)
+        steps.append((place & (LANE - 1), place < 0, place >= LANE))
+    weights = [jnp.broadcast_to(weights_ref[:, j : j + 1], (lines, LANE)) for j in range(TAPS)]
+    return steps, weights, lane
+
+
+def migrate(tiles, plan, loads):
+    steps, weights, lane = plan
+    pairs = []
+    for index, below, above in steps:
         turned = [
-            jnp.take_along_axis(load(tile), index, axis=1, mode="promise_in_bounds") for tile in range(-1, tiles + 2)
+            [
+                jnp.take_along_axis(load(tile), index, axis=1, mode="promise_in_bounds")
+                for tile in range(-1, tiles + 2)
+            ]
+            for load in loads
         ]
         pairs.append(
             [
-                jnp.where(place < 0, turned[tile], jnp.where(place >= LANE, turned[tile + 2], turned[tile + 1]))
-                for tile in range(tiles + 1)
+                [
+                    jnp.where(below, row[tile], jnp.where(above, row[tile + 2], row[tile + 1]))
+                    for tile in range(tiles + 1)
+                ]
+                for row in turned
             ]
         )
     totals = None
-    for k in (3, 2, 1, 0):
-        even, odd = [jnp.broadcast_to(weights_ref[:, 2 * k + n : 2 * k + n + 1], (lines, LANE)) for n in range(2)]
-        terms = [even * first + odd * second for first, second in zip(*pairs)]
-        if totals is None:
-            totals = terms
-        else:
-            rolled = [pltpu.roll(total, LANE - 2, axis=1) for total in totals]
-            rolled.append(jnp.zeros((lines, LANE), jnp.float32))
-            totals = [
-                jnp.where(inside, rolled[tile], rolled[tile + 1]) + terms[tile] for tile in range(tiles + 1)
-            ]
-    return totals[:tiles]
+    for k in range(TAPS // 2):
+        terms = [
+            [weights[2 * k] * one + weights[2 * k + 1] * two for one, two in zip(*rows)] for rows in zip(*pairs)
+        ]
+        if k == 0:
+            totals = [row[:tiles] for row in terms]
+            continue
+        rolled = [[pltpu.roll(term, LANE - 2 * k, axis=1) for term in row] for row in terms]
+        inside = lane < LANE - 2 * k
+        totals = [
+            [total[tile] + jnp.where(inside, row[tile], row[tile + 1]) for tile in range(tiles)]
+            for total, row in zip(totals, rolled)
+        ]
+    return totals
 
 
 def range_call(own, echoes, taps, shift_bins, weights, planes):
@@ -202,7 +229,11 @@
     else:
         in_specs = [pl.BlockSpec(memory_space=pltpu.SMEM), vmem, vmem, vmem]
         out_shape = jax.ShapeDtypeStruct((segments * levels * inner, 2 * lines, bins), jnp.float32)
-        out_specs = vmem
+        out_specs = hbm
+        scratch += [
+            pltpu.VMEM((levels, segments, inner, 2 * lines, bins), jnp.float32),
+            pltpu.SemaphoreType.DMA((levels, segments)),
+        ]
     return pl.pallas_call(
         functools.partial(range_kernel, own, planes, lines, blocks, sections),
         out_shape=out_shape,
@@ -291,91 +322,69 @@
         yield 1, at, product(b, 0, 1) - product(b, 1, 0)
 
 
-def clear_other(lines_ref, segments, core):
-    run = lines_ref.shape[1] // (CORES * segments)
-    for segment in range(segments):
-        rows = pl.ds(pl.multiple_of((CORES * segment + 1 - core) * run, run), run)
-        for part in range(2):
-            lines_ref[part, rows, :] = jnp.zeros((run, lines_ref.shape[2]), jnp.float32)
-
-
-def azimuth_first(planes, *refs):
+def azimuth_kernel(planes, *refs):
     segments, levels, inner = planes
-    taps_ref, *sources, out_ref, table, lines_ref, sems = refs
-    lines = sources[0].shape[1] // 2
+    table, moved_ref, *arrived, out_hbm, lines_ref, image, sems = refs
+    lines = moved_ref.shape[1] // 2
+    run = levels * inner
     core = lax.rem(lax.axis_index("gx"), CORES)
     level = lax.axis_index("gy") // inner
     mine = place_here(inner)
-    copies = []
-    for q, source in enumerate(sources):
+    for q, source in enumerate(arrived):
         place = mine ^ q
         for k in range(levels):
             device = (((place // inner) * CORES + core) * levels + (level ^ k)) * inner + lax.rem(place, inner)
             rows = pl.ds(pl.multiple_of(device * lines, lines), lines)
             for part in range(2):
-                copies.append(
-                    pltpu.make_async_copy(
-                        source.at[k, part * lines : (part + 1) * lines], lines_ref.at[part, rows], sems.at[q, k, part]
-                    )
-                )
-                copies[-1].start()
-    clear_other(lines_ref, segments, core)
-    for copy in copies:
-        copy.wait()
-    azimuth_tables(taps_ref, table)
+                lines_ref[part, rows, :] = source[k, part * lines : (part + 1) * lines, :]
+    for segment in range(segments):
+        first = (CORES * segment + 1 - core) * run * lines
+        rows = pl.ds(pl.multiple_of(first, run * lines), run * lines)
+        for part in range(2):
+            values = moved_ref[segment * run : (segment + 1) * run, part * lines : (part + 1) * lines, :]
+            lines_ref[part, rows, :] = values.reshape(run * lines, values.shape[-1])
+    sends = []
     for part, at, sums in azimuth_sums(table, lines_ref):
-        out_ref[part, at, :] = sums
-
-
-def azimuth_second(planes, table, moved_ref, earlier_ref, out_ref, lines_ref):
-    segments, levels, inner = planes
-    lines = moved_ref.shape[1] // 2
-    run = levels * inner * lines
-    core = lax.rem(lax.axis_index("gx"), CORES)
-    clear_other(lines_ref, segments, 1 - core)
-    for segment in range(segments):
-        rows = pl.ds(pl.multiple_of((CORES * segment + 1 - core) * run, run), run)
-        for part in range(2):
-            values = moved_ref[
-                segment * levels * inner : (segment + 1) * levels * inner, part * lines : (part + 1) * lines, :
-            ]
-            lines_ref[part, rows, :] = values.reshape(run, values.shape[-1])
-    for part, at, sums in azimuth_sums(table, lines_ref):
-        out_ref[part, at, :] = earlier_ref[part, at, :] + sums
-
-
-def azimuth_call(planes, count, bins, azimuth_ref, arrived=None, table=None, moved=None, earlier=None):
-    segments, levels, inner = planes
-    diagonals = min(azimuth_ref.shape[1] // BLOCK + 1, 2 * (count // BLOCK) - 1)
-    image = jax.ShapeDtypeStruct((2, count, bins), jnp.float32)
+        image[part, at, :] = sums
+        sends.append(pltpu.make_async_copy(image.at[part, at], out_hbm.at[part, at], sems.at[len(sends)]))
+        sends[-1].start()
+    for send in sends:
+        send.wait()
+
+
+def azimuth_call(planes, count, table, moved, arrived):
+    bins = moved.shape[-1]
     vmem = pl.BlockSpec(memory_space=pltpu.VMEM)
-    scratch = [pltpu.VMEM((2, count, bins), jnp.float32)]
-    if earlier is None:
-        kernel = azimuth_first
-        operands = [azimuth_ref, *arrived]
-        in_specs = [vmem] + [pl.BlockSpec(memory_space=pl.ANY)] * len(arrived)
-        out_shape = [image, jax.ShapeDtypeStruct((2, 2, diagonals, BLOCK, BLOCK), jnp.bfloat16)]
-        out_specs = [vmem, vmem]
-        scratch += [pltpu.SemaphoreType.DMA((segments * inner, levels, 2))]
-        weight = AHEAD
-    else:
-        kernel = azimuth_second
-        operands = [table, moved, earlier]
-        in_specs = [vmem] * 3
-        out_shape, out_specs = image, vmem
-        weight = 1
     return pl.pallas_call(
-        functools.partial(kernel, planes),
-        out_shape=out_shape,
-        in_specs=in_specs,
-        out_specs=out_specs,
-        scratch_shapes=scratch,
+        functools.partial(azimuth_kernel, planes),
+        out_shape=jax.ShapeDtypeStruct((2, count, bins), jnp.float32),
+        in_specs=[vmem] * (2 + len(arrived)),
+        out_specs=pl.BlockSpec(memory_space=pltpu.HBM),
+        scratch_shapes=[
+            pltpu.VMEM((2, count, bins), jnp.float32),
+            pltpu.VMEM((2, count, bins), jnp.float32),
+            pltpu.SemaphoreType.DMA((2 * count // BLOCK,)),
+        ],
         compiler_params=pltpu.CompilerParams(vmem_limit_bytes=24 << 20),
         cost_estimate=pl.CostEstimate(
-            flops=weight * 2 * 3 * 4 * count * BLOCK * bins, bytes_accessed=4 * 4 * count * bins, transcendentals=0
+            flops=2 * 3 * 4 * count * BLOCK * bins, bytes_accessed=4 * 4 * count * bins, transcendentals=0
         ),
-        name="azimuth_first" if earlier is None else "azimuth_second",
-    )(*operands)
+        name="azimuth",
+    )(table, moved, *arrived)
+
+
+def table_call(azimuth_ref, count):
+    diagonals = min(azimuth_ref.shape[1] // BLOCK + 1, 2 * (count // BLOCK) - 1)
+    vmem = pl.BlockSpec(memory_space=pltpu.VMEM)
+    return pl.pallas_call(
+        azimuth_tables,
+        out_shape=jax.ShapeDtypeStruct((2, 2, diagonals, BLOCK, BLOCK), jnp.bfloat16),
+        in_specs=[vmem],
+        out_specs=vmem,
+        compiler_params=pltpu.CompilerParams(vmem_limit_bytes=24 << 20),
+        cost_estimate=pl.CostEstimate(flops=AHEAD << 20, bytes_accessed=0, transcendentals=0),
+        name="azimuth_table",
+    )(azimuth_ref)
 
 
 def pairs_of(planes, level_step=0, place_step=0, core_step=0):
@@ -411,12 +420,12 @@
     moved = lax.all_to_all(migrated, AXES, split_axis=0, concat_axis=0, axis_index_groups=groups, tiled=True)
     *received, migrated = lax.optimization_barrier((*received, migrated))
     by_place = regroup_call(received)
+    *by_place, taps_later = lax.optimization_barrier((*by_place, azimuth_ref))
     arrived = [by_place[0]] + [
         lax.ppermute(by_place[q], AXES, pairs_of(planes, place_step=q)) for q in range(1, len(by_place))
     ]
     count = devices_all * echoes.shape[1]
-    image, table = azimuth_call(planes, count, bins, azimuth_ref, arrived)
-    return azimuth_call(planes, count, bins, azimuth_ref, table=table, moved=moved, earlier=image)
+    return azimuth_call(planes, count, table_call(taps_later, count), moved, arrived)
 
 
 def solution(mesh):

time: 41.2 us -> 39.8 us (0.966)
  Pallas kernels: 14.6 us -> 12.2 us
  waiting for transfers between devices: 9.48 us -> 10.4 us
    pallas_call x2, Pallas kernels: 4.22 us -> 2.17 us  [the longest x1 1.96 us: azimuth_call(): pl.pallas_call(functools.partial(azimuth_kernel, planes), out_shape=jax.S...]
    all_to_all x1, waiting for transfers between devices: 0.01 us -> 1.16 us  [per_device(): lax.all_to_all(migrated, AXES, split_axis=0, concat_axis=0, axis_index_gr...]
  transfers between devices with their start and end apart: 10 -> 10, of which waited for: 3 -> 4; matrix products, arithmetic and copies ran while one was open for 0% -> 0% of each run, Pallas kernels for 31% -> 26%
where the time goes in v6:
time: 39.8 us; the launch traced here: 39.6 us
  starting transfers between devices  16.8 us (42%)
  Pallas kernels  12.2 us (31%)
  waiting for transfers between devices  10.4 us (26%)
    ppermute x3, waiting for transfers between devices, per_device(): lax.ppermute(by_place[q], AXES, pairs_of(planes, place_step=q))  9.25 us
    pallas_call x2, Pallas kernels, range_call(): pl.pallas_call(functools.partial(range_kernel, own, planes, lines, blocks...  9.14 us
    all_to_all x1, starting transfers between devices, per_device(): lax.all_to_all(migrated, AXES, split_axis=0, concat_axis=0, axis_index_gr...  7.08 us
    ppermute x3, starting transfers between devices, per_device(): lax.ppermute(by_level[k], AXES, pairs_of(planes, level_step=k))  5.23 us
    ppermute x3, starting transfers between devices, per_device(): lax.ppermute(by_place[q], AXES, pairs_of(planes, place_step=q))  3.55 us
    pallas_call x1, Pallas kernels, azimuth_call(): pl.pallas_call(functools.partial(azimuth_kernel, planes), out_shape=jax.S...  1.96 us
    all_to_all x1, waiting for transfers between devices, per_device(): lax.all_to_all(migrated, AXES, split_axis=0, concat_axis=0, axis_index_gr...  1.16 us
    ppermute x3, starting transfers between devices, per_device(): lax.ppermute(array, AXES, pairs_of(planes, core_step=1))  0.96 us
  transfers between devices with their start and end apart: 10, of which 4 were waited for; matrix products, arithmetic and copies ran while one was open for 0% of the time, Pallas kernels for 26%

profile of v6, /device:TPU:0, one launch (start us, length us, event | category | flops | bytes accessed | tf_op | source)
XLA Modules:
  0.0 39.6 jit_solution(8252220925340791667)
XLA Ops:
  0.0 0.5 %collective-permute-start.5 = (f32[2,8,16384]{2,1,0:T(8,128)}, f32[2,8,16384]{2,1,0:T(8,128)S(1)}, u32[]{:S(2)}, u32[]{:S(2)}) collective-permute-start(f32[2,8,16384]{2,1,0:T(8,128)} %refs_3_.1), channel_id=1, source_target_pairs={{0,8},{1,9},{2,10},{3,11},{4,12},{5,13},{6,14},{7,15},{8,0},{9,1},... | collective-permute-start | bytes 3145736 | tf_op jit(solution)/shard_map/ppermute | solution.py:409
  0.5 0.1 collective-permute-start.3
  0.5 0.5 %collective-permute-start.4 = (f32[8,8]{1,0:T(8,128)}, f32[8,8]{1,0:T(8,128)S(1)}, u32[]{:S(2)}, u32[]{:S(2)}) collective-permute-start(f32[8,8]{1,0:T(8,128)} %refs_2_.1), channel_id=1, source_target_pairs={{0,8},{1,9},{2,10},{3,11},{4,12},{5,13},{6,14},{7,15},{8,0},{9,1},... | collective-permute-start | bytes 776 | tf_op jit(solution)/shard_map/ppermute | solution.py:409
  1.0 4.9 %range_own.1 = (f32[2,2,16,512]{3,2,1,0:T(8,128)S(1)}, f32[2,2,16,512]{3,2,1,0:T(8,128)S(1)}, f32[2,2,16,512]{3,2,1,0:T(8,128)S(1)}, f32[2,2,16,512]{3,2,1,0:T(8,128)S(1)}, bf16[3,2,256,1280]{3,2,1,0:T(8,128)(2,1)S(1)}) custom-call(s32[8]{0:T(128)} %refs_0_.1, f32[2,1024]{1,0:T(2,128)} %refs_1_.1, f32[8,8]{1,0:T(8,128)} %refs_2_.1, f32[2,8,16384]{2,1,0:T(8,128)} %refs_3_.1), custom_call_target="tpu_custom_call" | custom-call | flops 1698693120 | bytes 1572864 | tf_op jit(solution)/shard_map/range_own/pallas_call | solution.py:237
  5.8 2.6 %collective-permute-start = (f32[2,2,16,512]{3,2,1,0:T(8,128)S(1)}, f32[2,2,16,512]{3,2,1,0:T(8,128)S(1)}, u32[]{:S(2)}, u32[]{:S(2)}) collective-permute-start(f32[2,2,16,512]{3,2,1,0:T(8,128)S(1)} %get-tuple-element.24), channel_id=1, source_target_pairs={{0,2},{1,3},{2,0},{3,1},{4,6},{5,7},{6,4},{7,5},{8,10},{9,11},{10,... | collective-permute-start | bytes 393224 | tf_op jit(solution)/shard_map/ppermute | solution.py:413
  8.5 2.6 %collective-permute-start.1 = (f32[2,2,16,512]{3,2,1,0:T(8,128)S(1)}, f32[2,2,16,512]{3,2,1,0:T(8,128)S(1)}, u32[]{:S(2)}, u32[]{:S(2)}) collective-permute-start(f32[2,2,16,512]{3,2,1,0:T(8,128)S(1)} %get-tuple-element.25), channel_id=1, source_target_pairs={{0,4},{1,5},{2,6},{3,7},{4,0},{5,1},{6,2},{7,3},{8,12},{9,13},{10,... | collective-permute-start | bytes 393224 | tf_op jit(solution)/shard_map/ppermute | solution.py:413
  11.1 0.0 collective-permute-done.3.refs_0_
  11.1 0.0 collective-permute-start.2
  11.1 0.0 collective-permute-done.4.refs_2_
  11.1 0.0 collective-permute-done.5.refs_3_
  11.1 0.0 copy-start
  11.1 4.3 %range_partner.1 = f32[16,16,512]{2,1,0:T(8,128)} custom-call(s32[8]{0:T(128)S(1)} %collective-permute-done.3.refs_0_, bf16[3,2,256,1280]{3,2,1,0:T(8,128)(2,1)S(1)} %get-tuple-element.27.refs_1_, f32[8,8]{1,0:T(8,128)S(1)} %collective-permute-done.4.refs_2_, f32[2,8,16384]{2,1,0:T(8,128)S(1)} %collective-permute-done.5.refs_3_), custom_call_target="tpu_custom_call" | custom-call | flops 1698693120 | bytes 1572864 | tf_op jit(solution)/shard_map/range_partner/pallas_call | solution.py:237
  15.4 7.1 %all-to-all-start = ((f32[16,16,512]{2,1,0:T(8,128)}), f32[16,16,512]{2,1,0:T(8,128)S(1)}, u32[]{:S(2)}, u32[]{:S(2)}) async-start(f32[16,16,512]{2,1,0:T(8,128)} %range_partner.1), calls=%async_computation | async-start | bytes 1048576 | tf_op jit(solution)/shard_map/all_to_all | solution.py:420
  22.5 0.0 collective-permute-done.refs_1_
  22.5 0.0 collective-permute-done.1.refs_2_
  22.5 0.0 collective-permute-done.2.refs_3_
  22.5 0.9 %regroup.1 = (f32[4,16,512]{2,1,0:T(8,128)S(1)}, f32[4,16,512]{2,1,0:T(8,128)S(1)}, f32[4,16,512]{2,1,0:T(8,128)S(1)}, f32[4,16,512]{2,1,0:T(8,128)S(1)}) custom-call(f32[2,2,16,512]{3,2,1,0:T(8,128)S(1)} %get-tuple-element.28.refs_0_, f32[2,2,16,512]{3,2,1,0:T(8,128)S(1)} %collective-permute-done.refs_1_, ...), custom_call_target="tpu_custom_call" | custom-call | bytes 1048576 | tf_op jit(solution)/shard_map/regroup/pallas_call | solution.py:272
  23.4 2.0 %collective-permute-start.6 = (f32[4,16,512]{2,1,0:T(8,128)S(1)}, f32[4,16,512]{2,1,0:T(8,128)S(1)}, u32[]{:S(2)}, u32[]{:S(2)}) collective-permute-start(f32[4,16,512]{2,1,0:T(8,128)S(1)} %get-tuple-element.38), channel_id=1, source_target_pairs={{0,1},{1,0},{2,3},{3,2},{4,5},{5,4},{6,7},{7,6},{8,9},{9,8},{10,11... | collective-permute-start | bytes 393224 | tf_op jit(solution)/shard_map/ppermute | solution.py:425
  25.4 1.5 %collective-permute-start.7 = (f32[4,16,512]{2,1,0:T(8,128)S(1)}, f32[4,16,512]{2,1,0:T(8,128)S(1)}, u32[]{:S(2)}, u32[]{:S(2)}) collective-permute-start(f32[4,16,512]{2,1,0:T(8,128)S(1)} %get-tuple-element.39), channel_id=1, source_target_pairs={{0,16},{1,17},{2,18},{3,19},{4,20},{5,21},{6,22},{7,23},{8,24},{9,... | collective-permute-start | bytes 393224 | tf_op jit(solution)/shard_map/ppermute | solution.py:425
  26.9 0.1 collective-permute-start.8
  27.0 0.0 copy-done
  27.0 0.2 azimuth_table.1.refs_0_
  27.2 4.2 %collective-permute-done.6.refs_3_ = f32[4,16,512]{2,1,0:T(8,128)S(1)} collective-permute-done((f32[4,16,512]{2,1,0:T(8,128)S(1)}, f32[4,16,512]{2,1,0:T(8,128)S(1)}, u32[]{:S(2)}, u32[]{:S(2)}) %collective-permute-start.6) | collective-permute-done | bytes 131104 | tf_op jit(solution)/shard_map/ppermute | solution.py:425
  31.4 2.0 %collective-permute-done.7.refs_4_ = f32[4,16,512]{2,1,0:T(8,128)S(1)} collective-permute-done((f32[4,16,512]{2,1,0:T(8,128)S(1)}, f32[4,16,512]{2,1,0:T(8,128)S(1)}, u32[]{:S(2)}, u32[]{:S(2)}) %collective-permute-start.7) | collective-permute-done | bytes 131104 | tf_op jit(solution)/shard_map/ppermute | solution.py:425
  33.3 3.1 %collective-permute-done.8.refs_5_ = f32[4,16,512]{2,1,0:T(8,128)S(1)} collective-permute-done((f32[4,16,512]{2,1,0:T(8,128)S(1)}, f32[4,16,512]{2,1,0:T(8,128)S(1)}, u32[]{:S(2)}, u32[]{:S(2)}) %collective-permute-start.8) | collective-permute-done | bytes 131104 | tf_op jit(solution)/shard_map/ppermute | solution.py:425
  36.4 1.2 %all-to-all-done.refs_1_ = f32[16,16,512]{2,1,0:T(8,128)S(1)} async-done(((f32[16,16,512]{2,1,0:T(8,128)}), f32[16,16,512]{2,1,0:T(8,128)S(1)}, u32[]{:S(2)}, u32[]{:S(2)}) %all-to-all-start) | async-done | bytes 524320 | tf_op jit(solution)/shard_map/all_to_all | solution.py:420
  37.6 2.0 %azimuth.1 = f32[2,256,512]{2,1,0:T(8,128)} custom-call(bf16[2,2,1,256,256]{4,3,2,1,0:T(8,128)(2,1)S(1)} %azimuth_table.1.refs_0_, f32[16,16,512]{2,1,0:T(8,128)S(1)} %all-to-all-done.refs_1_, f32[4,16,512]{2,1,0:T(8,128)S(1)} %get-tuple-element.37.refs_2_, f32[4,16,512]{2,1,0:T(8,128)S(1)} %collective-permute-done.6.refs_3_, ...), custom_call_target="tpu_custom_call" | custom-call | flops 805306368 | bytes 2097152 | tf_op jit(solution)/shard_map/azimuth/pallas_call | solution.py:358
Async XLA Ops:
  0.0 11.1 %collective-permute-start.5 = (f32[2,8,16384]{2,1,0:T(8,128)}, f32[2,8,16384]{2,1,0:T(8,128)S(1)}, u32[]{:S(2)}, u32[]{:S(2)}) collective-permute-start(f32[2,8,16384]{2,1,0:T(8,128)} %refs_3_.1), channel_id=1, source_target_pairs={{0,8},{1,9},{2,10},{3,11},{4,12},{5,13},{6,14},{7,15},{8,0},{9,1},... | collective-permute-start | bytes 3145736 | tf_op jit(solution)/shard_map/ppermute | solution.py:409
  0.5 10.6 %collective-permute-start.3 = (s32[8]{0:T(128)}, s32[8]{0:T(128)S(1)}, u32[]{:S(2)}, u32[]{:S(2)}) collective-permute-start(s32[8]{0:T(128)} %refs_0_.1), channel_id=1, source_target_pairs={{0,8},{1,9},{2,10},{3,11},{4,12},{5,13},{6,14},{7,15},{8,0},{9,1},... | collective-permute-start | bytes 104 | tf_op jit(solution)/shard_map/ppermute | solution.py:409
  0.5 10.6 %collective-permute-start.4 = (f32[8,8]{1,0:T(8,128)}, f32[8,8]{1,0:T(8,128)S(1)}, u32[]{:S(2)}, u32[]{:S(2)}) collective-permute-start(f32[8,8]{1,0:T(8,128)} %refs_2_.1), channel_id=1, source_target_pairs={{0,8},{1,9},{2,10},{3,11},{4,12},{5,13},{6,14},{7,15},{8,0},{9,1},... | collective-permute-start | bytes 776 | tf_op jit(solution)/shard_map/ppermute | solution.py:409
  5.8 16.6 %collective-permute-start = (f32[2,2,16,512]{3,2,1,0:T(8,128)S(1)}, f32[2,2,16,512]{3,2,1,0:T(8,128)S(1)}, u32[]{:S(2)}, u32[]{:S(2)}) collective-permute-start(f32[2,2,16,512]{3,2,1,0:T(8,128)S(1)} %get-tuple-element.24), channel_id=1, source_target_pairs={{0,2},{1,3},{2,0},{3,1},{4,6},{5,7},{6,4},{7,5},{8,10},{9,11},{10,... | collective-permute-start | bytes 393224 | tf_op jit(solution)/shard_map/ppermute | solution.py:413
  8.5 14.0 %collective-permute-start.1 = (f32[2,2,16,512]{3,2,1,0:T(8,128)S(1)}, f32[2,2,16,512]{3,2,1,0:T(8,128)S(1)}, u32[]{:S(2)}, u32[]{:S(2)}) collective-permute-start(f32[2,2,16,512]{3,2,1,0:T(8,128)S(1)} %get-tuple-element.25), channel_id=1, source_target_pairs={{0,4},{1,5},{2,6},{3,7},{4,0},{5,1},{6,2},{7,3},{8,12},{9,13},{10,... | collective-permute-start | bytes 393224 | tf_op jit(solution)/shard_map/ppermute | solution.py:413
  11.1 11.4 %collective-permute-start.2 = (f32[2,2,16,512]{3,2,1,0:T(8,128)S(1)}, f32[2,2,16,512]{3,2,1,0:T(8,128)S(1)}, u32[]{:S(2)}, u32[]{:S(2)}) collective-permute-start(f32[2,2,16,512]{3,2,1,0:T(8,128)S(1)} %get-tuple-element.26), channel_id=1, source_target_pairs={{0,6},{1,7},{2,4},{3,5},{4,2},{5,3},{6,0},{7,1},{8,14},{9,15},{10,... | collective-permute-start | bytes 393224 | tf_op jit(solution)/shard_map/ppermute | solution.py:413
  11.1 15.9 %copy-start = (f32[2,512]{1,0:T(2,128)S(1)}, f32[2,512]{1,0:T(2,128)}, u32[]{:S(2)}) copy-start(f32[2,512]{1,0:T(2,128)} %taps_ref) | copy-start | bytes 12292
  15.4 22.2 %all-to-all-start = ((f32[16,16,512]{2,1,0:T(8,128)}), f32[16,16,512]{2,1,0:T(8,128)S(1)}, u32[]{:S(2)}, u32[]{:S(2)}) async-start(f32[16,16,512]{2,1,0:T(8,128)} %range_partner.1), calls=%async_computation | async-start | bytes 1048576 | tf_op jit(solution)/shard_map/all_to_all | solution.py:420
  23.4 8.0 %collective-permute-start.6 = (f32[4,16,512]{2,1,0:T(8,128)S(1)}, f32[4,16,512]{2,1,0:T(8,128)S(1)}, u32[]{:S(2)}, u32[]{:S(2)}) collective-permute-start(f32[4,16,512]{2,1,0:T(8,128)S(1)} %get-tuple-element.38), channel_id=1, source_target_pairs={{0,1},{1,0},{2,3},{3,2},{4,5},{5,4},{6,7},{7,6},{8,9},{9,8},{10,11... | collective-permute-start | bytes 393224 | tf_op jit(solution)/shard_map/ppermute | solution.py:425
  25.4 7.9 %collective-permute-start.7 = (f32[4,16,512]{2,1,0:T(8,128)S(1)}, f32[4,16,512]{2,1,0:T(8,128)S(1)}, u32[]{:S(2)}, u32[]{:S(2)}) collective-permute-start(f32[4,16,512]{2,1,0:T(8,128)S(1)} %get-tuple-element.39), channel_id=1, source_target_pairs={{0,16},{1,17},{2,18},{3,19},{4,20},{5,21},{6,22},{7,23},{8,24},{9,... | collective-permute-start | bytes 393224 | tf_op jit(solution)/shard_map/ppermute | solution.py:425
  26.9 9.6 %collective-permute-start.8 = (f32[4,16,512]{2,1,0:T(8,128)S(1)}, f32[4,16,512]{2,1,0:T(8,128)S(1)}, u32[]{:S(2)}, u32[]{:S(2)}) collective-permute-start(f32[4,16,512]{2,1,0:T(8,128)S(1)} %get-tuple-element.40), channel_id=1, source_target_pairs={{0,17},{1,16},{2,19},{3,18},{4,21},{5,20},{6,23},{7,22},{8,25},{9,... | collective-permute-start | bytes 393224 | tf_op jit(solution)/shard_map/ppermute | solution.py:425

commit v7 on v6

--- a/solution.py
+++ b/solution.py
@@ -12,7 +12,7 @@
 LANE = 128
 AXES = ("gx", "gy")
 CORES = 2
-LEVELS = 4
+DISTANCES = (0, 2, 3, 1)
 AHEAD = 20000
 
 ROWS_BY_ROWS = (((1,), (1,)), ((), ()))
@@ -32,9 +32,9 @@
 
 def range_kernel(own, planes, lines, blocks, sections, *refs):
     if own:
-        shift_ref, taps_hbm, weights_hbm, echoes_hbm, *outs, table, taps_ref, weights_ref, echoes_ref, even, odd, compressed, sems = refs
+        shift_ref, taps_hbm, weights_hbm, echoes_hbm, *outs, settings, table, taps_ref, weights_ref, echoes_ref, even, odd, compressed, sems = refs
     else:
-        shift_ref, table, weights_ref, echoes_ref, out_ref, even, odd, compressed, ready, sems = refs
+        settings, table, echoes_ref, out_ref, even, odd, compressed, ready, sems = refs
     segments, levels, inner = planes
     core = lax.rem(lax.axis_index("gx"), CORES)
     width = blocks // (CORES * segments)
@@ -55,6 +55,7 @@
         imag = toeplitz(taps_ref[1:2, :], BLOCK, sections * BLOCK)
         for kind, values in enumerate((real, imag, real - imag)):
             table[kind, 0], table[kind, 1] = split(values)
+        settings[...] = settings_of(lines, shift_ref, weights_ref)
         copies[2].wait()
 
     def piece(segment, part, block):
@@ -107,11 +108,11 @@
         compressed[part, low, :] = jnp.where(at_start, 0.0, compressed[part, low, :])
         compressed[part, high, :] = jnp.where(at_end, 0.0, compressed[part, high, :])
 
-    plan = migration_plan(lines, shift_ref, weights_ref)
+    plan = migration_plan(settings[...])
     sends = []
     run = width // levels
     for step in range(levels):
-        level = (lax.axis_index("gy") // inner) ^ step if own else step
+        level = (lax.axis_index("gy") // inner) ^ DISTANCES[step] if own else step
         streams = [(segment, part) for segment in range(segments) for part in range(2)]
 
         def loader(segment, part):
@@ -146,18 +147,27 @@
         send.wait()
 
 
-def migration_plan(lines, shift_ref, weights_ref):
+def settings_of(lines, shift_ref, weights_ref):
     lane = lax.broadcasted_iota(jnp.int32, (lines, LANE), 1)
     row = lax.broadcasted_iota(jnp.int32, (lines, LANE), 0)
-    shift = jnp.zeros((lines, LANE), jnp.int32)
+    settings = jnp.zeros((lines, LANE), jnp.float32)
     for line in range(lines):
-        shift = jnp.where(row == line, shift_ref[line], shift)
+        settings = jnp.where((row == line) & (lane == TAPS), shift_ref[line].astype(jnp.float32), settings)
+    for j in range(TAPS):
+        settings = jnp.where(lane == j, weights_ref[:, j : j + 1], settings)
+    return settings
+
+
+def migration_plan(settings):
+    lines = settings.shape[0]
+    lane = lax.broadcasted_iota(jnp.int32, (lines, LANE), 1)
+    columns = [jnp.broadcast_to(settings[:, j : j + 1], (lines, LANE)) for j in range(TAPS + 1)]
+    shift = columns[TAPS].astype(jnp.int32)
     steps = []
     for step in range(2):
         place = lane + shift - (TAPS // 2 - 1) + step
         steps.append((place & (LANE - 1), place < 0, place >= LANE))
-    weights = [jnp.broadcast_to(weights_ref[:, j : j + 1], (lines, LANE)) for j in range(TAPS)]
-    return steps, weights, lane
+    return steps, columns[:TAPS], lane
 
 
 def migrate(tiles, plan, loads):
@@ -197,7 +207,7 @@
     return totals
 
 
-def range_call(own, echoes, taps, shift_bins, weights, planes):
+def range_call(own, planes, echoes, taps, *settings):
     lines, range_total = echoes.shape[1], echoes.shape[2]
     blocks = range_total // BLOCK
     sections = (taps.shape[1] if own else taps.shape[-1] - BLOCK) // BLOCK + 1
@@ -212,13 +222,15 @@
         pltpu.VMEM((3, 2, segments * span * lines, BLOCK), jnp.bfloat16),
         pltpu.VMEM((2, segments * (width + 2) * lines, BLOCK), jnp.float32),
     ]
-    operands = [shift_bins, taps, weights, echoes]
     if own:
+        shift_bins, weights = settings
+        operands = [shift_bins, taps, weights, echoes]
         operands = [pltpu.with_memory_space_constraint(array, pltpu.HBM) for array in operands]
         in_specs = [pl.BlockSpec(memory_space=pltpu.SMEM), hbm, hbm, hbm]
         out_shape = [jax.ShapeDtypeStruct((segments, inner, 2 * lines, bins), jnp.float32)] * levels
+        out_shape += [jax.ShapeDtypeStruct((lines, LANE), jnp.float32)]
         out_shape += [jax.ShapeDtypeStruct((3, 2, BLOCK, sections * BLOCK), jnp.bfloat16)]
-        out_specs = [vmem] * (levels + 1)
+        out_specs = [vmem] * (levels + 2)
         scratch = [
             pltpu.VMEM(taps.shape, jnp.float32),
             pltpu.VMEM(weights.shape, jnp.float32),
@@ -227,7 +239,8 @@
             pltpu.SemaphoreType.DMA((3,)),
         ]
     else:
-        in_specs = [pl.BlockSpec(memory_space=pltpu.SMEM), vmem, vmem, vmem]
+        operands = [*settings, taps, echoes]
+        in_specs = [vmem] * 3
         out_shape = jax.ShapeDtypeStruct((segments * levels * inner, 2 * lines, bins), jnp.float32)
         out_specs = hbm
         scratch += [
@@ -333,7 +346,7 @@
     for q, source in enumerate(arrived):
         place = mine ^ q
         for k in range(levels):
-            device = (((place // inner) * CORES + core) * levels + (level ^ k)) * inner + lax.rem(place, inner)
+            device = (((place // inner) * CORES + core) * levels + (level ^ DISTANCES[k])) * inner + lax.rem(place, inner)
             rows = pl.ds(pl.multiple_of(device * lines, lines), lines)
             for part in range(2):
                 lines_ref[part, rows, :] = source[k, part * lines : (part + 1) * lines, :]
@@ -401,18 +414,18 @@
 
 def per_device(echoes, range_ref, azimuth_ref, shift_bins, interp_weights):
     outer, run = lax.axis_size("gx"), lax.axis_size("gy")
-    segments, levels = outer // CORES, LEVELS
+    segments, levels = outer // CORES, len(DISTANCES)
     planes = (segments, levels, run // levels)
     devices_all = outer * run
     bins = echoes.shape[2] // devices_all
-    partner = [
-        lax.ppermute(array, AXES, pairs_of(planes, core_step=1)) for array in (echoes, shift_bins, interp_weights)
+    echoes_partner = lax.ppermute(echoes, AXES, pairs_of(planes, core_step=1))
+    *by_level, settings, table = range_call(True, planes, echoes, range_ref, shift_bins, interp_weights)
+    received = [by_level[0]] + [
+        lax.ppermute(array, AXES, pairs_of(planes, level_step=distance))
+        for distance, array in zip(DISTANCES[1:], by_level[1:])
     ]
-    *by_level, table = range_call(True, echoes, range_ref, shift_bins, interp_weights, planes)
-    received = [by_level[0]] + [
-        lax.ppermute(by_level[k], AXES, pairs_of(planes, level_step=k)) for k in range(1, levels)
-    ]
-    migrated = range_call(False, partner[0], table, partner[1], partner[2], planes)
+    settings_partner = lax.ppermute(settings, AXES, pairs_of(planes, core_step=1))
+    migrated = range_call(False, planes, echoes_partner, table, settings_partner)
     groups = [
         [(segment * CORES + core) * run + at for segment in range(segments) for at in range(run)]
         for core in range(CORES)

time: 39.8 us -> 38 us (0.955)
  starting transfers between devices: 16.8 us -> 15.9 us
  Pallas kernels: 12.2 us -> 11.7 us
  waiting for transfers between devices: 10.4 us -> 10 us
    all_to_all x1, starting transfers between devices: 7.08 us -> 6.2 us  [per_device(): lax.all_to_all(migrated, AXES, split_axis=0, concat_axis=0, axis_index_gr...]
    pallas_call x2, Pallas kernels: 9.14 us -> 8.67 us  [range_call(): pl.pallas_call(functools.partial(range_kernel, own, planes, lines, blocks...]
    ppermute x3, waiting for transfers between devices: 9.25 us -> 8.85 us  [per_device(): lax.ppermute(by_place[q], AXES, pairs_of(planes, place_step=q))]
    ppermute x6 -> x5, starting transfers between devices: 6.19 us -> 6.19 us  [the longest x3 5.61 us: per_device(): lax.ppermute(array, AXES, pairs_of(planes, level_step=distance))]
  transfers between devices with their start and end apart: 10 -> 9, of which waited for: 4 -> 4; matrix products, arithmetic and copies ran while one was open for 0% -> 0% of each run, Pallas kernels for 26% -> 26%
where the time goes in v7:
time: 38 us; the launch traced here: 37.7 us
  starting transfers between devices  15.9 us (42%)
  Pallas kernels  11.7 us (31%)
  waiting for transfers between devices  10 us (26%)
    ppermute x3, waiting for transfers between devices, per_device(): lax.ppermute(by_place[q], AXES, pairs_of(planes, place_step=q))  8.85 us
    pallas_call x2, Pallas kernels, range_call(): pl.pallas_call(functools.partial(range_kernel, own, planes, lines, blocks...  8.67 us
    all_to_all x1, starting transfers between devices, per_device(): lax.all_to_all(migrated, AXES, split_axis=0, concat_axis=0, axis_index_gr...  6.2 us
    ppermute x3, starting transfers between devices, per_device(): lax.ppermute(array, AXES, pairs_of(planes, level_step=distance))  5.61 us
    ppermute x3, starting transfers between devices, per_device(): lax.ppermute(by_place[q], AXES, pairs_of(planes, place_step=q))  3.55 us
    pallas_call x1, Pallas kernels, azimuth_call(): pl.pallas_call(functools.partial(azimuth_kernel, planes), out_shape=jax.S...  1.96 us
    all_to_all x1, waiting for transfers between devices, per_device(): lax.all_to_all(migrated, AXES, split_axis=0, concat_axis=0, axis_index_gr...  1.14 us
    pallas_call x1, Pallas kernels, regroup_call(): pl.pallas_call(functools.partial(regroup_kernel, levels, plane), out_shap...  0.9 us
  transfers between devices with their start and end apart: 9, of which 4 were waited for; matrix products, arithmetic and copies ran while one was open for 0% of the time, Pallas kernels for 26%

profile of v7, /device:TPU:0, one launch (start us, length us, event | category | flops | bytes accessed | tf_op | source)
XLA Modules:
  0.0 37.7 jit_solution(6308356311634127949)
XLA Ops:
  0.0 0.5 %collective-permute-start.4 = (f32[2,8,16384]{2,1,0:T(8,128)}, f32[2,8,16384]{2,1,0:T(8,128)S(1)}, u32[]{:S(2)}, u32[]{:S(2)}) collective-permute-start(f32[2,8,16384]{2,1,0:T(8,128)} %refs_3_.1), channel_id=1, source_target_pairs={{0,8},{1,9},{2,10},{3,11},{4,12},{5,13},{6,14},{7,15},{8,0},{9,1},... | collective-permute-start | bytes 3145736 | tf_op jit(solution)/shard_map/ppermute | solution.py:421
  0.5 4.9 %range_own.1 = (f32[2,2,16,512]{3,2,1,0:T(8,128)S(1)}, f32[2,2,16,512]{3,2,1,0:T(8,128)S(1)}, f32[2,2,16,512]{3,2,1,0:T(8,128)S(1)}, f32[2,2,16,512]{3,2,1,0:T(8...) custom-call(s32[8]{0:T(128)} %refs_0_.1, f32[2,1024]{1,0:T(2,128)} %refs_1_.1, f32[8,8]{1,0:T(8,128)} %refs_2_.1, ...), custom_call_target="tpu_custom_call" | custom-call | flops 1698693120 | bytes 1572864 | tf_op jit(solution)/shard_map/range_own/pallas_call | solution.py:250
  5.4 0.1 collective-permute-start.3
  5.5 4.0 %collective-permute-start = (f32[2,2,16,512]{3,2,1,0:T(8,128)S(1)}, f32[2,2,16,512]{3,2,1,0:T(8,128)S(1)}, u32[]{:S(2)}, u32[]{:S(2)}) collective-permute-start(f32[2,2,16,512]{3,2,1,0:T(8,128)S(1)} %get-tuple-element.25), channel_id=1, source_target_pairs={{0,4},{1,5},{2,6},{3,7},{4,0},{5,1},{6,2},{7,3},{8,12},{9,13},{10,... | collective-permute-start | bytes 393224 | tf_op jit(solution)/shard_map/ppermute | solution.py:424
  9.5 1.3 %collective-permute-start.1 = (f32[2,2,16,512]{3,2,1,0:T(8,128)S(1)}, f32[2,2,16,512]{3,2,1,0:T(8,128)S(1)}, u32[]{:S(2)}, u32[]{:S(2)}) collective-permute-start(f32[2,2,16,512]{3,2,1,0:T(8,128)S(1)} %get-tuple-element.26), channel_id=1, source_target_pairs={{0,6},{1,7},{2,4},{3,5},{4,2},{5,3},{6,0},{7,1},{8,14},{9,15},{10,... | collective-permute-start | bytes 393224 | tf_op jit(solution)/shard_map/ppermute | solution.py:424
  10.9 0.2 collective-permute-start.2
  11.1 0.0 collective-permute-done.3.refs_0_
  11.1 0.0 collective-permute-done.4.refs_2_
  11.1 0.0 copy-start
  11.1 3.8 %range_partner.1 = f32[16,16,512]{2,1,0:T(8,128)} custom-call(f32[8,128]{1,0:T(8,128)S(1)} %collective-permute-done.3.refs_0_, bf16[3,2,256,1280]{3,2,1,0:T(8,128)(2,1)S(1)} %get-tuple-element.29.refs_1_, f32[2,8,16384]{2,1,0:T(8,128)S(1)} %collective-permute-done.4.refs_2_), custom_call_target="tpu_custom_call" | custom-call | flops 1698693120 | bytes 1572864 | tf_op jit(solution)/shard_map/range_partner/pallas_call | solution.py:250
  14.9 6.2 %all-to-all-start = ((f32[16,16,512]{2,1,0:T(8,128)}), f32[16,16,512]{2,1,0:T(8,128)S(1)}, u32[]{:S(2)}, u32[]{:S(2)}) async-start(f32[16,16,512]{2,1,0:T(8,128)} %range_partner.1), calls=%async_computation | async-start | bytes 1048576 | tf_op jit(solution)/shard_map/all_to_all | solution.py:433
  21.1 0.0 collective-permute-done.refs_1_
  21.1 0.0 collective-permute-done.1.refs_2_
  21.1 0.0 collective-permute-done.2.refs_3_
  21.1 0.9 %regroup.1 = (f32[4,16,512]{2,1,0:T(8,128)S(1)}, f32[4,16,512]{2,1,0:T(8,128)S(1)}, f32[4,16,512]{2,1,0:T(8,128)S(1)}, f32[4,16,512]{2,1,0:T(8,128)S(1)}) custom-call(f32[2,2,16,512]{3,2,1,0:T(8,128)S(1)} %get-tuple-element.30.refs_0_, f32[2,2,16,512]{3,2,1,0:T(8,128)S(1)} %collective-permute-done.refs_1_, ...), custom_call_target="tpu_custom_call" | custom-call | bytes 1048576 | tf_op jit(solution)/shard_map/regroup/pallas_call | solution.py:285
  22.0 2.0 %collective-permute-start.5 = (f32[4,16,512]{2,1,0:T(8,128)S(1)}, f32[4,16,512]{2,1,0:T(8,128)S(1)}, u32[]{:S(2)}, u32[]{:S(2)}) collective-permute-start(f32[4,16,512]{2,1,0:T(8,128)S(1)} %get-tuple-element.40), channel_id=1, source_target_pairs={{0,1},{1,0},{2,3},{3,2},{4,5},{5,4},{6,7},{7,6},{8,9},{9,8},{10,11... | collective-permute-start | bytes 393224 | tf_op jit(solution)/shard_map/ppermute | solution.py:438
  24.0 1.5 %collective-permute-start.6 = (f32[4,16,512]{2,1,0:T(8,128)S(1)}, f32[4,16,512]{2,1,0:T(8,128)S(1)}, u32[]{:S(2)}, u32[]{:S(2)}) collective-permute-start(f32[4,16,512]{2,1,0:T(8,128)S(1)} %get-tuple-element.41), channel_id=1, source_target_pairs={{0,16},{1,17},{2,18},{3,19},{4,20},{5,21},{6,22},{7,23},{8,24},{9,... | collective-permute-start | bytes 393224 | tf_op jit(solution)/shard_map/ppermute | solution.py:438
  25.5 0.1 collective-permute-start.7
  25.6 0.0 copy-done
  25.6 0.2 azimuth_table.1.refs_0_
  25.8 4.3 %collective-permute-done.5.refs_3_ = f32[4,16,512]{2,1,0:T(8,128)S(1)} collective-permute-done((f32[4,16,512]{2,1,0:T(8,128)S(1)}, f32[4,16,512]{2,1,0:T(8,128)S(1)}, u32[]{:S(2)}, u32[]{:S(2)}) %collective-permute-start.5) | collective-permute-done | bytes 131104 | tf_op jit(solution)/shard_map/ppermute | solution.py:438
  30.1 1.1 %collective-permute-done.6.refs_4_ = f32[4,16,512]{2,1,0:T(8,128)S(1)} collective-permute-done((f32[4,16,512]{2,1,0:T(8,128)S(1)}, f32[4,16,512]{2,1,0:T(8,128)S(1)}, u32[]{:S(2)}, u32[]{:S(2)}) %collective-permute-start.6) | collective-permute-done | bytes 131104 | tf_op jit(solution)/shard_map/ppermute | solution.py:438
  31.2 3.4 %collective-permute-done.7.refs_5_ = f32[4,16,512]{2,1,0:T(8,128)S(1)} collective-permute-done((f32[4,16,512]{2,1,0:T(8,128)S(1)}, f32[4,16,512]{2,1,0:T(8,128)S(1)}, u32[]{:S(2)}, u32[]{:S(2)}) %collective-permute-start.7) | collective-permute-done | bytes 131104 | tf_op jit(solution)/shard_map/ppermute | solution.py:438
  34.6 1.1 %all-to-all-done.refs_1_ = f32[16,16,512]{2,1,0:T(8,128)S(1)} async-done(((f32[16,16,512]{2,1,0:T(8,128)}), f32[16,16,512]{2,1,0:T(8,128)S(1)}, u32[]{:S(2)}, u32[]{:S(2)}) %all-to-all-start) | async-done | bytes 524320 | tf_op jit(solution)/shard_map/all_to_all | solution.py:433
  35.8 2.0 %azimuth.1 = f32[2,256,512]{2,1,0:T(8,128)} custom-call(bf16[2,2,1,256,256]{4,3,2,1,0:T(8,128)(2,1)S(1)} %azimuth_table.1.refs_0_, f32[16,16,512]{2,1,0:T(8,128)S(1)} %all-to-all-done.refs_1_, f32[4,16,512]{2,1,0:T(8,128)S(1)} %get-tuple-element.39.refs_2_, f32[4,16,512]{2,1,0:T(8,128)S(1)} %collective-permute-done.5.refs_3_, ...), custom_call_target="tpu_custom_call" | custom-call | flops 805306368 | bytes 2097152 | tf_op jit(solution)/shard_map/azimuth/pallas_call | solution.py:371
Async XLA Ops:
  0.0 11.1 %collective-permute-start.4 = (f32[2,8,16384]{2,1,0:T(8,128)}, f32[2,8,16384]{2,1,0:T(8,128)S(1)}, u32[]{:S(2)}, u32[]{:S(2)}) collective-permute-start(f32[2,8,16384]{2,1,0:T(8,128)} %refs_3_.1), channel_id=1, source_target_pairs={{0,8},{1,9},{2,10},{3,11},{4,12},{5,13},{6,14},{7,15},{8,0},{9,1},... | collective-permute-start | bytes 3145736 | tf_op jit(solution)/shard_map/ppermute | solution.py:421
  5.4 5.7 %collective-permute-start.3 = (f32[8,128]{1,0:T(8,128)S(1)}, f32[8,128]{1,0:T(8,128)S(1)}, u32[]{:S(2)}, u32[]{:S(2)}) collective-permute-start(f32[8,128]{1,0:T(8,128)S(1)} %get-tuple-element.28), channel_id=1, source_target_pairs={{0,8},{1,9},{2,10},{3,11},{4,12},{5,13},{6,14},{7,15},{8,0},{9,1},... | collective-permute-start | bytes 12296 | tf_op jit(solution)/shard_map/ppermute | solution.py:427
  5.5 15.6 %collective-permute-start = (f32[2,2,16,512]{3,2,1,0:T(8,128)S(1)}, f32[2,2,16,512]{3,2,1,0:T(8,128)S(1)}, u32[]{:S(2)}, u32[]{:S(2)}) collective-permute-start(f32[2,2,16,512]{3,2,1,0:T(8,128)S(1)} %get-tuple-element.25), channel_id=1, source_target_pairs={{0,4},{1,5},{2,6},{3,7},{4,0},{5,1},{6,2},{7,3},{8,12},{9,13},{10,... | collective-permute-start | bytes 393224 | tf_op jit(solution)/shard_map/ppermute | solution.py:424
  9.5 11.6 %collective-permute-start.1 = (f32[2,2,16,512]{3,2,1,0:T(8,128)S(1)}, f32[2,2,16,512]{3,2,1,0:T(8,128)S(1)}, u32[]{:S(2)}, u32[]{:S(2)}) collective-permute-start(f32[2,2,16,512]{3,2,1,0:T(8,128)S(1)} %get-tuple-element.26), channel_id=1, source_target_pairs={{0,6},{1,7},{2,4},{3,5},{4,2},{5,3},{6,0},{7,1},{8,14},{9,15},{10,... | collective-permute-start | bytes 393224 | tf_op jit(solution)/shard_map/ppermute | solution.py:424
  10.9 10.2 %collective-permute-start.2 = (f32[2,2,16,512]{3,2,1,0:T(8,128)S(1)}, f32[2,2,16,512]{3,2,1,0:T(8,128)S(1)}, u32[]{:S(2)}, u32[]{:S(2)}) collective-permute-start(f32[2,2,16,512]{3,2,1,0:T(8,128)S(1)} %get-tuple-element.27), channel_id=1, source_target_pairs={{0,2},{1,3},{2,0},{3,1},{4,6},{5,7},{6,4},{7,5},{8,10},{9,11},{10,... | collective-permute-start | bytes 393224 | tf_op jit(solution)/shard_map/ppermute | solution.py:424
  11.1 14.5 %copy-start = (f32[2,512]{1,0:T(2,128)S(1)}, f32[2,512]{1,0:T(2,128)}, u32[]{:S(2)}) copy-start(f32[2,512]{1,0:T(2,128)} %taps_ref) | copy-start | bytes 12292
  14.9 20.9 %all-to-all-start = ((f32[16,16,512]{2,1,0:T(8,128)}), f32[16,16,512]{2,1,0:T(8,128)S(1)}, u32[]{:S(2)}, u32[]{:S(2)}) async-start(f32[16,16,512]{2,1,0:T(8,128)} %range_partner.1), calls=%async_computation | async-start | bytes 1048576 | tf_op jit(solution)/shard_map/all_to_all | solution.py:433
  22.0 8.1 %collective-permute-start.5 = (f32[4,16,512]{2,1,0:T(8,128)S(1)}, f32[4,16,512]{2,1,0:T(8,128)S(1)}, u32[]{:S(2)}, u32[]{:S(2)}) collective-permute-start(f32[4,16,512]{2,1,0:T(8,128)S(1)} %get-tuple-element.40), channel_id=1, source_target_pairs={{0,1},{1,0},{2,3},{3,2},{4,5},{5,4},{6,7},{7,6},{8,9},{9,8},{10,11... | collective-permute-start | bytes 393224 | tf_op jit(solution)/shard_map/ppermute | solution.py:438
  24.0 7.2 %collective-permute-start.6 = (f32[4,16,512]{2,1,0:T(8,128)S(1)}, f32[4,16,512]{2,1,0:T(8,128)S(1)}, u32[]{:S(2)}, u32[]{:S(2)}) collective-permute-start(f32[4,16,512]{2,1,0:T(8,128)S(1)} %get-tuple-element.41), channel_id=1, source_target_pairs={{0,16},{1,17},{2,18},{3,19},{4,20},{5,21},{6,22},{7,23},{8,24},{9,... | collective-permute-start | bytes 393224 | tf_op jit(solution)/shard_map/ppermute | solution.py:438
  25.5 9.2 %collective-permute-start.7 = (f32[4,16,512]{2,1,0:T(8,128)S(1)}, f32[4,16,512]{2,1,0:T(8,128)S(1)}, u32[]{:S(2)}, u32[]{:S(2)}) collective-permute-start(f32[4,16,512]{2,1,0:T(8,128)S(1)} %get-tuple-element.42), channel_id=1, source_target_pairs={{0,17},{1,16},{2,19},{3,18},{4,21},{5,20},{6,23},{7,22},{8,25},{9,... | collective-permute-start | bytes 393224 | tf_op jit(solution)/shard_map/ppermute | solution.py:438

commit v8 on v7

--- a/solution.py
+++ b/solution.py
@@ -260,18 +260,13 @@
 
 
 def regroup_kernel(levels, plane, *refs):
-    sources, outs, sems = refs[:levels], refs[levels:-1], refs[-1]
+    sources, outs = refs[:levels], refs[levels:]
     inner = sources[0].shape[1]
     mine = place_here(inner)
-    copies = []
     for q in range(plane):
         place = mine ^ q
         for k in range(levels):
-            source = sources[k].at[place // inner, lax.rem(place, inner)]
-            copies.append(pltpu.make_async_copy(source, outs[q].at[k], sems.at[q, k]))
-            copies[-1].start()
-    for copy in copies:
-        copy.wait()
+            outs[q][k] = sources[k][place // inner, lax.rem(place, inner)]
 
 
 def place_here(inner):
@@ -285,9 +280,8 @@
     return pl.pallas_call(
         functools.partial(regroup_kernel, levels, plane),
         out_shape=[jax.ShapeDtypeStruct((levels, rows, bins), jnp.float32)] * plane,
-        in_specs=[pl.BlockSpec(memory_space=pl.ANY)] * levels,
-        out_specs=[pl.BlockSpec(memory_space=pltpu.HBM)] * plane,
-        scratch_shapes=[pltpu.SemaphoreType.DMA((plane, levels))],
+        in_specs=[pl.BlockSpec(memory_space=pltpu.VMEM)] * levels,
+        out_specs=[pl.BlockSpec(memory_space=pltpu.VMEM)] * plane,
         compiler_params=pltpu.CompilerParams(vmem_limit_bytes=8 << 20),
         cost_estimate=pl.CostEstimate(flops=0, bytes_accessed=8 * levels * plane * rows * bins, transcendentals=0),
         name="regroup",
@@ -299,31 +293,35 @@
     diagonals = table.shape[2]
     first = (length // BLOCK + 1 - diagonals) // 2
     zeros = jnp.zeros((1, BLOCK), jnp.float32)
+    width = (diagonals + 1) * BLOCK
+    full = []
     for part in range(2):
         row = jnp.concatenate([zeros, taps_ref[part : part + 1, :], zeros], axis=1)
-        width = (diagonals + 1) * BLOCK
-        full = toeplitz(row[:, first * BLOCK : first * BLOCK + width], BLOCK, width)
+        full.append(toeplitz(row[:, first * BLOCK : first * BLOCK + width], BLOCK, width))
+    for kind, values in enumerate((full[0], full[1], full[0] - full[1])):
         for n in range(diagonals):
             at = (n + 1) * BLOCK
-            table[part, 0, n], table[part, 1, n] = split(full[:, at : at + BLOCK])
+            table[kind, 0, n], table[kind, 1, n] = split(values[:, at : at + BLOCK])
 
 
 def azimuth_sums(table, lines_ref):
     diagonals = table.shape[2]
     middle = diagonals // 2
     blocks = lines_ref.shape[1] // BLOCK
-    pieces = [
-        [split(lines_ref[part, b * BLOCK : (b + 1) * BLOCK, :]) for b in range(blocks)] for part in range(2)
-    ]
-
-    def product(b, taps, part):
+    pieces = [[], [], []]
+    for b in range(blocks):
+        real, imag = [lines_ref[part, b * BLOCK : (b + 1) * BLOCK, :] for part in range(2)]
+        for kind, values in enumerate((real, imag, real + imag)):
+            pieces[kind].append(split(values))
+
+    def product(b, kind):
         sums = None
         for diagonal in range(diagonals):
             other = b + diagonal - middle
             if not 0 <= other < blocks:
                 continue
-            m_high, m_low = pieces[part][other]
-            t_high, t_low = table[taps, 0, diagonal], table[taps, 1, diagonal]
+            m_high, m_low = pieces[kind][other]
+            t_high, t_low = table[kind, 0, diagonal], table[kind, 1, diagonal]
             for left, right in ((t_high, m_high), (t_high, m_low), (t_low, m_high)):
                 term = lax.dot_general(left, right, PLAIN, preferred_element_type=jnp.float32)
                 sums = term if sums is None else sums + term
@@ -331,8 +329,9 @@
 
     for b in range(blocks):
         at = slice(b * BLOCK, (b + 1) * BLOCK)
-        yield 0, at, product(b, 0, 0) + product(b, 1, 1)
-        yield 1, at, product(b, 0, 1) - product(b, 1, 0)
+        first, second = product(b, 0), product(b, 1)
+        yield 0, at, first + second
+        yield 1, at, product(b, 2) - first + second
 
 
 def azimuth_kernel(planes, *refs):
@@ -391,7 +390,7 @@
     vmem = pl.BlockSpec(memory_space=pltpu.VMEM)
     return pl.pallas_call(
         azimuth_tables,
-        out_shape=jax.ShapeDtypeStruct((2, 2, diagonals, BLOCK, BLOCK), jnp.bfloat16),
+        out_shape=jax.ShapeDtypeStruct((3, 2, diagonals, BLOCK, BLOCK), jnp.bfloat16),
         in_specs=[vmem],
         out_specs=vmem,
         compiler_params=pltpu.CompilerParams(vmem_limit_bytes=24 << 20),

time: 38 us -> 37.8 us (level)
  Pallas kernels: 11.7 us -> 10.7 us
  waiting for transfers between devices: 10 us -> 10.8 us
    pallas_call x1, Pallas kernels: 0.9 us -> 0.06 us  [regroup_call(): pl.pallas_call(functools.partial(regroup_kernel, levels, plane), out_shap...]
    ppermute x3, waiting for transfers between devices: 8.85 us -> 9.47 us  [per_device(): lax.ppermute(by_place[q], AXES, pairs_of(planes, place_step=q))]
  transfers between devices with their start and end apart: 9 -> 9, of which waited for: 4 -> 4; matrix products, arithmetic and copies ran while one was open for 0% -> 0% of each run, Pallas kernels for 26% -> 24%
where the time goes in v8:
time: 37.8 us; the launch traced here: 37.6 us
  starting transfers between devices  15.9 us (42%)
  waiting for transfers between devices  10.8 us (29%)
  Pallas kernels  10.7 us (28%)
    ppermute x3, waiting for transfers between devices, per_device(): lax.ppermute(by_place[q], AXES, pairs_of(planes, place_step=q))  9.47 us
    pallas_call x2, Pallas kernels, range_call(): pl.pallas_call(functools.partial(range_kernel, own, planes, lines, blocks...  8.67 us
    all_to_all x1, starting transfers between devices, per_device(): lax.all_to_all(migrated, AXES, split_axis=0, concat_axis=0, axis_index_gr...  6.2 us
    ppermute x3, starting transfers between devices, per_device(): lax.ppermute(array, AXES, pairs_of(planes, level_step=distance))  5.61 us
    ppermute x3, starting transfers between devices, per_device(): lax.ppermute(by_place[q], AXES, pairs_of(planes, place_step=q))  3.55 us
    pallas_call x1, Pallas kernels, azimuth_call(): pl.pallas_call(functools.partial(azimuth_kernel, planes), out_shape=jax.S...  1.77 us
    all_to_all x1, waiting for transfers between devices, per_device(): lax.all_to_all(migrated, AXES, split_axis=0, concat_axis=0, axis_index_gr...  1.33 us
  transfers between devices with their start and end apart: 9, of which 4 were waited for; matrix products, arithmetic and copies ran while one was open for 0% of the time, Pallas kernels for 24%

profile of v8, /device:TPU:0, one launch (start us, length us, event | category | flops | bytes accessed | tf_op | source)
XLA Modules:
  0.0 37.6 jit_solution(5465682904938676001)
XLA Ops:
  0.0 0.5 %collective-permute-start.4 = (f32[2,8,16384]{2,1,0:T(8,128)}, f32[2,8,16384]{2,1,0:T(8,128)S(1)}, u32[]{:S(2)}, u32[]{:S(2)}) collective-permute-start(f32[2,8,16384]{2,1,0:T(8,128)} %refs_3_.1), channel_id=1, source_target_pairs={{0,8},{1,9},{2,10},{3,11},{4,12},{5,13},{6,14},{7,15},{8,0},{9,1},... | collective-permute-start | bytes 3145736 | tf_op jit(solution)/shard_map/ppermute | solution.py:420
  0.5 4.9 %range_own.1 = (f32[2,2,16,512]{3,2,1,0:T(8,128)S(1)}, f32[2,2,16,512]{3,2,1,0:T(8,128)S(1)}, f32[2,2,16,512]{3,2,1,0:T(8,128)S(1)}, f32[2,2,16,512]{3,2,1,0:T(8...) custom-call(s32[8]{0:T(128)} %refs_0_.1, f32[2,1024]{1,0:T(2,128)} %refs_1_.1, f32[8,8]{1,0:T(8,128)} %refs_2_.1, ...), custom_call_target="tpu_custom_call" | custom-call | flops 1698693120 | bytes 1572864 | tf_op jit(solution)/shard_map/range_own/pallas_call | solution.py:250
  5.4 0.1 collective-permute-start.3
  5.5 4.0 %collective-permute-start = (f32[2,2,16,512]{3,2,1,0:T(8,128)S(1)}, f32[2,2,16,512]{3,2,1,0:T(8,128)S(1)}, u32[]{:S(2)}, u32[]{:S(2)}) collective-permute-start(f32[2,2,16,512]{3,2,1,0:T(8,128)S(1)} %get-tuple-element.25), channel_id=1, source_target_pairs={{0,4},{1,5},{2,6},{3,7},{4,0},{5,1},{6,2},{7,3},{8,12},{9,13},{10,... | collective-permute-start | bytes 393224 | tf_op jit(solution)/shard_map/ppermute | solution.py:423
  9.5 1.3 %collective-permute-start.1 = (f32[2,2,16,512]{3,2,1,0:T(8,128)S(1)}, f32[2,2,16,512]{3,2,1,0:T(8,128)S(1)}, u32[]{:S(2)}, u32[]{:S(2)}) collective-permute-start(f32[2,2,16,512]{3,2,1,0:T(8,128)S(1)} %get-tuple-element.26), channel_id=1, source_target_pairs={{0,6},{1,7},{2,4},{3,5},{4,2},{5,3},{6,0},{7,1},{8,14},{9,15},{10,... | collective-permute-start | bytes 393224 | tf_op jit(solution)/shard_map/ppermute | solution.py:423
  10.9 0.2 collective-permute-start.2
  11.1 0.0 collective-permute-done.3.refs_0_
  11.1 0.0 collective-permute-done.4.refs_2_
  11.1 0.0 copy-start
  11.1 3.8 %range_partner.1 = f32[16,16,512]{2,1,0:T(8,128)} custom-call(f32[8,128]{1,0:T(8,128)S(1)} %collective-permute-done.3.refs_0_, bf16[3,2,256,1280]{3,2,1,0:T(8,128)(2,1)S(1)} %get-tuple-element.29.refs_1_, f32[2,8,16384]{2,1,0:T(8,128)S(1)} %collective-permute-done.4.refs_2_), custom_call_target="tpu_custom_call" | custom-call | flops 1698693120 | bytes 1572864 | tf_op jit(solution)/shard_map/range_partner/pallas_call | solution.py:250
  14.9 6.2 %all-to-all-start = ((f32[16,16,512]{2,1,0:T(8,128)}), f32[16,16,512]{2,1,0:T(8,128)S(1)}, u32[]{:S(2)}, u32[]{:S(2)}) async-start(f32[16,16,512]{2,1,0:T(8,128)} %range_partner.1), calls=%async_computation | async-start | bytes 1048576 | tf_op jit(solution)/shard_map/all_to_all | solution.py:432
  21.1 0.0 collective-permute-done.refs_1_
  21.1 0.0 collective-permute-done.1.refs_2_
  21.1 0.0 collective-permute-done.2.refs_3_
  21.1 0.1 regroup.1
  21.2 2.0 %collective-permute-start.5 = (f32[4,16,512]{2,1,0:T(8,128)S(1)}, f32[4,16,512]{2,1,0:T(8,128)S(1)}, u32[]{:S(2)}, u32[]{:S(2)}) collective-permute-start(f32[4,16,512]{2,1,0:T(8,128)S(1)} %get-tuple-element.40), channel_id=1, source_target_pairs={{0,1},{1,0},{2,3},{3,2},{4,5},{5,4},{6,7},{7,6},{8,9},{9,8},{10,11... | collective-permute-start | bytes 393224 | tf_op jit(solution)/shard_map/ppermute | solution.py:437
  23.2 1.5 %collective-permute-start.6 = (f32[4,16,512]{2,1,0:T(8,128)S(1)}, f32[4,16,512]{2,1,0:T(8,128)S(1)}, u32[]{:S(2)}, u32[]{:S(2)}) collective-permute-start(f32[4,16,512]{2,1,0:T(8,128)S(1)} %get-tuple-element.41), channel_id=1, source_target_pairs={{0,16},{1,17},{2,18},{3,19},{4,20},{5,21},{6,22},{7,23},{8,24},{9,... | collective-permute-start | bytes 393224 | tf_op jit(solution)/shard_map/ppermute | solution.py:437
  24.6 0.1 collective-permute-start.7
  24.7 0.0 copy-done
  24.8 0.2 azimuth_table.1.refs_0_
  25.0 3.4 %collective-permute-done.5.refs_3_ = f32[4,16,512]{2,1,0:T(8,128)S(1)} collective-permute-done((f32[4,16,512]{2,1,0:T(8,128)S(1)}, f32[4,16,512]{2,1,0:T(8,128)S(1)}, u32[]{:S(2)}, u32[]{:S(2)}) %collective-permute-start.5) | collective-permute-done | bytes 131104 | tf_op jit(solution)/shard_map/ppermute | solution.py:437
  28.3 2.8 %collective-permute-done.6.refs_4_ = f32[4,16,512]{2,1,0:T(8,128)S(1)} collective-permute-done((f32[4,16,512]{2,1,0:T(8,128)S(1)}, f32[4,16,512]{2,1,0:T(8,128)S(1)}, u32[]{:S(2)}, u32[]{:S(2)}) %collective-permute-start.6) | collective-permute-done | bytes 131104 | tf_op jit(solution)/shard_map/ppermute | solution.py:437
  31.2 3.3 %collective-permute-done.7.refs_5_ = f32[4,16,512]{2,1,0:T(8,128)S(1)} collective-permute-done((f32[4,16,512]{2,1,0:T(8,128)S(1)}, f32[4,16,512]{2,1,0:T(8,128)S(1)}, u32[]{:S(2)}, u32[]{:S(2)}) %collective-permute-start.7) | collective-permute-done | bytes 131104 | tf_op jit(solution)/shard_map/ppermute | solution.py:437
  34.5 1.3 %all-to-all-done.refs_1_ = f32[16,16,512]{2,1,0:T(8,128)S(1)} async-done(((f32[16,16,512]{2,1,0:T(8,128)}), f32[16,16,512]{2,1,0:T(8,128)S(1)}, u32[]{:S(2)}, u32[]{:S(2)}) %all-to-all-start) | async-done | bytes 524320 | tf_op jit(solution)/shard_map/all_to_all | solution.py:432
  35.8 1.8 %azimuth.1 = f32[2,256,512]{2,1,0:T(8,128)} custom-call(bf16[3,2,1,256,256]{4,3,2,1,0:T(8,128)(2,1)S(1)} %azimuth_table.1.refs_0_, f32[16,16,512]{2,1,0:T(8,128)S(1)} %all-to-all-done.refs_1_, f32[4,16,512]{2,1,0:T(8,128)S(1)} %get-tuple-element.39.refs_2_, f32[4,16,512]{2,1,0:T(8,128)S(1)} %collective-permute-done.5.refs_3_, ...), custom_call_target="tpu_custom_call" | custom-call | flops 805306368 | bytes 2097152 | tf_op jit(solution)/shard_map/azimuth/pallas_call | solution.py:370
Async XLA Ops:
  0.0 11.1 %collective-permute-start.4 = (f32[2,8,16384]{2,1,0:T(8,128)}, f32[2,8,16384]{2,1,0:T(8,128)S(1)}, u32[]{:S(2)}, u32[]{:S(2)}) collective-permute-start(f32[2,8,16384]{2,1,0:T(8,128)} %refs_3_.1), channel_id=1, source_target_pairs={{0,8},{1,9},{2,10},{3,11},{4,12},{5,13},{6,14},{7,15},{8,0},{9,1},... | collective-permute-start | bytes 3145736 | tf_op jit(solution)/shard_map/ppermute | solution.py:420
  5.4 5.7 %collective-permute-start.3 = (f32[8,128]{1,0:T(8,128)S(1)}, f32[8,128]{1,0:T(8,128)S(1)}, u32[]{:S(2)}, u32[]{:S(2)}) collective-permute-start(f32[8,128]{1,0:T(8,128)S(1)} %get-tuple-element.28), channel_id=1, source_target_pairs={{0,8},{1,9},{2,10},{3,11},{4,12},{5,13},{6,14},{7,15},{8,0},{9,1},... | collective-permute-start | bytes 12296 | tf_op jit(solution)/shard_map/ppermute | solution.py:426
  5.5 15.6 %collective-permute-start = (f32[2,2,16,512]{3,2,1,0:T(8,128)S(1)}, f32[2,2,16,512]{3,2,1,0:T(8,128)S(1)}, u32[]{:S(2)}, u32[]{:S(2)}) collective-permute-start(f32[2,2,16,512]{3,2,1,0:T(8,128)S(1)} %get-tuple-element.25), channel_id=1, source_target_pairs={{0,4},{1,5},{2,6},{3,7},{4,0},{5,1},{6,2},{7,3},{8,12},{9,13},{10,... | collective-permute-start | bytes 393224 | tf_op jit(solution)/shard_map/ppermute | solution.py:423
  9.5 11.6 %collective-permute-start.1 = (f32[2,2,16,512]{3,2,1,0:T(8,128)S(1)}, f32[2,2,16,512]{3,2,1,0:T(8,128)S(1)}, u32[]{:S(2)}, u32[]{:S(2)}) collective-permute-start(f32[2,2,16,512]{3,2,1,0:T(8,128)S(1)} %get-tuple-element.26), channel_id=1, source_target_pairs={{0,6},{1,7},{2,4},{3,5},{4,2},{5,3},{6,0},{7,1},{8,14},{9,15},{10,... | collective-permute-start | bytes 393224 | tf_op jit(solution)/shard_map/ppermute | solution.py:423
  10.9 10.2 %collective-permute-start.2 = (f32[2,2,16,512]{3,2,1,0:T(8,128)S(1)}, f32[2,2,16,512]{3,2,1,0:T(8,128)S(1)}, u32[]{:S(2)}, u32[]{:S(2)}) collective-permute-start(f32[2,2,16,512]{3,2,1,0:T(8,128)S(1)} %get-tuple-element.27), channel_id=1, source_target_pairs={{0,2},{1,3},{2,0},{3,1},{4,6},{5,7},{6,4},{7,5},{8,10},{9,11},{10,... | collective-permute-start | bytes 393224 | tf_op jit(solution)/shard_map/ppermute | solution.py:423
  11.1 13.6 %copy-start = (f32[2,512]{1,0:T(2,128)S(1)}, f32[2,512]{1,0:T(2,128)}, u32[]{:S(2)}) copy-start(f32[2,512]{1,0:T(2,128)} %taps_ref) | copy-start | bytes 12292
  14.9 20.9 %all-to-all-start = ((f32[16,16,512]{2,1,0:T(8,128)}), f32[16,16,512]{2,1,0:T(8,128)S(1)}, u32[]{:S(2)}, u32[]{:S(2)}) async-start(f32[16,16,512]{2,1,0:T(8,128)} %range_partner.1), calls=%async_computation | async-start | bytes 1048576 | tf_op jit(solution)/shard_map/all_to_all | solution.py:432
  21.2 7.1 %collective-permute-start.5 = (f32[4,16,512]{2,1,0:T(8,128)S(1)}, f32[4,16,512]{2,1,0:T(8,128)S(1)}, u32[]{:S(2)}, u32[]{:S(2)}) collective-permute-start(f32[4,16,512]{2,1,0:T(8,128)S(1)} %get-tuple-element.40), channel_id=1, source_target_pairs={{0,1},{1,0},{2,3},{3,2},{4,5},{5,4},{6,7},{7,6},{8,9},{9,8},{10,11... | collective-permute-start | bytes 393224 | tf_op jit(solution)/shard_map/ppermute | solution.py:437
  23.2 8.0 %collective-permute-start.6 = (f32[4,16,512]{2,1,0:T(8,128)S(1)}, f32[4,16,512]{2,1,0:T(8,128)S(1)}, u32[]{:S(2)}, u32[]{:S(2)}) collective-permute-start(f32[4,16,512]{2,1,0:T(8,128)S(1)} %get-tuple-element.41), channel_id=1, source_target_pairs={{0,16},{1,17},{2,18},{3,19},{4,20},{5,21},{6,22},{7,23},{8,24},{9,... | collective-permute-start | bytes 393224 | tf_op jit(solution)/shard_map/ppermute | solution.py:437
  24.6 9.8 %collective-permute-start.7 = (f32[4,16,512]{2,1,0:T(8,128)S(1)}, f32[4,16,512]{2,1,0:T(8,128)S(1)}, u32[]{:S(2)}, u32[]{:S(2)}) collective-permute-start(f32[4,16,512]{2,1,0:T(8,128)S(1)} %get-tuple-element.42), channel_id=1, source_target_pairs={{0,17},{1,16},{2,19},{3,18},{4,21},{5,20},{6,23},{7,22},{8,25},{9,... | collective-permute-start | bytes 393224 | tf_op jit(solution)/shard_map/ppermute | solution.py:437

commit v9 on v8

--- a/solution.py
+++ b/solution.py
@@ -417,12 +417,13 @@
     planes = (segments, levels, run // levels)
     devices_all = outer * run
     bins = echoes.shape[2] // devices_all
-    echoes_partner = lax.ppermute(echoes, AXES, pairs_of(planes, core_step=1))
     *by_level, settings, table = range_call(True, planes, echoes, range_ref, shift_bins, interp_weights)
     received = [by_level[0]] + [
         lax.ppermute(array, AXES, pairs_of(planes, level_step=distance))
         for distance, array in zip(DISTANCES[1:], by_level[1:])
     ]
+    settings, echoes_later = lax.optimization_barrier((settings, echoes))
+    echoes_partner = lax.ppermute(echoes_later, AXES, pairs_of(planes, core_step=1))
     settings_partner = lax.ppermute(settings, AXES, pairs_of(planes, core_step=1))
     migrated = range_call(False, planes, echoes_partner, table, settings_partner)
     groups = [

time: 37.8 us -> 38 us (level)
  transfers between devices with their start and end apart: 9 -> 9, of which waited for: 4 -> 4; matrix products, arithmetic and copies ran while one was open for 0% -> 0% of each run, Pallas kernels for 24% -> 11%
where the time goes in v9:
time: 38 us; the launch traced here: 37.7 us
  starting transfers between devices  15.9 us (42%)
  Pallas kernels  10.8 us (28%)
  waiting for transfers between devices  10.8 us (28%)
    ppermute x3, waiting for transfers between devices, per_device(): lax.ppermute(by_place[q], AXES, pairs_of(planes, place_step=q))  9.47 us
    pallas_call x2, Pallas kernels, range_call(): pl.pallas_call(functools.partial(range_kernel, own, planes, lines, blocks...  8.79 us
    all_to_all x1, starting transfers between devices, per_device(): lax.all_to_all(migrated, AXES, split_axis=0, concat_axis=0, axis_index_gr...  6.2 us
    ppermute x3, starting transfers between devices, per_device(): lax.ppermute(array, AXES, pairs_of(planes, level_step=distance))  5.59 us
    ppermute x3, starting transfers between devices, per_device(): lax.ppermute(by_place[q], AXES, pairs_of(planes, place_step=q))  3.55 us
    pallas_call x1, Pallas kernels, azimuth_call(): pl.pallas_call(functools.partial(azimuth_kernel, planes), out_shape=jax.S...  1.77 us
    all_to_all x1, waiting for transfers between devices, per_device(): lax.all_to_all(migrated, AXES, split_axis=0, concat_axis=0, axis_index_gr...  1.33 us
  transfers between devices with their start and end apart: 9, of which 4 were waited for; matrix products, arithmetic and copies ran while one was open for 0% of the time, Pallas kernels for 11%

profile of v9, /device:TPU:0, one launch (start us, length us, event | category | flops | bytes accessed | tf_op | source)
XLA Modules:
  0.0 37.7 jit_solution(9911869817109355124)
XLA Ops:
  0.0 0.0 copy-start.1
  0.0 5.0 %range_own.1 = (f32[2,2,16,512]{3,2,1,0:T(8,128)S(1)}, f32[2,2,16,512]{3,2,1,0:T(8,128)S(1)}, f32[2,2,16,512]{3,2,1,0:T(8,128)S(1)}, f32[2,2,16,512]{3,2,1,0:T(8...) custom-call(s32[8]{0:T(128)} %refs_0_.1, f32[2,1024]{1,0:T(2,128)} %refs_1_.1, f32[8,8]{1,0:T(8,128)} %refs_2_.1, ...), custom_call_target="tpu_custom_call" | custom-call | flops 1698693120 | bytes 1572864 | tf_op jit(solution)/shard_map/range_own/pallas_call | solution.py:250
  5.0 0.0 copy-done.1
  5.0 0.5 %collective-permute-start.4 = (f32[2,8,16384]{2,1,0:T(8,128)S(1)}, f32[2,8,16384]{2,1,0:T(8,128)S(1)}, u32[]{:S(2)}, u32[]{:S(2)}) collective-permute-start(f32[2,8,16384]{2,1,0:T(8,128)S(1)} %copy-done.1), channel_id=1, source_target_pairs={{0,8},{1,9},{2,10},{3,11},{4,12},{5,13},{6,14},{7,15},{8,0},{9,1},... | collective-permute-start | bytes 3145736 | tf_op jit(solution)/shard_map/ppermute | solution.py:426
  5.6 0.1 collective-permute-start.3
  5.6 4.0 %collective-permute-start = (f32[2,2,16,512]{3,2,1,0:T(8,128)S(1)}, f32[2,2,16,512]{3,2,1,0:T(8,128)S(1)}, u32[]{:S(2)}, u32[]{:S(2)}) collective-permute-start(f32[2,2,16,512]{3,2,1,0:T(8,128)S(1)} %get-tuple-element.27), channel_id=1, source_target_pairs={{0,4},{1,5},{2,6},{3,7},{4,0},{5,1},{6,2},{7,3},{8,12},{9,13},{10,... | collective-permute-start | bytes 393224 | tf_op jit(solution)/shard_map/ppermute | solution.py:422
  9.7 1.3 %collective-permute-start.1 = (f32[2,2,16,512]{3,2,1,0:T(8,128)S(1)}, f32[2,2,16,512]{3,2,1,0:T(8,128)S(1)}, u32[]{:S(2)}, u32[]{:S(2)}) collective-permute-start(f32[2,2,16,512]{3,2,1,0:T(8,128)S(1)} %get-tuple-element.28), channel_id=1, source_target_pairs={{0,6},{1,7},{2,4},{3,5},{4,2},{5,3},{6,0},{7,1},{8,14},{9,15},{10,... | collective-permute-start | bytes 393224 | tf_op jit(solution)/shard_map/ppermute | solution.py:422
  11.0 0.2 collective-permute-start.2
  11.2 0.0 collective-permute-done.3.refs_0_
  11.2 0.0 collective-permute-done.4.refs_2_
  11.2 0.0 copy-start
  11.3 3.8 %range_partner.1 = f32[16,16,512]{2,1,0:T(8,128)} custom-call(f32[8,128]{1,0:T(8,128)S(1)} %collective-permute-done.3.refs_0_, bf16[3,2,256,1280]{3,2,1,0:T(8,128)(2,1)S(1)} %get-tuple-element.32.refs_1_, f32[2,8,16384]{2,1,0:T(8,128)S(1)} %collective-permute-done.4.refs_2_), custom_call_target="tpu_custom_call" | custom-call | flops 1698693120 | bytes 1572864 | tf_op jit(solution)/shard_map/range_partner/pallas_call | solution.py:250
  15.0 6.2 %all-to-all-start = ((f32[16,16,512]{2,1,0:T(8,128)}), f32[16,16,512]{2,1,0:T(8,128)S(1)}, u32[]{:S(2)}, u32[]{:S(2)}) async-start(f32[16,16,512]{2,1,0:T(8,128)} %range_partner.1), calls=%async_computation | async-start | bytes 1048576 | tf_op jit(solution)/shard_map/all_to_all | solution.py:433
  21.2 0.0 collective-permute-done.refs_1_
  21.2 0.0 collective-permute-done.1.refs_2_
  21.3 0.0 collective-permute-done.2.refs_3_
  21.3 0.1 regroup.1
  21.3 2.0 %collective-permute-start.5 = (f32[4,16,512]{2,1,0:T(8,128)S(1)}, f32[4,16,512]{2,1,0:T(8,128)S(1)}, u32[]{:S(2)}, u32[]{:S(2)}) collective-permute-start(f32[4,16,512]{2,1,0:T(8,128)S(1)} %get-tuple-element.44), channel_id=1, source_target_pairs={{0,1},{1,0},{2,3},{3,2},{4,5},{5,4},{6,7},{7,6},{8,9},{9,8},{10,11... | collective-permute-start | bytes 393224 | tf_op jit(solution)/shard_map/ppermute | solution.py:438
  23.3 1.5 %collective-permute-start.6 = (f32[4,16,512]{2,1,0:T(8,128)S(1)}, f32[4,16,512]{2,1,0:T(8,128)S(1)}, u32[]{:S(2)}, u32[]{:S(2)}) collective-permute-start(f32[4,16,512]{2,1,0:T(8,128)S(1)} %get-tuple-element.45), channel_id=1, source_target_pairs={{0,16},{1,17},{2,18},{3,19},{4,20},{5,21},{6,22},{7,23},{8,24},{9,... | collective-permute-start | bytes 393224 | tf_op jit(solution)/shard_map/ppermute | solution.py:438
  24.8 0.1 collective-permute-start.7
  24.9 0.0 copy-done
  24.9 0.2 azimuth_table.1.refs_0_
  25.1 3.3 %collective-permute-done.5.refs_3_ = f32[4,16,512]{2,1,0:T(8,128)S(1)} collective-permute-done((f32[4,16,512]{2,1,0:T(8,128)S(1)}, f32[4,16,512]{2,1,0:T(8,128)S(1)}, u32[]{:S(2)}, u32[]{:S(2)}) %collective-permute-start.5) | collective-permute-done | bytes 131104 | tf_op jit(solution)/shard_map/ppermute | solution.py:438
  28.5 2.8 %collective-permute-done.6.refs_4_ = f32[4,16,512]{2,1,0:T(8,128)S(1)} collective-permute-done((f32[4,16,512]{2,1,0:T(8,128)S(1)}, f32[4,16,512]{2,1,0:T(8,128)S(1)}, u32[]{:S(2)}, u32[]{:S(2)}) %collective-permute-start.6) | collective-permute-done | bytes 131104 | tf_op jit(solution)/shard_map/ppermute | solution.py:438
  31.3 3.3 %collective-permute-done.7.refs_5_ = f32[4,16,512]{2,1,0:T(8,128)S(1)} collective-permute-done((f32[4,16,512]{2,1,0:T(8,128)S(1)}, f32[4,16,512]{2,1,0:T(8,128)S(1)}, u32[]{:S(2)}, u32[]{:S(2)}) %collective-permute-start.7) | collective-permute-done | bytes 131104 | tf_op jit(solution)/shard_map/ppermute | solution.py:438
  34.6 1.3 %all-to-all-done.refs_1_ = f32[16,16,512]{2,1,0:T(8,128)S(1)} async-done(((f32[16,16,512]{2,1,0:T(8,128)}), f32[16,16,512]{2,1,0:T(8,128)S(1)}, u32[]{:S(2)}, u32[]{:S(2)}) %all-to-all-start) | async-done | bytes 524320 | tf_op jit(solution)/shard_map/all_to_all | solution.py:433
  35.9 1.8 %azimuth.1 = f32[2,256,512]{2,1,0:T(8,128)} custom-call(bf16[3,2,1,256,256]{4,3,2,1,0:T(8,128)(2,1)S(1)} %azimuth_table.1.refs_0_, f32[16,16,512]{2,1,0:T(8,128)S(1)} %all-to-all-done.refs_1_, f32[4,16,512]{2,1,0:T(8,128)S(1)} %get-tuple-element.43.refs_2_, f32[4,16,512]{2,1,0:T(8,128)S(1)} %collective-permute-done.5.refs_3_, ...), custom_call_target="tpu_custom_call" | custom-call | flops 805306368 | bytes 2097152 | tf_op jit(solution)/shard_map/azimuth/pallas_call | solution.py:370
Async XLA Ops:
  0.0 5.0 %copy-start.1 = (f32[2,8,16384]{2,1,0:T(8,128)S(1)}, f32[2,8,16384]{2,1,0:T(8,128)}, u32[]{:S(2)}) copy-start(f32[2,8,16384]{2,1,0:T(8,128)} %refs_3_.1) | copy-start | bytes 3145732
  5.0 6.2 %collective-permute-start.4 = (f32[2,8,16384]{2,1,0:T(8,128)S(1)}, f32[2,8,16384]{2,1,0:T(8,128)S(1)}, u32[]{:S(2)}, u32[]{:S(2)}) collective-permute-start(f32[2,8,16384]{2,1,0:T(8,128)S(1)} %copy-done.1), channel_id=1, source_target_pairs={{0,8},{1,9},{2,10},{3,11},{4,12},{5,13},{6,14},{7,15},{8,0},{9,1},... | collective-permute-start | bytes 3145736 | tf_op jit(solution)/shard_map/ppermute | solution.py:426
  5.6 5.7 %collective-permute-start.3 = (f32[8,128]{1,0:T(8,128)S(1)}, f32[8,128]{1,0:T(8,128)S(1)}, u32[]{:S(2)}, u32[]{:S(2)}) collective-permute-start(f32[8,128]{1,0:T(8,128)S(1)} %get-tuple-element.31), channel_id=1, source_target_pairs={{0,8},{1,9},{2,10},{3,11},{4,12},{5,13},{6,14},{7,15},{8,0},{9,1},... | collective-permute-start | bytes 12296 | tf_op jit(solution)/shard_map/ppermute | solution.py:427
  5.6 15.6 %collective-permute-start = (f32[2,2,16,512]{3,2,1,0:T(8,128)S(1)}, f32[2,2,16,512]{3,2,1,0:T(8,128)S(1)}, u32[]{:S(2)}, u32[]{:S(2)}) collective-permute-start(f32[2,2,16,512]{3,2,1,0:T(8,128)S(1)} %get-tuple-element.27), channel_id=1, source_target_pairs={{0,4},{1,5},{2,6},{3,7},{4,0},{5,1},{6,2},{7,3},{8,12},{9,13},{10,... | collective-permute-start | bytes 393224 | tf_op jit(solution)/shard_map/ppermute | solution.py:422
  9.7 11.6 %collective-permute-start.1 = (f32[2,2,16,512]{3,2,1,0:T(8,128)S(1)}, f32[2,2,16,512]{3,2,1,0:T(8,128)S(1)}, u32[]{:S(2)}, u32[]{:S(2)}) collective-permute-start(f32[2,2,16,512]{3,2,1,0:T(8,128)S(1)} %get-tuple-element.28), channel_id=1, source_target_pairs={{0,6},{1,7},{2,4},{3,5},{4,2},{5,3},{6,0},{7,1},{8,14},{9,15},{10,... | collective-permute-start | bytes 393224 | tf_op jit(solution)/shard_map/ppermute | solution.py:422
  11.0 10.2 %collective-permute-start.2 = (f32[2,2,16,512]{3,2,1,0:T(8,128)S(1)}, f32[2,2,16,512]{3,2,1,0:T(8,128)S(1)}, u32[]{:S(2)}, u32[]{:S(2)}) collective-permute-start(f32[2,2,16,512]{3,2,1,0:T(8,128)S(1)} %get-tuple-element.29), channel_id=1, source_target_pairs={{0,2},{1,3},{2,0},{3,1},{4,6},{5,7},{6,4},{7,5},{8,10},{9,11},{10,... | collective-permute-start | bytes 393224 | tf_op jit(solution)/shard_map/ppermute | solution.py:422
  11.2 13.6 %copy-start = (f32[2,512]{1,0:T(2,128)S(1)}, f32[2,512]{1,0:T(2,128)}, u32[]{:S(2)}) copy-start(f32[2,512]{1,0:T(2,128)} %taps_ref) | copy-start | bytes 12292
  15.0 20.9 %all-to-all-start = ((f32[16,16,512]{2,1,0:T(8,128)}), f32[16,16,512]{2,1,0:T(8,128)S(1)}, u32[]{:S(2)}, u32[]{:S(2)}) async-start(f32[16,16,512]{2,1,0:T(8,128)} %range_partner.1), calls=%async_computation | async-start | bytes 1048576 | tf_op jit(solution)/shard_map/all_to_all | solution.py:433
  21.3 7.1 %collective-permute-start.5 = (f32[4,16,512]{2,1,0:T(8,128)S(1)}, f32[4,16,512]{2,1,0:T(8,128)S(1)}, u32[]{:S(2)}, u32[]{:S(2)}) collective-permute-start(f32[4,16,512]{2,1,0:T(8,128)S(1)} %get-tuple-element.44), channel_id=1, source_target_pairs={{0,1},{1,0},{2,3},{3,2},{4,5},{5,4},{6,7},{7,6},{8,9},{9,8},{10,11... | collective-permute-start | bytes 393224 | tf_op jit(solution)/shard_map/ppermute | solution.py:438
  23.3 8.0 %collective-permute-start.6 = (f32[4,16,512]{2,1,0:T(8,128)S(1)}, f32[4,16,512]{2,1,0:T(8,128)S(1)}, u32[]{:S(2)}, u32[]{:S(2)}) collective-permute-start(f32[4,16,512]{2,1,0:T(8,128)S(1)} %get-tuple-element.45), channel_id=1, source_target_pairs={{0,16},{1,17},{2,18},{3,19},{4,20},{5,21},{6,22},{7,23},{8,24},{9,... | collective-permute-start | bytes 393224 | tf_op jit(solution)/shard_map/ppermute | solution.py:438
  24.8 9.8 %collective-permute-start.7 = (f32[4,16,512]{2,1,0:T(8,128)S(1)}, f32[4,16,512]{2,1,0:T(8,128)S(1)}, u32[]{:S(2)}, u32[]{:S(2)}) collective-permute-start(f32[4,16,512]{2,1,0:T(8,128)S(1)} %get-tuple-element.46), channel_id=1, source_target_pairs={{0,17},{1,16},{2,19},{3,18},{4,21},{5,20},{6,23},{7,22},{8,25},{9,... | collective-permute-start | bytes 393224 | tf_op jit(solution)/shard_map/ppermute | solution.py:438

commit v10 on v7

--- a/solution.py
+++ b/solution.py
@@ -260,18 +260,13 @@
 
 
 def regroup_kernel(levels, plane, *refs):
-    sources, outs, sems = refs[:levels], refs[levels:-1], refs[-1]
+    sources, outs = refs[:levels], refs[levels:]
     inner = sources[0].shape[1]
     mine = place_here(inner)
-    copies = []
     for q in range(plane):
         place = mine ^ q
         for k in range(levels):
-            source = sources[k].at[place // inner, lax.rem(place, inner)]
-            copies.append(pltpu.make_async_copy(source, outs[q].at[k], sems.at[q, k]))
-            copies[-1].start()
-    for copy in copies:
-        copy.wait()
+            outs[q][k] = sources[k][place // inner, lax.rem(place, inner)]
 
 
 def place_here(inner):
@@ -285,9 +280,8 @@
     return pl.pallas_call(
         functools.partial(regroup_kernel, levels, plane),
         out_shape=[jax.ShapeDtypeStruct((levels, rows, bins), jnp.float32)] * plane,
-        in_specs=[pl.BlockSpec(memory_space=pl.ANY)] * levels,
-        out_specs=[pl.BlockSpec(memory_space=pltpu.HBM)] * plane,
-        scratch_shapes=[pltpu.SemaphoreType.DMA((plane, levels))],
+        in_specs=[pl.BlockSpec(memory_space=pltpu.VMEM)] * levels,
+        out_specs=[pl.BlockSpec(memory_space=pltpu.VMEM)] * plane,
         compiler_params=pltpu.CompilerParams(vmem_limit_bytes=8 << 20),
         cost_estimate=pl.CostEstimate(flops=0, bytes_accessed=8 * levels * plane * rows * bins, transcendentals=0),
         name="regroup",

time: 38 us -> 38 us (level)
  waiting for transfers between devices: 10 us -> 10.8 us
  Pallas kernels: 11.7 us -> 10.9 us
    pallas_call x1, Pallas kernels: 0.9 us -> 0.06 us  [regroup_call(): pl.pallas_call(functools.partial(regroup_kernel, levels, plane), out_shap...]
    ppermute x3, waiting for transfers between devices: 8.85 us -> 9.49 us  [per_device(): lax.ppermute(by_place[q], AXES, pairs_of(planes, place_step=q))]
  transfers between devices with their start and end apart: 9 -> 9, of which waited for: 4 -> 4; matrix products, arithmetic and copies ran while one was open for 0% -> 0% of each run, Pallas kernels for 26% -> 24%
where the time goes in v10:
time: 38 us; the launch traced here: 37.7 us
  starting transfers between devices  15.9 us (42%)
  Pallas kernels  10.9 us (29%)
  waiting for transfers between devices  10.8 us (28%)
    ppermute x3, waiting for transfers between devices, per_device(): lax.ppermute(by_place[q], AXES, pairs_of(planes, place_step=q))  9.49 us
    pallas_call x2, Pallas kernels, range_call(): pl.pallas_call(functools.partial(range_kernel, own, planes, lines, blocks...  8.67 us
    all_to_all x1, starting transfers between devices, per_device(): lax.all_to_all(migrated, AXES, split_axis=0, concat_axis=0, axis_index_gr...  6.2 us
    ppermute x3, starting transfers between devices, per_device(): lax.ppermute(array, AXES, pairs_of(planes, level_step=distance))  5.61 us
    ppermute x3, starting transfers between devices, per_device(): lax.ppermute(by_place[q], AXES, pairs_of(planes, place_step=q))  3.55 us
    pallas_call x1, Pallas kernels, azimuth_call(): pl.pallas_call(functools.partial(azimuth_kernel, planes), out_shape=jax.S...  1.96 us
    all_to_all x1, waiting for transfers between devices, per_device(): lax.all_to_all(migrated, AXES, split_axis=0, concat_axis=0, axis_index_gr...  1.33 us
  transfers between devices with their start and end apart: 9, of which 4 were waited for; matrix products, arithmetic and copies ran while one was open for 0% of the time, Pallas kernels for 24%

profile of v10, /device:TPU:0, one launch (start us, length us, event | category | flops | bytes accessed | tf_op | source)
XLA Modules:
  0.0 37.7 jit_solution(10891533970524777960)
XLA Ops:
  0.0 0.5 %collective-permute-start.4 = (f32[2,8,16384]{2,1,0:T(8,128)}, f32[2,8,16384]{2,1,0:T(8,128)S(1)}, u32[]{:S(2)}, u32[]{:S(2)}) collective-permute-start(f32[2,8,16384]{2,1,0:T(8,128)} %refs_3_.1), channel_id=1, source_target_pairs={{0,8},{1,9},{2,10},{3,11},{4,12},{5,13},{6,14},{7,15},{8,0},{9,1},... | collective-permute-start | bytes 3145736 | tf_op jit(solution)/shard_map/ppermute | solution.py:415
  0.5 4.9 %range_own.1 = (f32[2,2,16,512]{3,2,1,0:T(8,128)S(1)}, f32[2,2,16,512]{3,2,1,0:T(8,128)S(1)}, f32[2,2,16,512]{3,2,1,0:T(8,128)S(1)}, f32[2,2,16,512]{3,2,1,0:T(8...) custom-call(s32[8]{0:T(128)} %refs_0_.1, f32[2,1024]{1,0:T(2,128)} %refs_1_.1, f32[8,8]{1,0:T(8,128)} %refs_2_.1, ...), custom_call_target="tpu_custom_call" | custom-call | flops 1698693120 | bytes 1572864 | tf_op jit(solution)/shard_map/range_own/pallas_call | solution.py:250
  5.4 0.1 collective-permute-start.3
  5.5 4.0 %collective-permute-start = (f32[2,2,16,512]{3,2,1,0:T(8,128)S(1)}, f32[2,2,16,512]{3,2,1,0:T(8,128)S(1)}, u32[]{:S(2)}, u32[]{:S(2)}) collective-permute-start(f32[2,2,16,512]{3,2,1,0:T(8,128)S(1)} %get-tuple-element.25), channel_id=1, source_target_pairs={{0,4},{1,5},{2,6},{3,7},{4,0},{5,1},{6,2},{7,3},{8,12},{9,13},{10,... | collective-permute-start | bytes 393224 | tf_op jit(solution)/shard_map/ppermute | solution.py:418
  9.5 1.3 %collective-permute-start.1 = (f32[2,2,16,512]{3,2,1,0:T(8,128)S(1)}, f32[2,2,16,512]{3,2,1,0:T(8,128)S(1)}, u32[]{:S(2)}, u32[]{:S(2)}) collective-permute-start(f32[2,2,16,512]{3,2,1,0:T(8,128)S(1)} %get-tuple-element.26), channel_id=1, source_target_pairs={{0,6},{1,7},{2,4},{3,5},{4,2},{5,3},{6,0},{7,1},{8,14},{9,15},{10,... | collective-permute-start | bytes 393224 | tf_op jit(solution)/shard_map/ppermute | solution.py:418
  10.9 0.2 collective-permute-start.2
  11.1 0.0 collective-permute-done.3.refs_0_
  11.1 0.0 collective-permute-done.4.refs_2_
  11.1 0.0 copy-start
  11.1 3.8 %range_partner.1 = f32[16,16,512]{2,1,0:T(8,128)} custom-call(f32[8,128]{1,0:T(8,128)S(1)} %collective-permute-done.3.refs_0_, bf16[3,2,256,1280]{3,2,1,0:T(8,128)(2,1)S(1)} %get-tuple-element.29.refs_1_, f32[2,8,16384]{2,1,0:T(8,128)S(1)} %collective-permute-done.4.refs_2_), custom_call_target="tpu_custom_call" | custom-call | flops 1698693120 | bytes 1572864 | tf_op jit(solution)/shard_map/range_partner/pallas_call | solution.py:250
  14.9 6.2 %all-to-all-start = ((f32[16,16,512]{2,1,0:T(8,128)}), f32[16,16,512]{2,1,0:T(8,128)S(1)}, u32[]{:S(2)}, u32[]{:S(2)}) async-start(f32[16,16,512]{2,1,0:T(8,128)} %range_partner.1), calls=%async_computation | async-start | bytes 1048576 | tf_op jit(solution)/shard_map/all_to_all | solution.py:427
  21.1 0.0 collective-permute-done.refs_1_
  21.1 0.0 collective-permute-done.1.refs_2_
  21.1 0.0 collective-permute-done.2.refs_3_
  21.1 0.1 regroup.1
  21.2 2.0 %collective-permute-start.5 = (f32[4,16,512]{2,1,0:T(8,128)S(1)}, f32[4,16,512]{2,1,0:T(8,128)S(1)}, u32[]{:S(2)}, u32[]{:S(2)}) collective-permute-start(f32[4,16,512]{2,1,0:T(8,128)S(1)} %get-tuple-element.40), channel_id=1, source_target_pairs={{0,1},{1,0},{2,3},{3,2},{4,5},{5,4},{6,7},{7,6},{8,9},{9,8},{10,11... | collective-permute-start | bytes 393224 | tf_op jit(solution)/shard_map/ppermute | solution.py:432
  23.2 1.5 %collective-permute-start.6 = (f32[4,16,512]{2,1,0:T(8,128)S(1)}, f32[4,16,512]{2,1,0:T(8,128)S(1)}, u32[]{:S(2)}, u32[]{:S(2)}) collective-permute-start(f32[4,16,512]{2,1,0:T(8,128)S(1)} %get-tuple-element.41), channel_id=1, source_target_pairs={{0,16},{1,17},{2,18},{3,19},{4,20},{5,21},{6,22},{7,23},{8,24},{9,... | collective-permute-start | bytes 393224 | tf_op jit(solution)/shard_map/ppermute | solution.py:432
  24.6 0.1 collective-permute-start.7
  24.7 0.0 copy-done
  24.8 0.2 azimuth_table.1.refs_0_
  25.0 3.4 %collective-permute-done.5.refs_3_ = f32[4,16,512]{2,1,0:T(8,128)S(1)} collective-permute-done((f32[4,16,512]{2,1,0:T(8,128)S(1)}, f32[4,16,512]{2,1,0:T(8,128)S(1)}, u32[]{:S(2)}, u32[]{:S(2)}) %collective-permute-start.5) | collective-permute-done | bytes 131104 | tf_op jit(solution)/shard_map/ppermute | solution.py:432
  28.3 2.8 %collective-permute-done.6.refs_4_ = f32[4,16,512]{2,1,0:T(8,128)S(1)} collective-permute-done((f32[4,16,512]{2,1,0:T(8,128)S(1)}, f32[4,16,512]{2,1,0:T(8,128)S(1)}, u32[]{:S(2)}, u32[]{:S(2)}) %collective-permute-start.6) | collective-permute-done | bytes 131104 | tf_op jit(solution)/shard_map/ppermute | solution.py:432
  31.2 3.3 %collective-permute-done.7.refs_5_ = f32[4,16,512]{2,1,0:T(8,128)S(1)} collective-permute-done((f32[4,16,512]{2,1,0:T(8,128)S(1)}, f32[4,16,512]{2,1,0:T(8,128)S(1)}, u32[]{:S(2)}, u32[]{:S(2)}) %collective-permute-start.7) | collective-permute-done | bytes 131104 | tf_op jit(solution)/shard_map/ppermute | solution.py:432
  34.5 1.3 %all-to-all-done.refs_1_ = f32[16,16,512]{2,1,0:T(8,128)S(1)} async-done(((f32[16,16,512]{2,1,0:T(8,128)}), f32[16,16,512]{2,1,0:T(8,128)S(1)}, u32[]{:S(2)}, u32[]{:S(2)}) %all-to-all-start) | async-done | bytes 524320 | tf_op jit(solution)/shard_map/all_to_all | solution.py:427
  35.8 2.0 %azimuth.1 = f32[2,256,512]{2,1,0:T(8,128)} custom-call(bf16[2,2,1,256,256]{4,3,2,1,0:T(8,128)(2,1)S(1)} %azimuth_table.1.refs_0_, f32[16,16,512]{2,1,0:T(8,128)S(1)} %all-to-all-done.refs_1_, f32[4,16,512]{2,1,0:T(8,128)S(1)} %get-tuple-element.39.refs_2_, f32[4,16,512]{2,1,0:T(8,128)S(1)} %collective-permute-done.5.refs_3_, ...), custom_call_target="tpu_custom_call" | custom-call | flops 805306368 | bytes 2097152 | tf_op jit(solution)/shard_map/azimuth/pallas_call | solution.py:365
Async XLA Ops:
  0.0 11.1 %collective-permute-start.4 = (f32[2,8,16384]{2,1,0:T(8,128)}, f32[2,8,16384]{2,1,0:T(8,128)S(1)}, u32[]{:S(2)}, u32[]{:S(2)}) collective-permute-start(f32[2,8,16384]{2,1,0:T(8,128)} %refs_3_.1), channel_id=1, source_target_pairs={{0,8},{1,9},{2,10},{3,11},{4,12},{5,13},{6,14},{7,15},{8,0},{9,1},... | collective-permute-start | bytes 3145736 | tf_op jit(solution)/shard_map/ppermute | solution.py:415
  5.4 5.7 %collective-permute-start.3 = (f32[8,128]{1,0:T(8,128)S(1)}, f32[8,128]{1,0:T(8,128)S(1)}, u32[]{:S(2)}, u32[]{:S(2)}) collective-permute-start(f32[8,128]{1,0:T(8,128)S(1)} %get-tuple-element.28), channel_id=1, source_target_pairs={{0,8},{1,9},{2,10},{3,11},{4,12},{5,13},{6,14},{7,15},{8,0},{9,1},... | collective-permute-start | bytes 12296 | tf_op jit(solution)/shard_map/ppermute | solution.py:421
  5.5 15.6 %collective-permute-start = (f32[2,2,16,512]{3,2,1,0:T(8,128)S(1)}, f32[2,2,16,512]{3,2,1,0:T(8,128)S(1)}, u32[]{:S(2)}, u32[]{:S(2)}) collective-permute-start(f32[2,2,16,512]{3,2,1,0:T(8,128)S(1)} %get-tuple-element.25), channel_id=1, source_target_pairs={{0,4},{1,5},{2,6},{3,7},{4,0},{5,1},{6,2},{7,3},{8,12},{9,13},{10,... | collective-permute-start | bytes 393224 | tf_op jit(solution)/shard_map/ppermute | solution.py:418
  9.5 11.6 %collective-permute-start.1 = (f32[2,2,16,512]{3,2,1,0:T(8,128)S(1)}, f32[2,2,16,512]{3,2,1,0:T(8,128)S(1)}, u32[]{:S(2)}, u32[]{:S(2)}) collective-permute-start(f32[2,2,16,512]{3,2,1,0:T(8,128)S(1)} %get-tuple-element.26), channel_id=1, source_target_pairs={{0,6},{1,7},{2,4},{3,5},{4,2},{5,3},{6,0},{7,1},{8,14},{9,15},{10,... | collective-permute-start | bytes 393224 | tf_op jit(solution)/shard_map/ppermute | solution.py:418
  10.9 10.2 %collective-permute-start.2 = (f32[2,2,16,512]{3,2,1,0:T(8,128)S(1)}, f32[2,2,16,512]{3,2,1,0:T(8,128)S(1)}, u32[]{:S(2)}, u32[]{:S(2)}) collective-permute-start(f32[2,2,16,512]{3,2,1,0:T(8,128)S(1)} %get-tuple-element.27), channel_id=1, source_target_pairs={{0,2},{1,3},{2,0},{3,1},{4,6},{5,7},{6,4},{7,5},{8,10},{9,11},{10,... | collective-permute-start | bytes 393224 | tf_op jit(solution)/shard_map/ppermute | solution.py:418
  11.1 13.6 %copy-start = (f32[2,512]{1,0:T(2,128)S(1)}, f32[2,512]{1,0:T(2,128)}, u32[]{:S(2)}) copy-start(f32[2,512]{1,0:T(2,128)} %taps_ref) | copy-start | bytes 12292
  14.9 20.9 %all-to-all-start = ((f32[16,16,512]{2,1,0:T(8,128)}), f32[16,16,512]{2,1,0:T(8,128)S(1)}, u32[]{:S(2)}, u32[]{:S(2)}) async-start(f32[16,16,512]{2,1,0:T(8,128)} %range_partner.1), calls=%async_computation | async-start | bytes 1048576 | tf_op jit(solution)/shard_map/all_to_all | solution.py:427
  21.2 7.1 %collective-permute-start.5 = (f32[4,16,512]{2,1,0:T(8,128)S(1)}, f32[4,16,512]{2,1,0:T(8,128)S(1)}, u32[]{:S(2)}, u32[]{:S(2)}) collective-permute-start(f32[4,16,512]{2,1,0:T(8,128)S(1)} %get-tuple-element.40), channel_id=1, source_target_pairs={{0,1},{1,0},{2,3},{3,2},{4,5},{5,4},{6,7},{7,6},{8,9},{9,8},{10,11... | collective-permute-start | bytes 393224 | tf_op jit(solution)/shard_map/ppermute | solution.py:432
  23.2 8.0 %collective-permute-start.6 = (f32[4,16,512]{2,1,0:T(8,128)S(1)}, f32[4,16,512]{2,1,0:T(8,128)S(1)}, u32[]{:S(2)}, u32[]{:S(2)}) collective-permute-start(f32[4,16,512]{2,1,0:T(8,128)S(1)} %get-tuple-element.41), channel_id=1, source_target_pairs={{0,16},{1,17},{2,18},{3,19},{4,20},{5,21},{6,22},{7,23},{8,24},{9,... | collective-permute-start | bytes 393224 | tf_op jit(solution)/shard_map/ppermute | solution.py:432
  24.6 9.8 %collective-permute-start.7 = (f32[4,16,512]{2,1,0:T(8,128)S(1)}, f32[4,16,512]{2,1,0:T(8,128)S(1)}, u32[]{:S(2)}, u32[]{:S(2)}) collective-permute-start(f32[4,16,512]{2,1,0:T(8,128)S(1)} %get-tuple-element.42), channel_id=1, source_target_pairs={{0,17},{1,16},{2,19},{3,18},{4,21},{5,20},{6,23},{7,22},{8,25},{9,... | collective-permute-start | bytes 393224 | tf_op jit(solution)/shard_map/ppermute | solution.py:432
